TPU v7x, 32 devices: a whole 2x2x4 slice. The times are simulated.
32 devices in a mesh: pb: 4 (over y, core), ctx: 8 (over z, x).
Axes of the slice: x: 2, y: 2, z: 4, core: 2. Of those that a mesh axis runs over, the one named last changes fastest.
Arguments:
- queries: bfloat16 [32768, 1024], P(('pb', 'ctx')), may hold values from -64 to 64
- key_states: bfloat16 [32768, 128], P(('pb', 'ctx')), may hold values from -6 to 6
- value_states: bfloat16 [32768, 128], P(('pb', 'ctx')), may hold values from -6 to 6
- key_blocks: int32 [256, 8], replicated, may hold values from -1 to 255, as said below
Outputs:
- attended: bfloat16 [32768, 1024], P(('pb', 'ctx'))
Inputs may be any that keep to these rules, and one draw needn't show every extreme that they name: `key_blocks`: row i lists first the blocks 0 to 1, then those of blocks i - 1, i, i + 1 that exist and are not among them, in increasing order, then 3 distinct blocks of other devices with the same pb index, none among those already listed and none next to the device's own 8 blocks; -1 fills the rest. Over the 8 rows of one device, at most 4 of the random entries name blocks of any one other device, and every device reaches that.
All inputs are finite; a program needn't handle non-finite values.
Results may differ from a plain program's by a relative error of at most 0.0047.
Values may be sent and summed in bfloat16 or wider, within the bound.
No kernel may reach another device: no remote copies, remote signals or barrier semaphores. Data moves between devices by JAX's collectives and lax.ppermute only.
A program may use at most 128 MiB of HBM per device.

v0:
```python
import jax
import jax.numpy as jnp
from jax import lax
from jax.sharding import PartitionSpec as P

HEAD_DIM = 128
HEADS = 8
BLOCK = 128
GLOBAL = 2
RANDOM = 3
LIST = 8


def extended(shard, sides, width):
    for axis, dim in sides:
        devices, length = (lax.axis_size(axis), shard.shape[dim])
        up = [(i, (i + 1) % devices) for i in range(devices - 1)]
        down = [(j, i) for i, j in up]
        last = lax.slice_in_dim(shard, length - width, length, axis=dim)
        first = lax.slice_in_dim(shard, 0, width, axis=dim)
        before = lax.ppermute(last, axis, up)
        after = lax.ppermute(first, axis, down)
        shard = jnp.concatenate([before, shard, after], axis=dim)
    return shard


def spread(shard, axis, root):
    mine = lax.axis_index(axis) == root
    return lax.psum(jnp.where(mine, shard, jnp.zeros_like(shard)), axis)


def attend(query_block, key_rows, value_rows, key_mask):
    scores = jnp.einsum(
        "thd,ud->thu", query_block, key_rows, preferred_element_type=jnp.float32
    ) * HEAD_DIM ** (-0.5)
    scores = jnp.where(key_mask[None, None, :], scores, -1e30)
    row_max = jnp.max(scores, axis=-1, keepdims=True)
    weights = jnp.exp(scores - row_max)
    normalizer = jnp.sum(weights, axis=-1, keepdims=True)
    rounded = weights.astype(jnp.bfloat16)
    result = (
        jnp.einsum("thu,ud->thd", rounded, value_rows, preferred_element_type=jnp.float32)
        / normalizer
    )
    return result.astype(jnp.bfloat16)


def classify(entries, first_block, blocks_dev, ctx_count):
    usable = entries >= 0
    is_global = usable & (entries < GLOBAL)
    nearby = usable & (entries >= first_block - 1) & (entries <= first_block + blocks_dev)
    remote = usable & jnp.logical_not(is_global) & jnp.logical_not(nearby)
    holder = jnp.maximum(entries, 0) // blocks_dev % ctx_count
    owner_hits = ((holder[:, None] == jnp.arange(ctx_count)[None, :]) & remote[:, None]).astype(
        jnp.int32
    )
    slot_rank = jnp.sum(jnp.cumsum(owner_hits, axis=0) * owner_hits, axis=1) - 1
    return (usable, is_global, nearby, remote, holder, slot_rank)


def per_device(queries, key_states, value_states, key_blocks):
    blocks_dev = queries.shape[0] // BLOCK
    ctx_count = lax.axis_size("ctx")
    slot_most = (RANDOM * blocks_dev + ctx_count - 2) // (ctx_count - 1)
    device_now = lax.axis_index(("pb", "ctx"))
    column_now = lax.axis_index("ctx")
    own_first = device_now * blocks_dev
    group_first = (device_now - column_now) * blocks_dev
    local_kv = jnp.stack(
        [
            key_states.reshape(blocks_dev, BLOCK, HEAD_DIM),
            value_states.reshape(blocks_dev, BLOCK, HEAD_DIM),
        ]
    )
    padded = extended(local_kv, ((("pb", "ctx"), 1),), 1)
    shared = spread(local_kv[:, :GLOBAL], ("pb", "ctx"), 0)
    own_rows = lax.dynamic_slice_in_dim(key_blocks, own_first, blocks_dev, 0)
    own_list = own_rows.reshape(-1)
    usable, is_global, nearby, remote, holder, slot_rank = classify(
        own_list, own_first, blocks_dev, ctx_count
    )
    slot_ids = jnp.arange(slot_most)
    matched = (
        remote[:, None, None]
        & (holder[:, None, None] == jnp.arange(ctx_count)[None, :, None])
        & (slot_rank[:, None, None] == slot_ids[None, None, :])
    )
    group_index = jnp.sum(
        matched.astype(jnp.int32) * (own_list - group_first)[:, None, None], axis=0
    ).reshape(-1)
    filled = jnp.any(matched, axis=0).reshape(-1)
    empty_pool = jnp.zeros((2, ctx_count * slot_most, BLOCK, HEAD_DIM), jnp.bfloat16)
    shard_piece = lax.all_gather(local_kv, "ctx", axis=1, tiled=True)
    piece_len = shard_piece.shape[1]
    inside = filled & (group_index >= 0) & (group_index < piece_len)
    taken_blocks = jnp.take(shard_piece, jnp.clip(group_index, 0, piece_len - 1), axis=1)
    window_new = jnp.where(inside[None, :, None, None], taken_blocks, empty_pool)
    kv_pool = jnp.concatenate([padded, shared, window_new], axis=1)
    pool_size = kv_pool.shape[1]
    global_index = blocks_dev + 2 + own_list
    near_index = own_list - (own_first - 1)
    remote_index = blocks_dev + 2 + GLOBAL + holder * slot_most + slot_rank
    pool_index = jnp.where(is_global, global_index, jnp.where(nearby, near_index, remote_index))
    pool_index = jnp.clip(jnp.where(usable, pool_index, 0), 0, pool_size - 1).reshape(
        blocks_dev, LIST
    )
    usable_rows = usable.reshape(blocks_dev, LIST)
    query_cube = queries.reshape(blocks_dev, BLOCK, HEADS, HEAD_DIM)

    def per_block(inputs):
        query_block, row_index, row_usable = inputs
        selected = jnp.take(kv_pool, row_index, axis=1)
        key_rows = selected[0].reshape(LIST * BLOCK, HEAD_DIM)
        value_rows = selected[1].reshape(LIST * BLOCK, HEAD_DIM)
        key_mask = jnp.repeat(row_usable, BLOCK)
        return attend(query_block, key_rows, value_rows, key_mask)

    result = lax.map(per_block, (query_cube, pool_index, usable_rows))
    return result.reshape(blocks_dev * BLOCK, HEADS * HEAD_DIM)


def solution(mesh):
    in_specs = (P(("pb", "ctx"), None), P(("pb", "ctx"), None), P(("pb", "ctx"), None), P())
    out_specs = P(("pb", "ctx"), None)
    return jax.shard_map(
        per_device, mesh=mesh, in_specs=in_specs, out_specs=out_specs, check_vma=False
    )
```

profile of v0, /device:TPU:0, one launch (start us, length us, event | category | flops | bytes accessed | tf_op | source)
XLA Modules:
  0.0 246.7 jit_solution(3679912432769475257)
XLA Ops:
  7.4 1.0 fusion.22
  8.3 4.8 %collective-permute-start = (bf16[2,1,128,128]{3,2,0,1:T(8,128)(2,1)S(1)}, bf16[2,1,128,128]{3,2,0,1:T(8,128)(2,1)S(1)}, u32[]{:S(2)}, u32[]{:S(2)}) collective-permute-start(bf16[2,1,128,128]{3,2,0,1:T(8,128)(2,1)S(1)} %get-tuple-element.75), channel_id=1, source_target_pairs={{0,1},{1,2},{2,3},{3,4},{4,5},{5,6},{6,7},{7,8},{8,9},{9,10},{10,1... | collective-permute-start | bytes 196616 | tf_op jit(solution)/shard_map/ppermute | solution.py:21
  13.2 1.5 fusion.20
  15.1 0.6 constant_dynamic-update-slice_fusion.3
  15.7 2.4 pad_maximum_fusion
  18.1 1.3 collective-permute-start.1
  21.6 1.9 copy.30
  23.6 1.1 collective-permute-done.1
  25.3 150.8 %all-reduce.2.cloned.1.call-done = bf16[2,2,128,128]{3,2,0,1:T(8,128)(2,1)} async-done(((bf16[2,2,128,128]{3,2,0,1:T(8,128)(2,1)}), bf16[2,2,128,128]{3,2,0,1:T(8,128)(2,1)}) %all-reduce.2.cloned.1.call-update) | async-done | bytes 131088 | tf_op jit(solution)/shard_map/psum | solution.py:29
  176.1 1.6 constant_dynamic-update-slice_fusion
  177.7 4.7 %copy.22 = bf16[2,64,128,128]{3,2,1,0:T(8,128)(2,1)} copy(bf16[2,64,128,128]{3,2,0,1:T(8,128)(2,1)} %all-gather.2.cloned.1.call-done) | data formatting | bytes 8388608 | tf_op jit(solution)/shard_map/all_gather | solution.py:93
  182.4 3.1 %gather_fusion.1 = bf16[32,2,128,128]{3,2,1,0:T(8,128)(2,1)S(1)} fusion(bf16[2,64,128,128]{3,2,1,0:T(8,128)(2,1)} %copy.22, s32[1024]{0:T(1024)S(1)} %pad_clamp_fusion.1), kind=kCustom, calls=%fused_computation.1 | custom fusion | bytes 4194432 | tf_op jit(solution)/shard_map/jit(_take)/gather | solution.py:96
  185.6 2.4 bitcast_dynamic-update-slice_fusion
  188.0 2.0 copy.24
  190.0 45.7 %while.10 = (s32[]{:T(128)}, bf16[8,128,8,128]{3,2,1,0:T(8,128)(2,1)}, pred[8,8]{1,0:T(8,128)(4,1)S(1)}, bf16[8,128,8,128]{3,2,1,0:T(8,128)(2,1)}, s32[8,8]{1,0:...) while((s32[]{:T(128)}, bf16[8,128,8,128]{3,2,1,0:T(8,128)(2,1)}, pred[8,8]{1,0:T(8,128)(4,1)S(1)}, ...), condition=%wide.region_8.9_spmd, body=%wide.region_5.8_spmd.sunk | while | flops 548928576 | bytes 17855268 | solution.py:118
  190.0 0.6 gather_fusion
  190.9 1.0 constant_dynamic-slice_fusion.4
  191.9 0.8 fusion.53
  192.8 1.1 fusion.54
  193.8 1.0 fusion.55
  194.8 0.9 copy_dynamic-update-slice_fusion.2
  195.7 0.6 gather_fusion
  196.7 1.0 constant_dynamic-slice_fusion.4
  197.6 0.8 fusion.53
  198.5 1.1 fusion.54
  199.5 1.0 fusion.55
  200.5 0.9 copy_dynamic-update-slice_fusion.2
  201.4 0.6 gather_fusion
  202.4 1.0 constant_dynamic-slice_fusion.4
  203.3 0.8 fusion.53
  204.2 1.1 fusion.54
  205.2 1.0 fusion.55
  206.2 0.9 copy_dynamic-update-slice_fusion.2
  207.1 0.6 gather_fusion
  208.1 1.0 constant_dynamic-slice_fusion.4
  209.0 0.8 fusion.53
  209.9 1.1 fusion.54
  210.9 1.0 fusion.55
  211.9 0.9 copy_dynamic-update-slice_fusion.2
  212.8 0.6 gather_fusion
  213.8 1.0 constant_dynamic-slice_fusion.4
  214.7 0.8 fusion.53
  215.6 1.1 fusion.54
  216.6 1.0 fusion.55
  217.7 0.9 copy_dynamic-update-slice_fusion.2
  218.6 0.6 gather_fusion
  219.5 1.0 constant_dynamic-slice_fusion.4
  220.5 0.8 fusion.53
  221.3 1.1 fusion.54
  222.4 1.0 fusion.55
  223.4 0.9 copy_dynamic-update-slice_fusion.2
  224.3 0.6 gather_fusion
  225.2 1.0 constant_dynamic-slice_fusion.4
  226.2 0.8 fusion.53
  227.0 1.1 fusion.54
  228.1 1.0 fusion.55
  229.1 0.9 copy_dynamic-update-slice_fusion.2
  230.0 0.6 gather_fusion
  230.9 1.0 constant_dynamic-slice_fusion.4
  231.9 0.8 fusion.53
  232.7 1.1 fusion.54
  233.8 1.0 fusion.55
  234.8 0.9 copy_dynamic-update-slice_fusion.2
  235.7 3.5 %copy.38 = bf16[128,8,8,128]{3,1,2,0:T(8,128)(2,1)} copy(bf16[128,8,8,128]{3,2,1,0:T(8,128)(2,1)} %bitcast.22) | data formatting | bytes 4194304
  (101 shorter events, 5.2 us)
Async XLA Ops:
  7.4 12.1 %copy-start = (s32[256,8]{0,1:T(8,128)S(1)}, s32[256,8]{0,1:T(8,128)}, u32[]{:S(2)}) copy-start(s32[256,8]{0,1:T(8,128)} %param.9) | copy-start | bytes 24580
  7.4 14.2 %copy-start.1 = (bf16[1024,1024]{1,0:T(8,128)(2,1)S(1)}, bf16[1024,1024]{1,0:T(8,128)(2,1)}, u32[]{:S(2)}) copy-start(bf16[1024,1024]{1,0:T(8,128)(2,1)} %param.6) | copy-start | bytes 6291460
  7.4 168.7 %all-reduce.2.cloned.1.call-start = ((), (), s32[]{:S(2)}) async-start(), calls=%async_computation | async-start | bytes 262144 | tf_op jit(solution)/shard_map/psum | solution.py:29
  8.3 6.7 %collective-permute-start = (bf16[2,1,128,128]{3,2,0,1:T(8,128)(2,1)S(1)}, bf16[2,1,128,128]{3,2,0,1:T(8,128)(2,1)S(1)}, u32[]{:S(2)}, u32[]{:S(2)}) collective-permute-start(bf16[2,1,128,128]{3,2,0,1:T(8,128)(2,1)S(1)} %get-tuple-element.75), channel_id=1, source_target_pairs={{0,1},{1,2},{2,3},{3,4},{4,5},{5,6},{6,7},{7,8},{8,9},{9,10},{10,1... | collective-permute-start | bytes 196616 | tf_op jit(solution)/shard_map/ppermute | solution.py:21
  14.8 162.9 %all-gather.2.cloned.1.call-start = ((), (), s32[]{:S(2)}) async-start(), calls=%async_computation.1 | async-start | bytes 4718592 | tf_op jit(solution)/shard_map/all_gather | solution.py:93
  18.1 6.6 %collective-permute-start.1 = (bf16[2,1,128,128]{3,2,0,1:T(8,128)(2,1)S(1)}, bf16[2,1,128,128]{3,2,0,1:T(8,128)(2,1)S(1)}, u32[]{:S(2)}, u32[]{:S(2)}) collective-permute-start(bf16[2,1,128,128]{3,2,0,1:T(8,128)(2,1)S(1)} %get-tuple-element.74), channel_id=1, source_target_pairs={{1,0},{2,1},{3,2},{4,3},{5,4},{6,5},{7,6},{8,7},{9,8},{10,9},{11,1... | collective-permute-start | bytes 196616 | tf_op jit(solution)/shard_map/ppermute | solution.py:22
Sparse Core Ops, SparseCore 0:
  14.9 161.1 all-reduce.1
Sparse Core Ops, SparseCore 1:
  18.2 75.2 all-gather.1
where the time goes:
time: 247 us
  waiting for transfers between devices  152 us (62%)
  local copies, waits for them, and re-layouts  40.5 us (16%)
  other arithmetic  17.7 us (7%)
  between operations  15 us (6%)
  matrix products  14.8 us (6%)
  starting transfers between devices  6.18 us (3%)
    psum x1, waiting for transfers between devices, spread(): return lax.psum(jnp.where(mine, shard, jnp.zeros_like(shard)), axis)  151 us
    reduce_sum x8, other arithmetic, attend(): normalizer = jnp.sum(weights, axis=-1, keepdims=True)  8.41 us
    unnamed x10, local copies, waits for them, and re-layouts  8.39 us
    dot_general x8, matrix products, attend(): jnp.einsum('thu,ud->thd', rounded, value_rows, preferred_element_type=jnp...  8.04 us
    dynamic_slice x8, local copies, waits for them, and re-layouts, per_device(): result = lax.map(per_block, (query_cube, pool_index, usable_rows))  7.74 us
    dynamic_update_slice x8, local copies, waits for them, and re-layouts, per_device(): result = lax.map(per_block, (query_cube, pool_index, usable_rows))  7.07 us
    dot_general x8, matrix products, attend(): jnp.einsum('thd,ud->thu', query_block, key_rows, preferred_element_type=j...  6.75 us
    gather x8, local copies, waits for them, and re-layouts, per_block(): selected = jnp.take(kv_pool, row_index, axis=1)  5.18 us
  transfers between devices with their start and end apart: 4, of which 3 were waited for; matrix products, arithmetic and copies ran while one was open for 4% of the time, Pallas kernels for 0%

commit v1 on v0

v1 whole, which is shorter than its diff:
```python
import jax
import jax.numpy as jnp
from jax import lax
from jax.experimental import pallas as pl
from jax.experimental.pallas import tpu as pltpu
from jax.sharding import PartitionSpec as P

HEAD_DIM = 128
HEADS = 8
BLOCK = 128
GLOBAL = 2
RANDOM = 3
LIST = 8
COST = 1 << 30
CHUNK = 4
TO_LOG2 = HEAD_DIM**-0.5 * 1.4426950408889634

VMEM = pl.BlockSpec(memory_space=pltpu.VMEM)
SMEM = pl.BlockSpec(memory_space=pltpu.SMEM)


def random_start(row, n_blocks):
    low = jnp.maximum(row - 1, GLOBAL)
    high = jnp.minimum(row + 1, n_blocks - 1)
    return GLOBAL + high - low + 1


def group_rows(key_blocks):
    n_rows = key_blocks.shape[0] // lax.axis_size("pb")
    return lax.dynamic_slice_in_dim(
        key_blocks, lax.axis_index("pb") * n_rows, n_rows, 0
    ).reshape(-1)


def ring_of(n_ctx):
    return list(range(0, n_ctx, 2)) + list(range(n_ctx - 1, 0, -2))


def place_of(index, n_ctx):
    return jnp.where(index % 2 == 0, index // 2, n_ctx - 1 - index // 2)


def device_at(place, n_ctx):
    place = lax.rem(place + n_ctx, n_ctx)
    return jnp.where(place < n_ctx // 2, 2 * place, 2 * (n_ctx - 1 - place) + 1)


def plan_kernel(sizes, list_ref, plan_ref, counts):
    n_pb, n_ctx, n_dev, slots = sizes
    n_blocks = n_pb * n_ctx * n_dev
    me = lax.axis_index("ctx")
    group = lax.axis_index("pb") * (n_ctx * n_dev)
    place = place_of(me, n_ctx)
    half = slots // 2
    spare = 2 * (slots + half) + n_dev * RANDOM

    def entry(device, r, j):
        row = device * n_dev + r
        return list_ref[row * LIST + random_start(group + row, n_blocks) + j]

    for side, sign in enumerate((1, -1)):
        base = side * (slots + half)
        source = device_at(place - 2 * sign, n_ctx)
        first = group + source * n_dev
        for i in range(slots + half):
            plan_ref[base + i] = 0
        for steps, low, high, at in ((2, side * half, (side + 1) * half, 0), (1, 0, slots, half)):
            target = device_at(place + steps * sign, n_ctx)
            count = jnp.int32(0)
            for r in range(n_dev):
                for j in range(RANDOM):
                    local = entry(target, r, j) - first
                    hit = jnp.logical_and(local >= 0, local < n_dev)
                    use = jnp.logical_and(hit, jnp.logical_and(count >= low, count < high))
                    plan_ref[jnp.where(use, base + at + count - low, spare)] = local
                    count = count + hit.astype(jnp.int32)
    for h in range(n_ctx):
        counts[h] = 0
    for r in range(n_dev):
        for j in range(RANDOM):
            block = entry(me, r, j) - group
            holder = block // n_dev
            local = block - holder * n_dev
            rank = counts[holder]
            counts[holder] = rank + 1
            away = lax.rem(place - place_of(holder, n_ctx) + n_ctx, n_ctx)
            whole = jnp.where(away <= 2, away - 1, n_ctx + 1 - away) * n_dev + local
            few = jnp.where(away == 4, 0, jnp.where(away == 3, slots, 2 * slots)) + rank
            is_few = jnp.logical_and(away >= 3, away <= 5)
            plan_ref[2 * (slots + half) + r * RANDOM + j] = jnp.where(is_few, 4 * n_dev + few, whole)


def make_plan(sizes, lists):
    n_pb, n_ctx, n_dev, slots = sizes
    length = 2 * (slots + slots // 2) + n_dev * RANDOM + 1
    return pl.pallas_call(
        lambda *refs: plan_kernel(sizes, *refs),
        out_shape=jax.ShapeDtypeStruct((length,), jnp.int32),
        in_specs=[SMEM],
        out_specs=SMEM,
        scratch_shapes=[pltpu.SMEM((n_ctx,), jnp.int32)],
        name="plan",
    )(lists)


def pick_kernel(base, half, slots, plan_ref, k_ref, v_ref, far_ref, out_ref):
    for ref, at, n in ((far_ref, base, half), (out_ref, base + half, slots)):
        for s in range(n):
            ref[s, 0] = k_ref[plan_ref[at + s]]
            ref[s, 1] = v_ref[plan_ref[at + s]]


def pick(sizes, side, plan, keys, values):
    slots = sizes[3]
    half = slots // 2
    return pl.pallas_call(
        lambda *refs: pick_kernel(side * (slots + half), half, slots, *refs),
        out_shape=[
            jax.ShapeDtypeStruct((n, 2, BLOCK, HEAD_DIM), jnp.bfloat16) for n in (half, slots)
        ],
        in_specs=[SMEM, VMEM, VMEM],
        out_specs=[VMEM, VMEM],
        name="pick",
    )(plan, keys, values)


def pass_round(sizes, plan, keys, values):
    n_ctx, n_dev, slots = sizes[1:]
    half = slots // 2
    ring = ring_of(n_ctx)
    parts = []
    for side in range(2):
        step = 1 if side == 0 else -1
        pairs = [(ring[i], ring[(i + step) % n_ctx]) for i in range(n_ctx)]
        k, v = keys, values
        for hop in range(2):
            k, v = lax.ppermute(k, "ctx", pairs), lax.ppermute(v, "ctx", pairs)
            at = (2 * side + hop) * n_dev
            parts += [(k, at, 0), (v, at, 1)]
        onward, near = pick(sizes, side, plan, k, v)
        onward = lax.ppermute(onward, "ctx", pairs)
        near = lax.ppermute(near, "ctx", pairs)
        opposite = lax.ppermute(onward, "ctx", pairs)
        parts += [(opposite, 4 * n_dev + side * half, None), (near, 4 * n_dev + (1 + side) * slots, None)]
    return parts


def gather_kernel(sizes, list_ref, k_ref, v_ref, *rest):
    n_pb, n_ctx, n_dev, slots = sizes
    outs, table = rest[:-1], rest[-1]
    n_blocks = n_pb * n_ctx * n_dev
    me = lax.axis_index("ctx")
    group = lax.axis_index("pb") * (n_ctx * n_dev)
    own = group + me * n_dev
    for i in range((n_ctx - 1) * slots + 1):
        table[i] = 0
    for shift in range(1, n_ctx):
        first = lax.rem(me + shift, n_ctx) * n_dev
        count = jnp.int32(0)
        for r in range(n_dev):
            row = first + r
            start = row * LIST + random_start(group + row, n_blocks)
            for j in range(RANDOM):
                local = list_ref[start + j] - own
                hit = jnp.logical_and(local >= 0, local < n_dev)
                place = jnp.where(hit, (shift - 1) * slots + count, (n_ctx - 1) * slots)
                table[place] = local
                count = count + hit.astype(jnp.int32)
    for shift in range(1, n_ctx):
        for s in range(slots):
            local = table[(shift - 1) * slots + s]
            outs[shift - 1][s, 0] = k_ref[local]
            outs[shift - 1][s, 1] = v_ref[local]


def gather(sizes, lists, key_states, value_states):
    n_pb, n_ctx, n_dev, slots = sizes
    return pl.pallas_call(
        lambda *refs: gather_kernel(sizes, *refs),
        out_shape=[jax.ShapeDtypeStruct((slots, 2, BLOCK, HEAD_DIM), jnp.bfloat16)] * (n_ctx - 1),
        in_specs=[SMEM, VMEM, VMEM],
        out_specs=[VMEM] * (n_ctx - 1),
        scratch_shapes=[pltpu.SMEM(((n_ctx - 1) * slots + 1,), jnp.int32)],
        name="gather",
    )(lists, key_states, value_states)


def softmax_part(q_ref, heads, keys, values):
    q = jnp.concatenate([q_ref[:, h * HEAD_DIM : (h + 1) * HEAD_DIM] for h in heads], axis=0)
    scores = lax.dot_general(
        q, keys[...], (((1,), (1,)), ((), ())), preferred_element_type=jnp.float32
    )
    top = jnp.max(scores, axis=1, keepdims=True)
    weights = jnp.exp2((scores - top) * TO_LOG2).astype(jnp.bfloat16)
    total = jnp.dot(weights, values[...], preferred_element_type=jnp.float32)
    return top * TO_LOG2, total[:, :HEAD_DIM], total[:, HEAD_DIM:]


def attend(q_ref, keys, values, before, out_ref, lse_ref):
    lane = lax.broadcasted_iota(jnp.int32, (BLOCK, HEAD_DIM), 1)
    earlier = None if before is None else before[1][...]
    packed = jnp.zeros((BLOCK, HEAD_DIM), jnp.float32)
    for c in range(0, HEADS, CHUNK):
        heads = range(c, c + CHUNK)
        tops, totals, norms = softmax_part(q_ref, heads, keys, values)
        for n, h in enumerate(heads):
            rows = slice(n * BLOCK, (n + 1) * BLOCK)
            lanes = slice(h * HEAD_DIM, (h + 1) * HEAD_DIM)
            top, total, norm = tops[rows], totals[rows], norms[rows]
            if before is not None:
                lse = jnp.max(jnp.where(lane == h, earlier, -jnp.inf), axis=1, keepdims=True)
                highest = jnp.maximum(lse, top)
                a, b = jnp.exp2(lse - highest), jnp.exp2(top - highest)
                total, norm, top = before[0][:, lanes] * a + total * b, a + norm * b, highest
            out_ref[:, lanes] = (total / norm).astype(out_ref.dtype)
            if lse_ref is not None:
                packed = jnp.where(lane == h, top + jnp.log2(norm), packed)
    if lse_ref is not None:
        lse_ref[...] = packed


def put(keys, values, slot, block, counts=None):
    rows = slice(slot * BLOCK, (slot + 1) * BLOCK)
    keys[rows, :] = block[0]
    value, one = block[1], jnp.ones((BLOCK, HEAD_DIM), jnp.bfloat16)
    if counts is not None:
        value = jnp.where(counts, value, jnp.zeros_like(value))
        one = jnp.where(counts, one, jnp.zeros_like(one))
    values[rows, :HEAD_DIM] = value
    values[rows, HEAD_DIM:] = one


def near_kernel(sizes, q_ref, k_ref, v_ref, before_ref, after_ref, global_ref, out_ref, lse_ref, keys, values):
    n_pb, n_ctx, n_dev, slots = sizes
    n_blocks = n_pb * n_ctx * n_dev
    i = pl.program_id(0)
    row = (lax.axis_index("pb") * n_ctx + lax.axis_index("ctx")) * n_dev + i
    for g in range(GLOBAL):
        put(keys, values, g, (global_ref[g, 0], global_ref[g, 1]))
    for slot, step in enumerate((-1, 0, 1), GLOBAL):
        counts = jnp.logical_and(row + step >= GLOBAL, row + step < n_blocks)
        inside = jnp.logical_and(i + step >= 0, i + step < n_dev)
        here = jnp.logical_and(counts, inside)

        @pl.when(here)
        def _():
            put(keys, values, slot, (k_ref[i + step], v_ref[i + step]))

        @pl.when(jnp.logical_not(counts))
        def _():
            put(keys, values, slot, (global_ref[0, 0], global_ref[0, 1]), False)

        if step != 0:
            other = before_ref if step < 0 else after_ref

            @pl.when(jnp.logical_and(counts, jnp.logical_not(inside)))
            def _():
                put(keys, values, slot, other[0])

    attend(q_ref, keys, values, None, out_ref, lse_ref)


def random_kernel(places, table_at, plan_ref, q_ref, o_ref, l_ref, *rest):
    parts, (out_ref, keys, values, pool, sems) = rest[: len(places)], rest[len(places) :]
    i = pl.program_id(0)

    @pl.when(i == 0)
    def _():
        copies = []
        for n, (part, (at, which)) in enumerate(zip(parts, places)):
            rows = pl.ds(at, part.shape[0])
            target = pool.at[rows] if which is None else pool.at[rows, which]
            copies.append(pltpu.make_async_copy(part, target, sems.at[n]))
        for copy in copies:
            copy.start()
        values[:, HEAD_DIM:] = jnp.ones((RANDOM * BLOCK, HEAD_DIM), jnp.bfloat16)
        for copy in copies:
            copy.wait()

    for j in range(RANDOM):
        block = plan_ref[table_at + i * RANDOM + j]
        rows = slice(j * BLOCK, (j + 1) * BLOCK)
        keys[rows, :] = pool[block, 0]
        values[rows, :HEAD_DIM] = pool[block, 1]
    attend(q_ref, keys, values, (o_ref, l_ref), out_ref, None)


def shift_plan_kernel(sizes, list_ref, plan_ref, counts):
    n_pb, n_ctx, n_dev, slots = sizes
    n_blocks = n_pb * n_ctx * n_dev
    me = lax.axis_index("ctx")
    group = lax.axis_index("pb") * (n_ctx * n_dev)
    for h in range(n_ctx):
        counts[h] = 0
    for r in range(n_dev):
        row = me * n_dev + r
        start = row * LIST + random_start(group + row, n_blocks)
        for j in range(RANDOM):
            holder = (list_ref[start + j] - group) // n_dev
            rank = counts[holder]
            counts[holder] = rank + 1
            shift = lax.rem(me - holder + n_ctx, n_ctx)
            plan_ref[r * RANDOM + j] = (shift - 1) * slots + rank


def shift_round(sizes, lists, keys, values):
    n_pb, n_ctx, n_dev, slots = sizes
    plan = pl.pallas_call(
        lambda *refs: shift_plan_kernel(sizes, *refs),
        out_shape=jax.ShapeDtypeStruct((n_dev * RANDOM,), jnp.int32),
        in_specs=[SMEM],
        out_specs=SMEM,
        scratch_shapes=[pltpu.SMEM((n_ctx,), jnp.int32)],
        name="plan",
    )(lists)
    parts = []
    for shift, part in enumerate(gather(sizes, lists, keys, values), 1):
        got = lax.ppermute(part, "ctx", [(i, (i + shift) % n_ctx) for i in range(n_ctx)])
        parts.append((got, (shift - 1) * slots, None))
    return plan, parts


def call(kernel, name, n_dev, scalars, tiled, whole, parts, n_blocks, last, cost, scratch=()):
    width = HEADS * HEAD_DIM

    def tile(n):
        return pl.BlockSpec((BLOCK, n), lambda i: (i, 0))

    out_shape = [jax.ShapeDtypeStruct((n_dev * BLOCK, width), jnp.bfloat16 if last else jnp.float32)]
    if not last:
        out_shape.append(jax.ShapeDtypeStruct((n_dev * BLOCK, HEAD_DIM), jnp.float32))
    return pl.pallas_call(
        kernel,
        grid=(n_dev,),
        out_shape=out_shape,
        in_specs=[SMEM] * len(scalars)
        + [tile(a.shape[1]) for a in tiled]
        + [VMEM] * len(whole)
        + [pl.BlockSpec(memory_space=pl.ANY)] * len(parts),
        out_specs=[tile(a.shape[1]) for a in out_shape],
        scratch_shapes=[
            pltpu.VMEM((n_blocks * BLOCK, HEAD_DIM), jnp.bfloat16),
            pltpu.VMEM((n_blocks * BLOCK, 2 * HEAD_DIM), jnp.bfloat16),
            *scratch,
        ],
        cost_estimate=pl.CostEstimate(flops=cost, transcendentals=0, bytes_accessed=0),
        name=name,
    )(*scalars, *tiled, *whole, *parts)


def neighbours(first, last):
    axes = ("pb", "ctx")
    n = lax.axis_size(axes)
    up = [(i, i + 1) for i in range(n - 1)]
    down = [(i + 1, i) for i in range(n - 1)]
    return lax.ppermute(last, axes, up), lax.ppermute(first, axes, down)


def spread(shared):
    n_ctx, n_pb = lax.axis_size("ctx"), lax.axis_size("pb")
    column, group = lax.axis_index("ctx"), lax.axis_index("pb")
    axes = ("pb", "ctx")
    received = [lax.ppermute(shared, axes, [(0, far)]) for far in range(2, n_ctx, 2)]
    for far, got in zip(range(2, n_ctx, 2), received):
        shared = jnp.where(column == far, got, shared)
    got = lax.ppermute(shared, axes, [(c, c + 1) for c in range(0, n_ctx, 2)])
    shared = jnp.where(column % 2 == 1, got, shared)
    have = 1
    while have < n_pb:
        pairs = [(i, i + have) for i in range(min(have, n_pb - have))]
        got = lax.ppermute(shared, "pb", pairs)
        shared = jnp.where(jnp.logical_and(group >= have, group < 2 * have), got, shared)
        have *= 2
    return shared


def per_device(queries, key_states, value_states, key_blocks):
    n_pb, n_ctx = lax.axis_size("pb"), lax.axis_size("ctx")
    n_dev = queries.shape[0] // BLOCK
    slots = (RANDOM * n_dev + n_ctx - 2) // (n_ctx - 1)
    sizes = (n_pb, n_ctx, n_dev, slots)
    keys = key_states.reshape(n_dev, BLOCK, HEAD_DIM)
    values = value_states.reshape(n_dev, BLOCK, HEAD_DIM)
    lists = group_rows(key_blocks)
    if n_ctx == 8:
        plan = make_plan(sizes, lists)
        table_at = 2 * (slots + slots // 2)
        parts = pass_round(sizes, plan, keys, values)
    else:
        table_at = 0
        plan, parts = shift_round(sizes, lists, keys, values)
    first = jnp.stack([keys[:GLOBAL], values[:GLOBAL]], axis=1)
    last = jnp.stack([keys[-1:], values[-1:]], axis=1)
    before, after = neighbours(first[:1], last)
    shared = spread(first)
    out, lse = call(
        lambda *refs: near_kernel(sizes, *refs), "near", n_dev, [], [queries],
        [keys, values, before, after, shared], [], GLOBAL + 3, False, COST,
    )
    places = [part[1:] for part in parts]
    n_pool = max(at + part.shape[0] for part, at, _ in parts)
    (out,) = call(
        lambda *refs: random_kernel(places, table_at, *refs), "random", n_dev, [plan], [queries, out, lse], [],
        [part[0] for part in parts], RANDOM, True, COST,
        scratch=[
            pltpu.VMEM((n_pool, 2, BLOCK, HEAD_DIM), jnp.bfloat16),
            pltpu.SemaphoreType.DMA((len(parts),)),
        ],
    )
    return out


def solution(mesh):
    in_specs = (P(("pb", "ctx"), None), P(("pb", "ctx"), None), P(("pb", "ctx"), None), P())
    out_specs = P(("pb", "ctx"), None)
    return jax.shard_map(
        per_device, mesh=mesh, in_specs=in_specs, out_specs=out_specs, check_vma=False
    )
```

time: 247 us -> 86 us (0.35)
  the two profiles are of different devices: /device:TPU:0 before, /device:TPU:1 now
where the time goes in v1:
time: 86 us; the launch traced here: 85.2 us
  starting transfers between devices  37 us (43%)
  Pallas kernels  31.1 us (36%)
  waiting for transfers between devices  8.41 us (10%)
  local copies, waits for them, and re-layouts  7.56 us (9%)
    pallas_call x2, Pallas kernels, call(): pl.pallas_call(kernel, grid=(n_dev,), out_shape=out_shape, in_specs=[SMEM...  25.3 us
    ppermute x2, starting transfers between devices, neighbours(): return (lax.ppermute(last, axes, up), lax.ppermute(first, axes, down))  15.1 us
    ppermute x8, starting transfers between devices, pass_round(): k, v = (lax.ppermute(k, 'ctx', pairs), lax.ppermute(v, 'ctx', pairs))  12.1 us
    ppermute x2, waiting for transfers between devices, spread(): got = lax.ppermute(shared, 'pb', pairs)  5.51 us
    pallas_call x2, Pallas kernels, pick(): pl.pallas_call(lambda *refs: pick_kernel(side * (slots + half), half, slo...  3.62 us
    unnamed x30, local copies, waits for them, and re-layouts  3.51 us
    ppermute x2, waiting for transfers between devices, neighbours(): return (lax.ppermute(last, axes, up), lax.ppermute(first, axes, down))  2.86 us
    ppermute x2, starting transfers between devices, spread(): got = lax.ppermute(shared, 'pb', pairs)  2.59 us
  transfers between devices with their start and end apart: 22, of which 2 were waited for; matrix products, arithmetic and copies ran while one was open for 4% of the time, Pallas kernels for 22%

profile of v1, /device:TPU:1, one launch (start us, length us, event | category | flops | bytes accessed | tf_op | source)
XLA Modules:
  0.0 85.2 jit_solution(8846538051797910954)
XLA Ops:
  0.0 0.9 %slice.21 = bf16[256,128]{1,0:T(8,128)(2,1)S(1)} slice(bf16[1024,128]{1,0:T(8,128)(2,1)} %param.5), slice={[0:256], [0:128]} | slice | bytes 131072 | tf_op jit(solution)/shard_map/slice | solution.py:392
  0.9 0.8 slice.22
  1.7 0.7 collective-permute-start.3
  2.4 0.7 collective-permute-start.2
  3.1 0.7 collective-permute-start.4
  3.8 2.1 %collective-permute-start.15 = (bf16[8,128,128]{2,1,0:T(8,128)(2,1)}, bf16[8,128,128]{2,1,0:T(8,128)(2,1)S(1)}, u32[]{:S(2)}, u32[]{:S(2)}) collective-permute-start(bf16[8,128,128]{2,1,0:T(8,128)(2,1)} %bitcast.14), channel_id=1, source_target_pairs={{0,1},{2,0},{4,2},{6,4},{7,6},{5,7},{3,5},{1,3},{8,9},{10,8},{12,1... | collective-permute-start | bytes 786440 | tf_op jit(solution)/shard_map/ppermute | solution.py:137
  5.8 0.2 collective-permute-start.8
  6.0 0.0 collective-permute-done.3
  6.0 1.3 %collective-permute-start.16 = (bf16[8,128,128]{2,1,0:T(8,128)(2,1)}, bf16[8,128,128]{2,1,0:T(8,128)(2,1)S(1)}, u32[]{:S(2)}, u32[]{:S(2)}) collective-permute-start(bf16[8,128,128]{2,1,0:T(8,128)(2,1)} %bitcast.17), channel_id=1, source_target_pairs={{0,1},{2,0},{4,2},{6,4},{7,6},{5,7},{3,5},{1,3},{8,9},{10,8},{12,1... | collective-permute-start | bytes 786440 | tf_op jit(solution)/shard_map/ppermute | solution.py:137
  7.3 0.0 collective-permute-done.2
  7.3 0.2 collective-permute-start.9
  7.5 0.0 collective-permute-done.4
  7.5 0.7 collective-permute-start.5
  8.2 0.8 slice_bitcast_fusion.1
  8.9 0.0 collective-permute-done.5
  9.0 1.3 %collective-permute-start.6 = (bf16[2,2,128,128]{3,2,1,0:T(8,128)(2,1)S(1)}, bf16[2,2,128,128]{3,2,1,0:T(8,128)(2,1)S(1)}, u32[]{:S(2)}, u32[]{:S(2)}) collective-permute-start(bf16[2,2,128,128]{3,2,1,0:T(8,128)(2,1)S(1)} %broadcast_select_fusion), channel_id=1, source_target_pairs={{0,8},{1,9},{2,10},{3,11},{4,12},{5,13},{6,14},{7,15}} | collective-permute-start | bytes 393224 | tf_op jit(solution)/shard_map/ppermute | solution.py:371
  10.3 0.0 collective-permute-done.15.refs_10_
  10.3 2.1 %collective-permute-start.17 = (bf16[8,128,128]{2,1,0:T(8,128)(2,1)S(1)}, bf16[8,128,128]{2,1,0:T(8,128)(2,1)S(1)}, u32[]{:S(2)}, u32[]{:S(2)}) collective-permute-start(bf16[8,128,128]{2,1,0:T(8,128)(2,1)S(1)} %collective-permute-done.15.refs_10_), channel_id=1, source_target_pairs={{0,1},{2,0},{4,2},{6,4},{7,6},{5,7},{3,5},{1,3},{8,9},{10,8},{12,1... | collective-permute-start | bytes 786440 | tf_op jit(solution)/shard_map/ppermute | solution.py:137
  12.4 0.0 collective-permute-done.8.refs_4_
  12.4 0.3 collective-permute-start.10
  12.8 0.0 collective-permute-done.16.refs_11_
  12.8 5.3 %collective-permute-start.18 = (bf16[8,128,128]{2,1,0:T(8,128)(2,1)S(1)}, bf16[8,128,128]{2,1,0:T(8,128)(2,1)S(1)}, u32[]{:S(2)}, u32[]{:S(2)}) collective-permute-start(bf16[8,128,128]{2,1,0:T(8,128)(2,1)S(1)} %collective-permute-done.16.refs_11_), channel_id=1, source_target_pairs={{0,1},{2,0},{4,2},{6,4},{7,6},{5,7},{3,5},{1,3},{8,9},{10,8},{12,1... | collective-permute-start | bytes 786440 | tf_op jit(solution)/shard_map/ppermute | solution.py:137
  18.1 0.0 collective-permute-done.9.refs_5_
  18.1 0.7 collective-permute-start.11
  18.8 0.1 constant_dynamic-slice_fusion
  18.8 0.1 copy.5
  18.9 0.7 reshape.17.refs_0_
  19.6 2.2 %plan.1.refs_0_ = s32[37]{0:T(128)} custom-call(s32[512]{0:T(512)} %reshape.17.refs_0_), custom_call_target="tpu_custom_call" | custom-call | tf_op jit(solution)/shard_map/plan/pallas_call | solution.py:96
  21.8 5.5 %collective-permute-done.6 = bf16[2,2,128,128]{3,2,1,0:T(8,128)(2,1)S(1)} collective-permute-done((bf16[2,2,128,128]{3,2,1,0:T(8,128)(2,1)S(1)}, bf16[2,2,128,128]{3,2,1,0:T(8,128)(2,1)S(1)}, u32[]{:S(2)}, u32[]{:S(2)}) %collective-permute-start.6) | collective-permute-done | bytes 131104 | tf_op jit(solution)/shard_map/ppermute | solution.py:371
  27.4 13.2 %collective-permute-start.1 = (bf16[1,2,128,128]{3,2,1,0:T(8,128)(2,1)S(1)}, bf16[1,2,128,128]{3,2,1,0:T(8,128)(2,1)S(1)}, u32[]{:S(2)}, u32[]{:S(2)}) collective-permute-start(bf16[1,2,128,128]{3,2,1,0:T(8,128)(2,1)S(1)} %fusion), channel_id=1, source_target_pairs={{1,0},{2,1},{3,2},{4,3},{5,4},{6,5},{7,6},{8,7},{9,8},{10,9},{11,1... | collective-permute-start | bytes 196616 | tf_op jit(solution)/shard_map/ppermute | solution.py:356
  40.6 0.0 collective-permute-done.10.refs_1_.refs_6_
  40.6 1.3 %collective-permute-start.7 = (bf16[2,2,128,128]{3,2,1,0:T(8,128)(2,1)S(1)}, bf16[2,2,128,128]{3,2,1,0:T(8,128)(2,1)S(1)}, u32[]{:S(2)}, u32[]{:S(2)}) collective-permute-start(bf16[2,2,128,128]{3,2,1,0:T(8,128)(2,1)S(1)} %broadcast_select_fusion.1), channel_id=1, source_target_pairs={{0,16},{8,24},{1,17},{9,25},{2,18},{10,26},{3,19},{11,27},{4,20},{... | collective-permute-start | bytes 393224 | tf_op jit(solution)/shard_map/ppermute | solution.py:371
  41.9 0.0 collective-permute-done.11.refs_2_.refs_7_
  42.0 0.7 copy-done.4
  42.6 1.8 %pick.2 = (bf16[2,2,128,128]{3,2,1,0:T(8,128)(2,1)}, bf16[4,2,128,128]{3,2,1,0:T(8,128)(2,1)}) custom-call(s32[37]{0:T(128)} %plan.1.refs_0_, bf16[8,128,128]{2,1,0:T(8,128)(2,1)} %copy-done.2, bf16[8,128,128]{2,1,0:T(8,128)(2,1)} %copy-done.4), custom_call_target="tpu_custom_call" | custom-call | tf_op jit(solution)/shard_map/pick/pallas_call | solution.py:116
  44.4 0.0 collective-permute-start.12
  44.5 0.0 collective-permute-done.17.refs_1_.refs_12_
  44.5 0.0 collective-permute-done.18.refs_2_.refs_13_
  44.5 0.7 copy-done.1
  45.2 0.7 copy-done.3
  45.9 1.8 %pick.3 = (bf16[2,2,128,128]{3,2,1,0:T(8,128)(2,1)}, bf16[4,2,128,128]{3,2,1,0:T(8,128)(2,1)}) custom-call(s32[37]{0:T(128)} %plan.1.refs_0_, bf16[8,128,128]{2,1,0:T(8,128)(2,1)} %copy-done.1, bf16[8,128,128]{2,1,0:T(8,128)(2,1)} %copy-done.3), custom_call_target="tpu_custom_call" | custom-call | tf_op jit(solution)/shard_map/pick/pallas_call | solution.py:116
  47.7 1.5 %collective-permute-start.19 = (bf16[2,2,128,128]{3,2,1,0:T(8,128)(2,1)}, bf16[2,2,128,128]{3,2,1,0:T(8,128)(2,1)S(1)}, u32[]{:S(2)}, u32[]{:S(2)}) collective-permute-start(bf16[2,2,128,128]{3,2,1,0:T(8,128)(2,1)} %get-tuple-element.15), channel_id=1, source_target_pairs={{0,1},{2,0},{4,2},{6,4},{7,6},{5,7},{3,5},{1,3},{8,9},{10,8},{12,1... | collective-permute-start | bytes 393224 | tf_op jit(solution)/shard_map/ppermute | solution.py:141
  49.1 0.8 slice_bitcast_fusion
  49.9 1.9 %collective-permute-start = (bf16[1,2,128,128]{3,2,1,0:T(8,128)(2,1)S(1)}, bf16[1,2,128,128]{3,2,1,0:T(8,128)(2,1)S(1)}, u32[]{:S(2)}, u32[]{:S(2)}) collective-permute-start(bf16[1,2,128,128]{3,2,1,0:T(8,128)(2,1)S(1)} %pad_maximum_fusion.1), channel_id=1, source_target_pairs={{0,1},{1,2},{2,3},{3,4},{4,5},{5,6},{6,7},{7,8},{8,9},{9,10},{10,1... | collective-permute-start | bytes 196616 | tf_op jit(solution)/shard_map/ppermute | solution.py:356
  51.8 0.0 collective-permute-done.1.refs_4_
  51.9 0.1 collective-permute-start.14
  51.9 0.0 collective-permute-done.7
  51.9 1.4 %collective-permute-start.21 = (bf16[4,2,128,128]{3,2,1,0:T(8,128)(2,1)}, bf16[4,2,128,128]{3,2,1,0:T(8,128)(2,1)S(1)}, u32[]{:S(2)}, u32[]{:S(2)}) collective-permute-start(bf16[4,2,128,128]{3,2,1,0:T(8,128)(2,1)} %get-tuple-element.16), channel_id=1, source_target_pairs={{0,1},{2,0},{4,2},{6,4},{7,6},{5,7},{3,5},{1,3},{8,9},{10,8},{12,1... | collective-permute-start | bytes 786440 | tf_op jit(solution)/shard_map/ppermute | solution.py:142
  53.4 0.0 collective-permute-done.12
  53.4 0.1 collective-permute-start.13
  53.5 0.0 collective-permute-done.19
  53.5 1.4 %collective-permute-start.20 = (bf16[2,2,128,128]{3,2,1,0:T(8,128)(2,1)S(1)}, bf16[2,2,128,128]{3,2,1,0:T(8,128)(2,1)S(1)}, u32[]{:S(2)}, u32[]{:S(2)}) collective-permute-start(bf16[2,2,128,128]{3,2,1,0:T(8,128)(2,1)S(1)} %collective-permute-done.19), channel_id=1, source_target_pairs={{0,1},{2,0},{4,2},{6,4},{7,6},{5,7},{3,5},{1,3},{8,9},{10,8},{12,1... | collective-permute-start | bytes 393224 | tf_op jit(solution)/shard_map/ppermute | solution.py:143
  54.9 0.7 broadcast_select_fusion.2.refs_5_
  55.5 2.9 %collective-permute-done.refs_3_ = bf16[1,2,128,128]{3,2,1,0:T(8,128)(2,1)S(1)} collective-permute-done((bf16[1,2,128,128]{3,2,1,0:T(8,128)(2,1)S(1)}, bf16[1,2,128,128]{3,2,1,0:T(8,128)(2,1)S(1)}, u32[]{:S(2)}, u32[]{:S(2)}) %collective-permute-start) | collective-permute-done | bytes 65568 | tf_op jit(solution)/shard_map/ppermute | solution.py:356
  58.4 0.6 copy-done.14
  59.0 13.0 %near.1 = (f32[1024,1024]{1,0:T(8,128)}, f32[1024,128]{1,0:T(8,128)}) custom-call(bf16[1024,1024]{1,0:T(8,128)(2,1)} %refs_1_.1, bf16[8,128,128]{2,1,0:T(8,128)(2,1)} %bitcast.16, bf16[8,128,128]{2,1,0:T(8,128)(2,1)} %bitcast.19, bf16[1,2,128,128]{3,2,1,0:T(8,128)(2,1)} %copy-done.14, bf16[1,2,128,128]{3,2,1,0:T(8,128)(2,1)} %copy-done.13, ...), custom_call_target="tpu_custom_call" | custom-call | flops 1073741824 | tf_op jit(solution)/shard_map/near/pallas_call | solution.py:332
  72.0 0.0 collective-permute-done.14.refs_9_
  72.1 0.0 collective-permute-done.13.refs_8_
  72.1 0.0 collective-permute-done.20.refs_14_
  72.1 0.6 copy-done.9
  72.7 0.1 copy-done.10
  72.8 0.1 copy-done.11
  72.9 0.0 copy-done.12
  72.9 12.2 %random.1 = bf16[1024,1024]{1,0:T(8,128)(2,1)} custom-call(s32[37]{0:T(128)} %plan.1.refs_0_, bf16[1024,1024]{1,0:T(8,128)(2,1)} %refs_1_.1, f32[1024,1024]{1,0:T(8,128)} %get-tuple-element.11.refs_2_, f32[1024,128]{1,0:T(8,128)} %get-tuple-element.12.refs_3_, bf16[8,128,128]{2,1,0:T(8,128)(2,1)} %copy-done.6, bf16[8,128,128]{2,1,0:T(8,128)(2,1)} %copy-done.8, ...), custom_call_target="tpu_custom_call" | custom-call | flops 1073741824 | tf_op jit(solution)/shard_map/random/pallas_call | solution.py:332
  (29 shorter events, 0.1 us)
Async XLA Ops:
  0.0 18.8 %copy-start = (s32[256,8]{0,1:T(8,128)S(1)}, s32[256,8]{0,1:T(8,128)}, u32[]{:S(2)}) copy-start(s32[256,8]{0,1:T(8,128)} %param.7) | copy-start | bytes 24580
  1.7 4.3 %collective-permute-start.3 = (bf16[2,2,128,128]{3,2,1,0:T(8,128)(2,1)S(1)}, bf16[2,2,128,128]{3,2,1,0:T(8,128)(2,1)S(1)}, u32[]{:S(2)}, u32[]{:S(2)}) collective-permute-start(bf16[2,2,128,128]{3,2,1,0:T(8,128)(2,1)S(1)} %pad_maximum_fusion), channel_id=1, source_target_pairs={{0,4}} | collective-permute-start | bytes 393224 | tf_op jit(solution)/shard_map/ppermute | solution.py:363
  2.4 4.9 %collective-permute-start.2 = (bf16[2,2,128,128]{3,2,1,0:T(8,128)(2,1)S(1)}, bf16[2,2,128,128]{3,2,1,0:T(8,128)(2,1)S(1)}, u32[]{:S(2)}, u32[]{:S(2)}) collective-permute-start(bf16[2,2,128,128]{3,2,1,0:T(8,128)(2,1)S(1)} %pad_maximum_fusion), channel_id=1, source_target_pairs={{0,6}} | collective-permute-start | bytes 393224 | tf_op jit(solution)/shard_map/ppermute | solution.py:363
  3.1 4.4 %collective-permute-start.4 = (bf16[2,2,128,128]{3,2,1,0:T(8,128)(2,1)S(1)}, bf16[2,2,128,128]{3,2,1,0:T(8,128)(2,1)S(1)}, u32[]{:S(2)}, u32[]{:S(2)}) collective-permute-start(bf16[2,2,128,128]{3,2,1,0:T(8,128)(2,1)S(1)} %pad_maximum_fusion), channel_id=1, source_target_pairs={{0,2}} | collective-permute-start | bytes 393224 | tf_op jit(solution)/shard_map/ppermute | solution.py:363
  3.8 6.5 %collective-permute-start.15 = (bf16[8,128,128]{2,1,0:T(8,128)(2,1)}, bf16[8,128,128]{2,1,0:T(8,128)(2,1)S(1)}, u32[]{:S(2)}, u32[]{:S(2)}) collective-permute-start(bf16[8,128,128]{2,1,0:T(8,128)(2,1)} %bitcast.14), channel_id=1, source_target_pairs={{0,1},{2,0},{4,2},{6,4},{7,6},{5,7},{3,5},{1,3},{8,9},{10,8},{12,1... | collective-permute-start | bytes 786440 | tf_op jit(solution)/shard_map/ppermute | solution.py:137
  5.8 6.6 %collective-permute-start.8 = (bf16[8,128,128]{2,1,0:T(8,128)(2,1)}, bf16[8,128,128]{2,1,0:T(8,128)(2,1)S(1)}, u32[]{:S(2)}, u32[]{:S(2)}) collective-permute-start(bf16[8,128,128]{2,1,0:T(8,128)(2,1)} %bitcast.15), channel_id=1, source_target_pairs={{0,2},{2,4},{4,6},{6,7},{7,5},{5,3},{3,1},{1,0},{8,10},{10,12},{12... | collective-permute-start | bytes 786440 | tf_op jit(solution)/shard_map/ppermute | solution.py:137
  6.0 6.8 %collective-permute-start.16 = (bf16[8,128,128]{2,1,0:T(8,128)(2,1)}, bf16[8,128,128]{2,1,0:T(8,128)(2,1)S(1)}, u32[]{:S(2)}, u32[]{:S(2)}) collective-permute-start(bf16[8,128,128]{2,1,0:T(8,128)(2,1)} %bitcast.17), channel_id=1, source_target_pairs={{0,1},{2,0},{4,2},{6,4},{7,6},{5,7},{3,5},{1,3},{8,9},{10,8},{12,1... | collective-permute-start | bytes 786440 | tf_op jit(solution)/shard_map/ppermute | solution.py:137
  7.3 10.7 %collective-permute-start.9 = (bf16[8,128,128]{2,1,0:T(8,128)(2,1)}, bf16[8,128,128]{2,1,0:T(8,128)(2,1)S(1)}, u32[]{:S(2)}, u32[]{:S(2)}) collective-permute-start(bf16[8,128,128]{2,1,0:T(8,128)(2,1)} %bitcast.18), channel_id=1, source_target_pairs={{0,2},{2,4},{4,6},{6,7},{7,5},{5,3},{3,1},{1,0},{8,10},{10,12},{12... | collective-permute-start | bytes 786440 | tf_op jit(solution)/shard_map/ppermute | solution.py:137
  7.5 1.4 %collective-permute-start.5 = (bf16[2,2,128,128]{3,2,1,0:T(8,128)(2,1)S(1)}, bf16[2,2,128,128]{3,2,1,0:T(8,128)(2,1)S(1)}, u32[]{:S(2)}, u32[]{:S(2)}) collective-permute-start(bf16[2,2,128,128]{3,2,1,0:T(8,128)(2,1)S(1)} %select_select_fusion), channel_id=1, source_target_pairs={{0,1},{2,3},{4,5},{6,7}} | collective-permute-start | bytes 393224 | tf_op jit(solution)/shard_map/ppermute | solution.py:366
  9.0 18.4 %collective-permute-start.6 = (bf16[2,2,128,128]{3,2,1,0:T(8,128)(2,1)S(1)}, bf16[2,2,128,128]{3,2,1,0:T(8,128)(2,1)S(1)}, u32[]{:S(2)}, u32[]{:S(2)}) collective-permute-start(bf16[2,2,128,128]{3,2,1,0:T(8,128)(2,1)S(1)} %broadcast_select_fusion), channel_id=1, source_target_pairs={{0,8},{1,9},{2,10},{3,11},{4,12},{5,13},{6,14},{7,15}} | collective-permute-start | bytes 393224 | tf_op jit(solution)/shard_map/ppermute | solution.py:371
  10.3 61.7 %copy-start.5 = (bf16[8,128,128]{2,1,0:T(8,128)(2,1)}, bf16[8,128,128]{2,1,0:T(8,128)(2,1)S(1)}, u32[]{:S(2)}) copy-start(bf16[8,128,128]{2,1,0:T(8,128)(2,1)S(1)} %collective-permute-done.15.refs_10_) | copy-start | bytes 786436
  10.3 34.1 %collective-permute-start.17 = (bf16[8,128,128]{2,1,0:T(8,128)(2,1)S(1)}, bf16[8,128,128]{2,1,0:T(8,128)(2,1)S(1)}, u32[]{:S(2)}, u32[]{:S(2)}) collective-permute-start(bf16[8,128,128]{2,1,0:T(8,128)(2,1)S(1)} %collective-permute-done.15.refs_10_), channel_id=1, source_target_pairs={{0,1},{2,0},{4,2},{6,4},{7,6},{5,7},{3,5},{1,3},{8,9},{10,8},{12,1... | collective-permute-start | bytes 786440 | tf_op jit(solution)/shard_map/ppermute | solution.py:137
  12.4 59.7 %copy-start.6 = (bf16[8,128,128]{2,1,0:T(8,128)(2,1)}, bf16[8,128,128]{2,1,0:T(8,128)(2,1)S(1)}, u32[]{:S(2)}) copy-start(bf16[8,128,128]{2,1,0:T(8,128)(2,1)S(1)} %collective-permute-done.8.refs_4_) | copy-start | bytes 786436
  12.4 28.2 %collective-permute-start.10 = (bf16[8,128,128]{2,1,0:T(8,128)(2,1)S(1)}, bf16[8,128,128]{2,1,0:T(8,128)(2,1)S(1)}, u32[]{:S(2)}, u32[]{:S(2)}) collective-permute-start(bf16[8,128,128]{2,1,0:T(8,128)(2,1)S(1)} %collective-permute-done.8.refs_4_), channel_id=1, source_target_pairs={{0,2},{2,4},{4,6},{6,7},{7,5},{5,3},{3,1},{1,0},{8,10},{10,12},{12... | collective-permute-start | bytes 786440 | tf_op jit(solution)/shard_map/ppermute | solution.py:137
  12.8 59.3 %copy-start.7 = (bf16[8,128,128]{2,1,0:T(8,128)(2,1)}, bf16[8,128,128]{2,1,0:T(8,128)(2,1)S(1)}, u32[]{:S(2)}) copy-start(bf16[8,128,128]{2,1,0:T(8,128)(2,1)S(1)} %collective-permute-done.16.refs_11_) | copy-start | bytes 786436
  12.8 31.7 %collective-permute-start.18 = (bf16[8,128,128]{2,1,0:T(8,128)(2,1)S(1)}, bf16[8,128,128]{2,1,0:T(8,128)(2,1)S(1)}, u32[]{:S(2)}, u32[]{:S(2)}) collective-permute-start(bf16[8,128,128]{2,1,0:T(8,128)(2,1)S(1)} %collective-permute-done.16.refs_11_), channel_id=1, source_target_pairs={{0,1},{2,0},{4,2},{6,4},{7,6},{5,7},{3,5},{1,3},{8,9},{10,8},{12,1... | collective-permute-start | bytes 786440 | tf_op jit(solution)/shard_map/ppermute | solution.py:137
  18.1 54.1 %copy-start.8 = (bf16[8,128,128]{2,1,0:T(8,128)(2,1)}, bf16[8,128,128]{2,1,0:T(8,128)(2,1)S(1)}, u32[]{:S(2)}) copy-start(bf16[8,128,128]{2,1,0:T(8,128)(2,1)S(1)} %collective-permute-done.9.refs_5_) | copy-start | bytes 786436
  18.1 23.9 %collective-permute-start.11 = (bf16[8,128,128]{2,1,0:T(8,128)(2,1)S(1)}, bf16[8,128,128]{2,1,0:T(8,128)(2,1)S(1)}, u32[]{:S(2)}, u32[]{:S(2)}) collective-permute-start(bf16[8,128,128]{2,1,0:T(8,128)(2,1)S(1)} %collective-permute-done.9.refs_5_), channel_id=1, source_target_pairs={{0,2},{2,4},{4,6},{6,7},{7,5},{5,3},{3,1},{1,0},{8,10},{10,12},{12... | collective-permute-start | bytes 786440 | tf_op jit(solution)/shard_map/ppermute | solution.py:137
  27.4 24.5 %collective-permute-start.1 = (bf16[1,2,128,128]{3,2,1,0:T(8,128)(2,1)S(1)}, bf16[1,2,128,128]{3,2,1,0:T(8,128)(2,1)S(1)}, u32[]{:S(2)}, u32[]{:S(2)}) collective-permute-start(bf16[1,2,128,128]{3,2,1,0:T(8,128)(2,1)S(1)} %fusion), channel_id=1, source_target_pairs={{1,0},{2,1},{3,2},{4,3},{5,4},{6,5},{7,6},{8,7},{9,8},{10,9},{11,1... | collective-permute-start | bytes 196616 | tf_op jit(solution)/shard_map/ppermute | solution.py:356
  40.6 1.3 %copy-start.2 = (bf16[8,128,128]{2,1,0:T(8,128)(2,1)}, bf16[8,128,128]{2,1,0:T(8,128)(2,1)S(1)}, u32[]{:S(2)}) copy-start(bf16[8,128,128]{2,1,0:T(8,128)(2,1)S(1)} %collective-permute-done.10.refs_1_.refs_6_) | copy-start | bytes 786436
  40.6 11.3 %collective-permute-start.7 = (bf16[2,2,128,128]{3,2,1,0:T(8,128)(2,1)S(1)}, bf16[2,2,128,128]{3,2,1,0:T(8,128)(2,1)S(1)}, u32[]{:S(2)}, u32[]{:S(2)}) collective-permute-start(bf16[2,2,128,128]{3,2,1,0:T(8,128)(2,1)S(1)} %broadcast_select_fusion.1), channel_id=1, source_target_pairs={{0,16},{8,24},{1,17},{9,25},{2,18},{10,26},{3,19},{11,27},{4,20},{... | collective-permute-start | bytes 393224 | tf_op jit(solution)/shard_map/ppermute | solution.py:371
  41.9 0.7 copy-start.4
  44.4 8.9 %collective-permute-start.12 = (bf16[2,2,128,128]{3,2,1,0:T(8,128)(2,1)}, bf16[2,2,128,128]{3,2,1,0:T(8,128)(2,1)S(1)}, u32[]{:S(2)}, u32[]{:S(2)}) collective-permute-start(bf16[2,2,128,128]{3,2,1,0:T(8,128)(2,1)} %get-tuple-element.13), channel_id=1, source_target_pairs={{0,2},{2,4},{4,6},{6,7},{7,5},{5,3},{3,1},{1,0},{8,10},{10,12},{12... | collective-permute-start | bytes 393224 | tf_op jit(solution)/shard_map/ppermute | solution.py:141
  44.5 0.7 copy-start.1
  45.2 0.7 copy-start.3
  47.7 5.8 %collective-permute-start.19 = (bf16[2,2,128,128]{3,2,1,0:T(8,128)(2,1)}, bf16[2,2,128,128]{3,2,1,0:T(8,128)(2,1)S(1)}, u32[]{:S(2)}, u32[]{:S(2)}) collective-permute-start(bf16[2,2,128,128]{3,2,1,0:T(8,128)(2,1)} %get-tuple-element.15), channel_id=1, source_target_pairs={{0,1},{2,0},{4,2},{6,4},{7,6},{5,7},{3,5},{1,3},{8,9},{10,8},{12,1... | collective-permute-start | bytes 393224 | tf_op jit(solution)/shard_map/ppermute | solution.py:141
  49.9 8.5 %collective-permute-start = (bf16[1,2,128,128]{3,2,1,0:T(8,128)(2,1)S(1)}, bf16[1,2,128,128]{3,2,1,0:T(8,128)(2,1)S(1)}, u32[]{:S(2)}, u32[]{:S(2)}) collective-permute-start(bf16[1,2,128,128]{3,2,1,0:T(8,128)(2,1)S(1)} %pad_maximum_fusion.1), channel_id=1, source_target_pairs={{0,1},{1,2},{2,3},{3,4},{4,5},{5,6},{6,7},{7,8},{8,9},{9,10},{10,1... | collective-permute-start | bytes 196616 | tf_op jit(solution)/shard_map/ppermute | solution.py:356
  51.9 6.5 %copy-start.13 = (bf16[1,2,128,128]{3,2,1,0:T(8,128)(2,1)}, bf16[1,2,128,128]{3,2,1,0:T(8,128)(2,1)S(1)}, u32[]{:S(2)}) copy-start(bf16[1,2,128,128]{3,2,1,0:T(8,128)(2,1)S(1)} %collective-permute-done.1.refs_4_) | copy-start | bytes 196612
  51.9 20.2 %collective-permute-start.14 = (bf16[4,2,128,128]{3,2,1,0:T(8,128)(2,1)}, bf16[4,2,128,128]{3,2,1,0:T(8,128)(2,1)S(1)}, u32[]{:S(2)}, u32[]{:S(2)}) collective-permute-start(bf16[4,2,128,128]{3,2,1,0:T(8,128)(2,1)} %get-tuple-element.14), channel_id=1, source_target_pairs={{0,2},{2,4},{4,6},{6,7},{7,5},{5,3},{3,1},{1,0},{8,10},{10,12},{12... | collective-permute-start | bytes 786440 | tf_op jit(solution)/shard_map/ppermute | solution.py:142
  51.9 20.1 %collective-permute-start.21 = (bf16[4,2,128,128]{3,2,1,0:T(8,128)(2,1)}, bf16[4,2,128,128]{3,2,1,0:T(8,128)(2,1)S(1)}, u32[]{:S(2)}, u32[]{:S(2)}) collective-permute-start(bf16[4,2,128,128]{3,2,1,0:T(8,128)(2,1)} %get-tuple-element.16), channel_id=1, source_target_pairs={{0,1},{2,0},{4,2},{6,4},{7,6},{5,7},{3,5},{1,3},{8,9},{10,8},{12,1... | collective-permute-start | bytes 786440 | tf_op jit(solution)/shard_map/ppermute | solution.py:142
  53.4 18.7 %collective-permute-start.13 = (bf16[2,2,128,128]{3,2,1,0:T(8,128)(2,1)S(1)}, bf16[2,2,128,128]{3,2,1,0:T(8,128)(2,1)S(1)}, u32[]{:S(2)}, u32[]{:S(2)}) collective-permute-start(bf16[2,2,128,128]{3,2,1,0:T(8,128)(2,1)S(1)} %collective-permute-done.12), channel_id=1, source_target_pairs={{0,2},{2,4},{4,6},{6,7},{7,5},{5,3},{3,1},{1,0},{8,10},{10,12},{12... | collective-permute-start | bytes 393224 | tf_op jit(solution)/shard_map/ppermute | solution.py:143
  53.5 18.6 %collective-permute-start.20 = (bf16[2,2,128,128]{3,2,1,0:T(8,128)(2,1)S(1)}, bf16[2,2,128,128]{3,2,1,0:T(8,128)(2,1)S(1)}, u32[]{:S(2)}, u32[]{:S(2)}) collective-permute-start(bf16[2,2,128,128]{3,2,1,0:T(8,128)(2,1)S(1)} %collective-permute-done.19), channel_id=1, source_target_pairs={{0,1},{2,0},{4,2},{6,4},{7,6},{5,7},{3,5},{1,3},{8,9},{10,8},{12,1... | collective-permute-start | bytes 393224 | tf_op jit(solution)/shard_map/ppermute | solution.py:143
  58.4 0.6 copy-start.14
  72.0 0.7 copy-start.9
  72.1 0.8 copy-start.10
  72.1 0.8 copy-start.11
  72.1 0.8 copy-start.12

commit v2 on v0

v2 whole, which is shorter than its diff:
```python
import jax
import jax.numpy as jnp
from jax import lax
from jax.experimental import pallas as pl
from jax.experimental.pallas import tpu as pltpu
from jax.sharding import PartitionSpec as P

HEAD_DIM = 128
HEADS = 8
BLOCK = 128
GLOBAL = 2
RANDOM = 3
LIST = 8
COST = (1 << 30, 1 << 30)
TO_LOG2 = HEAD_DIM**-0.5 * 1.4426950408889634

VMEM = pl.BlockSpec(memory_space=pltpu.VMEM)
SMEM = pl.BlockSpec(memory_space=pltpu.SMEM)


def random_start(row, n_blocks):
    low = jnp.maximum(row - 1, GLOBAL)
    high = jnp.minimum(row + 1, n_blocks - 1)
    return GLOBAL + high - low + 1


def group_rows(key_blocks):
    n_rows = key_blocks.shape[0] // lax.axis_size("pb")
    return lax.dynamic_slice_in_dim(
        key_blocks, lax.axis_index("pb") * n_rows, n_rows, 0
    ).reshape(-1)


def ring_of(n_ctx):
    return list(range(0, n_ctx, 2)) + list(range(n_ctx - 1, 0, -2))


def place_of(index, n_ctx):
    return jnp.where(index % 2 == 0, index // 2, n_ctx - 1 - index // 2)


def edges(keys, values):
    n_dev = keys.shape[0]

    def kernel(k_first, v_first, k_last, v_last, shared_ref, first_ref, last_ref):
        for which, (first, last) in enumerate(((k_first, k_last), (v_first, v_last))):
            for g in range(GLOBAL):
                shared_ref[g, which] = first[g]
            first_ref[0, which] = first[0]
            last_ref[0, which] = last[0]

    head = pl.BlockSpec((GLOBAL, BLOCK, HEAD_DIM), lambda i: (0, 0, 0))
    tail = pl.BlockSpec((1, BLOCK, HEAD_DIM), lambda i: (n_dev - 1, 0, 0))
    return pl.pallas_call(
        kernel,
        grid=(1,),
        out_shape=[
            jax.ShapeDtypeStruct((n, 2, BLOCK, HEAD_DIM), jnp.bfloat16) for n in (GLOBAL, 1, 1)
        ],
        in_specs=[head, head, tail, tail],
        out_specs=[pl.BlockSpec((n, 2, BLOCK, HEAD_DIM), lambda i: (0, 0, 0, 0)) for n in (GLOBAL, 1, 1)],
        compiler_params=pltpu.CompilerParams(vmem_limit_bytes=2 << 20),
        name="edges",
    )(keys, values, keys, values)


def pass_round(keys, values):
    n_ctx = lax.axis_size("ctx")
    ring = ring_of(n_ctx)
    ahead = [(ring[i], ring[(i + 1) % n_ctx]) for i in range(n_ctx)]
    back = [(b, a) for a, b in ahead]
    parts = {}
    k = [keys, keys]
    v = [values, values]
    for hop in range(1, n_ctx // 2):
        for side, pairs in enumerate((ahead, back)):
            k[side] = lax.ppermute(k[side], "ctx", pairs)
        for side, pairs in enumerate((ahead, back)):
            v[side] = lax.ppermute(v[side], "ctx", pairs)
        parts[hop], parts[n_ctx - hop] = (k[0], v[0]), (k[1], v[1])
    parts[n_ctx // 2] = (lax.ppermute(k[0], "ctx", ahead), lax.ppermute(v[1], "ctx", back))
    return [parts[away] for away in range(1, n_ctx)]


def gather_kernel(sizes, list_ref, k_ref, v_ref, *rest):
    n_pb, n_ctx, n_dev, slots = sizes
    outs, table = rest[:-1], rest[-1]
    n_blocks = n_pb * n_ctx * n_dev
    me = lax.axis_index("ctx")
    group = lax.axis_index("pb") * (n_ctx * n_dev)
    own = group + me * n_dev
    for i in range((n_ctx - 1) * slots + 1):
        table[i] = 0
    for shift in range(1, n_ctx):
        first = lax.rem(me + shift, n_ctx) * n_dev
        count = jnp.int32(0)
        for r in range(n_dev):
            row = first + r
            start = row * LIST + random_start(group + row, n_blocks)
            for j in range(RANDOM):
                local = list_ref[start + j] - own
                hit = jnp.logical_and(local >= 0, local < n_dev)
                place = jnp.where(hit, (shift - 1) * slots + count, (n_ctx - 1) * slots)
                table[place] = local
                count = count + hit.astype(jnp.int32)
    for shift in range(1, n_ctx):
        for s in range(slots):
            local = table[(shift - 1) * slots + s]
            outs[shift - 1][s, 0] = k_ref[local]
            outs[shift - 1][s, 1] = v_ref[local]


def gather(sizes, lists, key_states, value_states):
    n_pb, n_ctx, n_dev, slots = sizes
    return pl.pallas_call(
        lambda *refs: gather_kernel(sizes, *refs),
        out_shape=[jax.ShapeDtypeStruct((slots, 2, BLOCK, HEAD_DIM), jnp.bfloat16)] * (n_ctx - 1),
        in_specs=[SMEM, VMEM, VMEM],
        out_specs=[VMEM] * (n_ctx - 1),
        scratch_shapes=[pltpu.SMEM(((n_ctx - 1) * slots + 1,), jnp.int32)],
        name="gather",
    )(lists, key_states, value_states)


def attend(n_dev, q_ref, before, out_ref, lse_ref, load_keys, load_values, buffers):
    scores, weights, scales = buffers[:2], buffers[2:4], buffers[4:6]
    half = HEADS // 2

    def lanes(h):
        return slice(h * HEAD_DIM, (h + 1) * HEAD_DIM)

    def rows_of(i):
        return pl.ds(pl.multiple_of(i * BLOCK, BLOCK), BLOCK)

    def form_scores(i, side):
        q = jnp.concatenate([q_ref[rows_of(i), lanes(side * half + n)] for n in range(half)], axis=0)
        scores[side][...] = lax.dot_general(
            q, load_keys(i), (((1,), (1,)), ((), ())), preferred_element_type=jnp.float32
        )

    def form_weights(i, side):
        for n in range(half):
            part = slice(n * BLOCK, (n + 1) * BLOCK)
            score = scores[side][part, :]
            top = jnp.max(score, axis=1, keepdims=True) * TO_LOG2
            if before is not None:
                lse = before[1][rows_of(i), lanes(side * half + n)]
                top = jnp.maximum(lse, top)
                scales[side][part, :] = jnp.exp2(lse - top)
                top = top[:, :1]
            else:
                scales[side][part, :] = jnp.broadcast_to(top, (BLOCK, HEAD_DIM))
            weights[side][part, :] = jnp.exp2(score * TO_LOG2 - top).astype(jnp.bfloat16)

    def sum_up(i, side):
        total = jnp.dot(weights[side][...], load_values(i), preferred_element_type=jnp.float32)
        for n in range(half):
            part = slice(n * BLOCK, (n + 1) * BLOCK)
            at = lanes(side * half + n)
            out, norm, scale = total[part, :HEAD_DIM], total[part, HEAD_DIM:], scales[side][part, :]
            if before is not None:
                out, norm = before[0][rows_of(i), at] * scale + out, scale + norm
            out_ref[rows_of(i), at] = (out / norm).astype(out_ref.dtype)
            if lse_ref is not None:
                lse_ref[rows_of(i), at] = scale + jnp.log2(norm)

    def step(u, _):
        now, last = jnp.minimum(u, n_dev - 1), jnp.maximum(u - 1, 0)
        form_scores(now, 0)
        form_weights(last, 1)
        sum_up(last, 0)
        form_scores(now, 1)
        form_weights(now, 0)
        sum_up(last, 1)
        return 0

    lax.fori_loop(0, n_dev + 1, step, 0)


def near_kernel(sizes, q_ref, k_ref, v_ref, before_ref, after_ref, global_ref, out_ref, lse_ref, pool, *buffers):
    n_pb, n_ctx, n_dev, slots = sizes
    n_blocks = n_pb * n_ctx * n_dev
    first = (lax.axis_index("pb") * n_ctx + lax.axis_index("ctx")) * n_dev
    shared = n_dev + 2
    pool[0] = before_ref[0]
    pool[1 : n_dev + 1, 0] = k_ref[...]
    pool[1 : n_dev + 1, 1] = v_ref[...]
    pool[n_dev + 1] = after_ref[0]
    pool[shared : shared + GLOBAL] = global_ref[...]

    def listed(i, step):
        block = first + i + step
        return jnp.logical_and(block >= GLOBAL, block < n_blocks)

    def load_keys(i):
        near = [pool[jnp.where(listed(i, step), i + 1 + step, shared), 0] for step in (-1, 0, 1)]
        return jnp.concatenate([pool[shared + g, 0] for g in range(GLOBAL)] + near, axis=0)

    def load_values(i):
        one = jnp.ones((BLOCK, HEAD_DIM), jnp.bfloat16)
        parts = [jnp.concatenate([pool[shared + g, 1], one], axis=1) for g in range(GLOBAL)]
        for step in (-1, 0, 1):
            part = jnp.concatenate([pool[i + 1 + step, 1], one], axis=1)
            parts.append(jnp.where(listed(i, step), part, jnp.zeros_like(part)))
        return jnp.concatenate(parts, axis=0)

    attend(n_dev, q_ref, None, out_ref, lse_ref, load_keys, load_values, buffers)


def random_kernel(sizes, where, list_ref, q_ref, o_ref, l_ref, *rest):
    n_pb, n_ctx, n_dev, slots = sizes
    parts, (out_ref, pool, table, counts, sems, *buffers) = rest[: len(where)], rest[len(where) :]
    copies = []
    for n, (part, (at, which)) in enumerate(zip(parts, where)):
        rows = pl.ds(at, part.shape[0])
        target = pool.at[rows] if which is None else pool.at[rows, which]
        copies.append(pltpu.make_async_copy(part, target, sems.at[n]))
    for copy in copies:
        copy.start()
    n_blocks = n_pb * n_ctx * n_dev
    me = lax.axis_index("ctx")
    group = lax.axis_index("pb") * (n_ctx * n_dev)
    whole = where[0][1] is not None
    for h in range(n_ctx):
        counts[h] = 0
    for r in range(n_dev):
        row = me * n_dev + r
        start = row * LIST + random_start(group + row, n_blocks)
        for j in range(RANDOM):
            block = list_ref[start + j] - group
            holder = block // n_dev
            if whole:
                away = lax.rem(place_of(me, n_ctx) - place_of(holder, n_ctx) + n_ctx, n_ctx)
                table[r * RANDOM + j] = (away - 1) * n_dev + block - holder * n_dev
            else:
                rank = counts[holder]
                counts[holder] = rank + 1
                table[r * RANDOM + j] = (lax.rem(me - holder + n_ctx, n_ctx) - 1) * slots + rank
    for copy in copies:
        copy.wait()

    def load_keys(i):
        return jnp.concatenate([pool[table[i * RANDOM + j], 0] for j in range(RANDOM)], axis=0)

    def load_values(i):
        values = jnp.concatenate([pool[table[i * RANDOM + j], 1] for j in range(RANDOM)], axis=0)
        return jnp.concatenate([values, jnp.ones_like(values)], axis=1)

    attend(n_dev, q_ref, (o_ref, l_ref), out_ref, None, load_keys, load_values, buffers)


def call(kernel, name, out_shape, scalars, whole, parts, n_keys, cost, scratch):
    rows = HEADS // 2 * BLOCK
    return pl.pallas_call(
        kernel,
        out_shape=out_shape,
        in_specs=[SMEM] * len(scalars)
        + [VMEM] * len(whole)
        + [pl.BlockSpec(memory_space=pl.ANY)] * len(parts),
        out_specs=[VMEM] * len(out_shape),
        scratch_shapes=[
            *scratch,
            *[pltpu.VMEM((rows, n_keys * BLOCK), jnp.float32)] * 2,
            *[pltpu.VMEM((rows, n_keys * BLOCK), jnp.bfloat16)] * 2,
            *[pltpu.VMEM((rows, HEAD_DIM), jnp.float32)] * 2,
        ],
        compiler_params=pltpu.CompilerParams(vmem_limit_bytes=20 << 20),
        cost_estimate=pl.CostEstimate(flops=cost, transcendentals=0, bytes_accessed=0),
        name=name,
    )(*scalars, *whole, *parts)


def shift_round(sizes, lists, keys, values):
    n_ctx = sizes[1]
    return [
        lax.ppermute(part, "ctx", [(i, (i + shift) % n_ctx) for i in range(n_ctx)])
        for shift, part in enumerate(gather(sizes, lists, keys, values), 1)
    ]


def neighbours(first, last):
    axes = ("pb", "ctx")
    n = lax.axis_size(axes)
    up = [(i, i + 1) for i in range(n - 1)]
    down = [(i + 1, i) for i in range(n - 1)]
    return lax.ppermute(last, axes, up), lax.ppermute(first, axes, down)


def spread(shared):
    n_ctx, n_pb = lax.axis_size("ctx"), lax.axis_size("pb")
    column, group = lax.axis_index("ctx"), lax.axis_index("pb")

    def fan(shared, axes, index, targets):
        received = [lax.ppermute(shared, axes, [(0, target)]) for target in targets]
        for target, got in zip(targets, received):
            shared = jnp.where(index == target, got, shared)
        return shared

    shared = fan(shared, ("pb", "ctx"), column, range(2, n_ctx, 2))
    got = lax.ppermute(shared, ("pb", "ctx"), [(c, c + 1) for c in range(0, n_ctx, 2)])
    shared = jnp.where(column % 2 == 1, got, shared)
    return fan(shared, "pb", group, range(1, n_pb))


def per_device(queries, key_states, value_states, key_blocks):
    n_pb, n_ctx = lax.axis_size("pb"), lax.axis_size("ctx")
    n_dev = queries.shape[0] // BLOCK
    slots = (RANDOM * n_dev + n_ctx - 2) // (n_ctx - 1)
    sizes = (n_pb, n_ctx, n_dev, slots)
    keys = key_states.reshape(n_dev, BLOCK, HEAD_DIM)
    values = value_states.reshape(n_dev, BLOCK, HEAD_DIM)
    lists = group_rows(key_blocks)
    if n_ctx == 8:
        parts, where = [], []
        for n, pair in enumerate(pass_round(keys, values)):
            parts += pair
            where += [(n * n_dev, 0), (n * n_dev, 1)]
    else:
        parts = shift_round(sizes, lists, keys, values)
        where = [(n * slots, None) for n in range(n_ctx - 1)]
    shared, first, last = edges(keys, values)
    before, after = neighbours(first, last)
    shared = spread(shared)
    return attention(sizes, queries, keys, values, before, after, shared, lists, where, parts)


def attention(sizes, queries, keys, values, before, after, shared, lists, where, parts):
    n_dev = sizes[2]
    partial = jax.ShapeDtypeStruct(queries.shape, jnp.float32)
    out, lse = call(
        lambda *refs: near_kernel(sizes, *refs), "near", [partial] * 2, [],
        [queries, keys, values, before, after, shared], [], GLOBAL + 3, COST[0],
        [pltpu.VMEM((n_dev + 2 + GLOBAL, 2, BLOCK, HEAD_DIM), jnp.bfloat16)],
    )
    n_pool = max(at + part.shape[0] for part, (at, _) in zip(parts, where))
    (out,) = call(
        lambda *refs: random_kernel(sizes, where, *refs), "random",
        [jax.ShapeDtypeStruct(queries.shape, jnp.bfloat16)], [lists], [queries, out, lse], parts, RANDOM, COST[1],
        [
            pltpu.VMEM((n_pool, 2, BLOCK, HEAD_DIM), jnp.bfloat16),
            pltpu.SMEM((n_dev * RANDOM,), jnp.int32),
            pltpu.SMEM((sizes[1],), jnp.int32),
            pltpu.SemaphoreType.DMA((len(parts),)),
        ],
    )
    return out


def solution(mesh):
    in_specs = (P(("pb", "ctx"), None), P(("pb", "ctx"), None), P(("pb", "ctx"), None), P())
    out_specs = P(("pb", "ctx"), None)
    return jax.shard_map(
        per_device, mesh=mesh, in_specs=in_specs, out_specs=out_specs, check_vma=False
    )
```

time: 247 us -> 72.6 us (0.29)
  waiting for transfers between devices: 152 us -> 10.3 us
  local copies, waits for them, and re-layouts: 40.5 us -> 1.85 us
  starting transfers between devices: 6.18 us -> 38 us
  Pallas kernels: 0 us -> 21.8 us
  other arithmetic: 17.7 us -> 0.07 us
  matrix products: 14.8 us -> 0 us
  between operations: 15 us -> 0.25 us
    psum x1 -> x0, waiting for transfers between devices: 151 us -> none  [spread(): return lax.psum(jnp.where(mine, shard, jnp.zeros_like(shard)), axis)]
    ppermute x2 -> x23, starting transfers between devices: 6.14 us -> 38 us  [the longest x6 16.1 us: fan(): received = [lax.ppermute(shared, axes, [(0, target)]) for target in targets]]
    pallas_call x0 -> x3, Pallas kernels: none -> 21.8 us  [the longest x2 20.9 us: call(): pl.pallas_call(kernel, out_shape=out_shape, in_specs=[SMEM] * len(scalars...]
    dot_general x16 -> x0, matrix products: 14.8 us -> none  [the longest x8 8.04 us: attend(): jnp.einsum('thu,ud->thd', rounded, value_rows, preferred_element_type=jnp...]
    ppermute x2 -> x23, waiting for transfers between devices: 1.37 us -> 10.3 us  [the longest x6 6.21 us: fan(): received = [lax.ppermute(shared, axes, [(0, target)]) for target in targets]]
    reduce_sum x10 -> x0, other arithmetic: 8.76 us -> none  [the longest x8 8.41 us: attend(): normalizer = jnp.sum(weights, axis=-1, keepdims=True)]
    gather x9 -> x0, local copies, waits for them, and re-layouts: 8.31 us -> none  [the longest x8 5.18 us: per_block(): selected = jnp.take(kv_pool, row_index, axis=1)]
    dynamic_slice x9 -> x2, local copies, waits for them, and re-layouts: 7.82 us -> 0.16 us  [group_rows(): lax.dynamic_slice_in_dim(key_blocks, lax.axis_index('pb') * n_rows, n_row...]
  transfers between devices with their start and end apart: 4 -> 23, of which waited for: 3 -> 6; matrix products, arithmetic and copies ran while one was open for 4% -> 0% of each run, Pallas kernels for 0% -> 15%
where the time goes in v2:
time: 72.6 us; the launch traced here: 72.2 us
  starting transfers between devices  38 us (52%)
  Pallas kernels  21.8 us (30%)
  waiting for transfers between devices  10.3 us (14%)
  local copies, waits for them, and re-layouts  1.85 us (3%)
    pallas_call x2, Pallas kernels, call(): pl.pallas_call(kernel, out_shape=out_shape, in_specs=[SMEM] * len(scalars...  20.9 us
    ppermute x6, starting transfers between devices, fan(): received = [lax.ppermute(shared, axes, [(0, target)]) for target in targets]  16.1 us
    ppermute x6, starting transfers between devices, pass_round(): v[side] = lax.ppermute(v[side], 'ctx', pairs)  10 us
    ppermute x6, waiting for transfers between devices, fan(): received = [lax.ppermute(shared, axes, [(0, target)]) for target in targets]  6.21 us
    ppermute x2, starting transfers between devices, neighbours(): return (lax.ppermute(last, axes, up), lax.ppermute(first, axes, down))  5.66 us
    ppermute x6, waiting for transfers between devices, pass_round(): k[side] = lax.ppermute(k[side], 'ctx', pairs)  3.13 us
    ppermute x6, starting transfers between devices, pass_round(): k[side] = lax.ppermute(k[side], 'ctx', pairs)  2.9 us
    ppermute x1, starting transfers between devices, pass_round(): lax.ppermute(v[1], 'ctx', back)  2.02 us
  transfers between devices with their start and end apart: 23, of which 6 were waited for; matrix products, arithmetic and copies ran while one was open for 0% of the time, Pallas kernels for 15%

profile of v2, /device:TPU:0, one launch (start us, length us, event | category | flops | bytes accessed | tf_op | source)
XLA Modules:
  0.0 72.2 jit_solution(12359422185767460284)
XLA Ops:
  0.0 0.0 copy-start
  0.0 0.9 %edges.1 = (bf16[2,2,128,128]{3,2,1,0:T(8,128)(2,1)S(1)}, bf16[1,2,128,128]{3,2,1,0:T(8,128)(2,1)S(1)}, bf16[1,2,128,128]{3,2,1,0:T(8,128)(2,1)S(1)}) custom-call(bf16[8,128,128]{2,1,0:T(8,128)(2,1)} %bitcast.k_first.k_last.refs_1_, bf16[8,128,128]{2,1,0:T(8,128)(2,1)} %bitcast.1.v_first.v_last.refs_2_, bf16[8,128,128]{2,1,0:T(8,128)(2,1)} %bitcast.k_first.k_last.refs_1_, ...), custom_call_target="tpu_custom_call" | custom-call | tf_op jit(solution)/shard_map/edges/pallas_call | solution.py:54
  0.9 4.9 %collective-permute-start.4 = (bf16[2,2,128,128]{3,2,1,0:T(8,128)(2,1)S(1)}, bf16[2,2,128,128]{3,2,1,0:T(8,128)(2,1)S(1)}, u32[]{:S(2)}, u32[]{:S(2)}) collective-permute-start(bf16[2,2,128,128]{3,2,1,0:T(8,128)(2,1)S(1)} %get-tuple-element.12), channel_id=1, source_target_pairs={{0,2}} | collective-permute-start | bytes 393224 | tf_op jit(solution)/shard_map/ppermute | solution.py:294
  5.9 1.7 %collective-permute-start.3 = (bf16[2,2,128,128]{3,2,1,0:T(8,128)(2,1)S(1)}, bf16[2,2,128,128]{3,2,1,0:T(8,128)(2,1)S(1)}, u32[]{:S(2)}, u32[]{:S(2)}) collective-permute-start(bf16[2,2,128,128]{3,2,1,0:T(8,128)(2,1)S(1)} %get-tuple-element.12), channel_id=1, source_target_pairs={{0,4}} | collective-permute-start | bytes 393224 | tf_op jit(solution)/shard_map/ppermute | solution.py:294
  7.6 1.7 %collective-permute-start.2 = (bf16[2,2,128,128]{3,2,1,0:T(8,128)(2,1)S(1)}, bf16[2,2,128,128]{3,2,1,0:T(8,128)(2,1)S(1)}, u32[]{:S(2)}, u32[]{:S(2)}) collective-permute-start(bf16[2,2,128,128]{3,2,1,0:T(8,128)(2,1)S(1)} %get-tuple-element.12), channel_id=1, source_target_pairs={{0,6}} | collective-permute-start | bytes 393224 | tf_op jit(solution)/shard_map/ppermute | solution.py:294
  9.2 0.1 collective-permute-start.9
  9.3 2.0 %collective-permute-start.16 = (bf16[8,128,128]{2,1,0:T(8,128)(2,1)}, bf16[8,128,128]{2,1,0:T(8,128)(2,1)S(1)}, u32[]{:S(2)}, u32[]{:S(2)}) collective-permute-start(bf16[8,128,128]{2,1,0:T(8,128)(2,1)} %bitcast.1.v_first.v_last.refs_2_), channel_id=1, source_target_pairs={{2,0},{4,2},{6,4},{7,6},{5,7},{3,5},{1,3},{0,1},{10,8},{12,10},{14... | collective-permute-start | bytes 786440 | tf_op jit(solution)/shard_map/ppermute | solution.py:79
  11.3 0.0 collective-permute-done.4
  11.3 1.2 %collective-permute-done.3 = bf16[2,2,128,128]{3,2,1,0:T(8,128)(2,1)S(1)} collective-permute-done((bf16[2,2,128,128]{3,2,1,0:T(8,128)(2,1)S(1)}, bf16[2,2,128,128]{3,2,1,0:T(8,128)(2,1)S(1)}, u32[]{:S(2)}, u32[]{:S(2)}) %collective-permute-start.3) | collective-permute-done | bytes 131104 | tf_op jit(solution)/shard_map/ppermute | solution.py:294
  12.5 2.8 %collective-permute-done.2 = bf16[2,2,128,128]{3,2,1,0:T(8,128)(2,1)S(1)} collective-permute-done((bf16[2,2,128,128]{3,2,1,0:T(8,128)(2,1)S(1)}, bf16[2,2,128,128]{3,2,1,0:T(8,128)(2,1)S(1)}, u32[]{:S(2)}, u32[]{:S(2)}) %collective-permute-start.2) | collective-permute-done | bytes 131104 | tf_op jit(solution)/shard_map/ppermute | solution.py:294
  15.3 1.3 %collective-permute-start.5 = (bf16[2,2,128,128]{3,2,1,0:T(8,128)(2,1)S(1)}, bf16[2,2,128,128]{3,2,1,0:T(8,128)(2,1)S(1)}, u32[]{:S(2)}, u32[]{:S(2)}) collective-permute-start(bf16[2,2,128,128]{3,2,1,0:T(8,128)(2,1)S(1)} %select_select_fusion.1), channel_id=1, source_target_pairs={{0,1},{2,3},{4,5},{6,7}} | collective-permute-start | bytes 393224 | tf_op jit(solution)/shard_map/ppermute | solution.py:300
  16.6 0.1 collective-permute-start.20
  16.7 2.0 %collective-permute-start.10 = (bf16[8,128,128]{2,1,0:T(8,128)(2,1)}, bf16[8,128,128]{2,1,0:T(8,128)(2,1)S(1)}, u32[]{:S(2)}, u32[]{:S(2)}) collective-permute-start(bf16[8,128,128]{2,1,0:T(8,128)(2,1)} %bitcast.1.v_first.v_last.refs_2_), channel_id=1, source_target_pairs={{0,2},{2,4},{4,6},{6,7},{7,5},{5,3},{3,1},{1,0},{8,10},{10,12},{12... | collective-permute-start | bytes 786440 | tf_op jit(solution)/shard_map/ppermute | solution.py:79
  18.7 0.9 %collective-permute-done.5 = bf16[2,2,128,128]{3,2,1,0:T(8,128)(2,1)S(1)} collective-permute-done((bf16[2,2,128,128]{3,2,1,0:T(8,128)(2,1)S(1)}, bf16[2,2,128,128]{3,2,1,0:T(8,128)(2,1)S(1)}, u32[]{:S(2)}, u32[]{:S(2)}) %collective-permute-start.5) | collective-permute-done | bytes 131104 | tf_op jit(solution)/shard_map/ppermute | solution.py:300
  19.6 4.4 %collective-permute-start = (bf16[1,2,128,128]{3,2,1,0:T(8,128)(2,1)S(1)}, bf16[1,2,128,128]{3,2,1,0:T(8,128)(2,1)S(1)}, u32[]{:S(2)}, u32[]{:S(2)}) collective-permute-start(bf16[1,2,128,128]{3,2,1,0:T(8,128)(2,1)S(1)} %get-tuple-element.10), channel_id=1, source_target_pairs={{0,1},{1,2},{2,3},{3,4},{4,5},{5,6},{6,7},{7,8},{8,9},{9,10},{10,1... | collective-permute-start | bytes 196616 | tf_op jit(solution)/shard_map/ppermute | solution.py:286
  24.0 0.0 collective-permute-done.9.refs_4_
  24.0 0.1 collective-permute-start.11
  24.1 0.0 collective-permute-done.16.refs_17_
  24.1 2.0 %collective-permute-start.17 = (bf16[8,128,128]{2,1,0:T(8,128)(2,1)S(1)}, bf16[8,128,128]{2,1,0:T(8,128)(2,1)S(1)}, u32[]{:S(2)}, u32[]{:S(2)}) collective-permute-start(bf16[8,128,128]{2,1,0:T(8,128)(2,1)S(1)} %collective-permute-done.16.refs_17_), channel_id=1, source_target_pairs={{2,0},{4,2},{6,4},{7,6},{5,7},{3,5},{1,3},{0,1},{10,8},{12,10},{14... | collective-permute-start | bytes 786440 | tf_op jit(solution)/shard_map/ppermute | solution.py:79
  26.1 0.0 collective-permute-done.refs_3_
  26.1 5.2 %collective-permute-start.8 = (bf16[2,2,128,128]{3,2,1,0:T(8,128)(2,1)S(1)}, bf16[2,2,128,128]{3,2,1,0:T(8,128)(2,1)S(1)}, u32[]{:S(2)}, u32[]{:S(2)}) collective-permute-start(bf16[2,2,128,128]{3,2,1,0:T(8,128)(2,1)S(1)} %broadcast_select_fusion), channel_id=1, source_target_pairs={{0,8},{1,9},{2,10},{3,11},{4,12},{5,13},{6,14},{7,15}} | collective-permute-start | bytes 393224 | tf_op jit(solution)/shard_map/ppermute | solution.py:294
  31.4 0.0 collective-permute-done.20.refs_16_
  31.4 1.3 %collective-permute-start.7 = (bf16[2,2,128,128]{3,2,1,0:T(8,128)(2,1)S(1)}, bf16[2,2,128,128]{3,2,1,0:T(8,128)(2,1)S(1)}, u32[]{:S(2)}, u32[]{:S(2)}) collective-permute-start(bf16[2,2,128,128]{3,2,1,0:T(8,128)(2,1)S(1)} %broadcast_select_fusion), channel_id=1, source_target_pairs={{0,16},{1,17},{2,18},{3,19},{4,20},{5,21},{6,22},{7,23}} | collective-permute-start | bytes 393224 | tf_op jit(solution)/shard_map/ppermute | solution.py:294
  32.7 0.0 collective-permute-done.10.refs_5_
  32.7 0.1 collective-permute-start.21
  32.7 0.0 collective-permute-done.8
  32.8 2.0 %collective-permute-start.12 = (bf16[8,128,128]{2,1,0:T(8,128)(2,1)S(1)}, bf16[8,128,128]{2,1,0:T(8,128)(2,1)S(1)}, u32[]{:S(2)}, u32[]{:S(2)}) collective-permute-start(bf16[8,128,128]{2,1,0:T(8,128)(2,1)S(1)} %collective-permute-done.10.refs_5_), channel_id=1, source_target_pairs={{0,2},{2,4},{4,6},{6,7},{7,5},{5,3},{3,1},{1,0},{8,10},{10,12},{12... | collective-permute-start | bytes 786440 | tf_op jit(solution)/shard_map/ppermute | solution.py:79
  34.8 0.0 collective-permute-done.11.refs_6_
  34.8 0.1 collective-permute-start.13
  34.8 0.0 collective-permute-done.17.refs_15_
  34.8 2.0 %collective-permute-start.18 = (bf16[8,128,128]{2,1,0:T(8,128)(2,1)S(1)}, bf16[8,128,128]{2,1,0:T(8,128)(2,1)S(1)}, u32[]{:S(2)}, u32[]{:S(2)}) collective-permute-start(bf16[8,128,128]{2,1,0:T(8,128)(2,1)S(1)} %collective-permute-done.17.refs_15_), channel_id=1, source_target_pairs={{2,0},{4,2},{6,4},{7,6},{5,7},{3,5},{1,3},{0,1},{10,8},{12,10},{14... | collective-permute-start | bytes 786440 | tf_op jit(solution)/shard_map/ppermute | solution.py:79
  36.8 0.0 collective-permute-done.7
  36.8 1.3 %collective-permute-start.6 = (bf16[2,2,128,128]{3,2,1,0:T(8,128)(2,1)S(1)}, bf16[2,2,128,128]{3,2,1,0:T(8,128)(2,1)S(1)}, u32[]{:S(2)}, u32[]{:S(2)}) collective-permute-start(bf16[2,2,128,128]{3,2,1,0:T(8,128)(2,1)S(1)} %broadcast_select_fusion), channel_id=1, source_target_pairs={{0,24},{1,25},{2,26},{3,27},{4,28},{5,29},{6,30},{7,31}} | collective-permute-start | bytes 393224 | tf_op jit(solution)/shard_map/ppermute | solution.py:294
  38.1 0.0 copy-done
  38.1 0.1 constant_dynamic-slice_fusion
  38.2 0.1 copy.5
  38.3 0.1 reshape.9.refs_0_
  38.4 2.2 %collective-permute-done.6 = bf16[2,2,128,128]{3,2,1,0:T(8,128)(2,1)S(1)} collective-permute-done((bf16[2,2,128,128]{3,2,1,0:T(8,128)(2,1)S(1)}, bf16[2,2,128,128]{3,2,1,0:T(8,128)(2,1)S(1)}, u32[]{:S(2)}, u32[]{:S(2)}) %collective-permute-start.6) | collective-permute-done | bytes 131104 | tf_op jit(solution)/shard_map/ppermute | solution.py:294
  40.6 1.3 %collective-permute-start.1 = (bf16[1,2,128,128]{3,2,1,0:T(8,128)(2,1)S(1)}, bf16[1,2,128,128]{3,2,1,0:T(8,128)(2,1)S(1)}, u32[]{:S(2)}, u32[]{:S(2)}) collective-permute-start(bf16[1,2,128,128]{3,2,1,0:T(8,128)(2,1)S(1)} %get-tuple-element.11), channel_id=1, source_target_pairs={{1,0},{2,1},{3,2},{4,3},{5,4},{6,5},{7,6},{8,7},{9,8},{10,9},{11,1... | collective-permute-start | bytes 196616 | tf_op jit(solution)/shard_map/ppermute | solution.py:286
  41.9 0.1 collective-permute-done.21.refs_14_
  42.0 2.6 %collective-permute-start.22 = (bf16[8,128,128]{2,1,0:T(8,128)(2,1)S(1)}, bf16[8,128,128]{2,1,0:T(8,128)(2,1)S(1)}, u32[]{:S(2)}, u32[]{:S(2)}) collective-permute-start(bf16[8,128,128]{2,1,0:T(8,128)(2,1)S(1)} %collective-permute-done.21.refs_14_), channel_id=1, source_target_pairs={{2,0},{4,2},{6,4},{7,6},{5,7},{3,5},{1,3},{0,1},{10,8},{12,10},{14... | collective-permute-start | bytes 786440 | tf_op jit(solution)/shard_map/ppermute | solution.py:77
  44.6 0.0 collective-permute-done.12.refs_7_
  44.6 0.0 collective-permute-start.14
  44.6 3.0 %collective-permute-done.13.refs_8_ = bf16[8,128,128]{2,1,0:T(8,128)(2,1)S(1)} collective-permute-done((bf16[8,128,128]{2,1,0:T(8,128)(2,1)S(1)}, bf16[8,128,128]{2,1,0:T(8,128)(2,1)S(1)}, u32[]{:S(2)}, u32[]{:S(2)}) %collective-permute-start.13) | collective-permute-done | bytes 262176 | tf_op jit(solution)/shard_map/ppermute | solution.py:77
  47.6 0.0 collective-permute-start.15
  47.6 0.0 collective-permute-done.18.refs_13_
  47.6 2.0 %collective-permute-start.19 = (bf16[8,128,128]{2,1,0:T(8,128)(2,1)S(1)}, bf16[8,128,128]{2,1,0:T(8,128)(2,1)S(1)}, u32[]{:S(2)}, u32[]{:S(2)}) collective-permute-start(bf16[8,128,128]{2,1,0:T(8,128)(2,1)S(1)} %collective-permute-done.18.refs_13_), channel_id=1, source_target_pairs={{2,0},{4,2},{6,4},{7,6},{5,7},{3,5},{1,3},{0,1},{10,8},{12,10},{14... | collective-permute-start | bytes 786440 | tf_op jit(solution)/shard_map/ppermute | solution.py:81
  49.7 0.0 collective-permute-done.1.refs_4_
  49.7 0.0 copy-start.1
  49.7 1.6 %copy-done.1 = bf16[1024,1024]{1,0:T(8,128)(2,1)S(1)} copy-done((bf16[1024,1024]{1,0:T(8,128)(2,1)S(1)}, bf16[1024,1024]{1,0:T(8,128)(2,1)}, u32[]{:S(2)}) %copy-start.1) | copy-done | bytes 2097176
  51.3 11.0 %near.1 = (f32[1024,1024]{1,0:T(8,128)S(1)}, f32[1024,1024]{1,0:T(8,128)S(1)}) custom-call(bf16[1024,1024]{1,0:T(8,128)(2,1)S(1)} %copy-done.1, bf16[8,128,128]{2,1,0:T(8,128)(2,1)} %bitcast.k_first.k_last.refs_1_, bf16[8,128,128]{2,1,0:T(8,128)(2,1)} %bitcast.1.v_first.v_last.refs_2_, bf16[1,2,128,128]{3,2,1,0:T(8,128)(2,1)S(1)} %collective-permute-done.refs_3_, ...), custom_call_target="tpu_custom_call" | custom-call | flops 1073741824 | tf_op jit(solution)/shard_map/near/pallas_call | solution.py:254
  62.3 0.0 collective-permute-done.22.refs_12_
  62.3 0.0 collective-permute-done.14.refs_9_
  62.3 0.0 collective-permute-done.15.refs_10_
  62.3 0.0 collective-permute-done.19.refs_11_
  62.3 9.9 %random.1 = bf16[1024,1024]{1,0:T(8,128)(2,1)} custom-call(s32[512]{0:T(512)S(1)} %reshape.9.refs_0_, bf16[1024,1024]{1,0:T(8,128)(2,1)S(1)} %copy-done.1, f32[1024,1024]{1,0:T(8,128)S(1)} %get-tuple-element.13.refs_2_, f32[1024,1024]{1,0:T(8,128)S(1)} %get-tuple-element.14.refs_3_, bf16[8,128,128]{2,1,0:T(8,128)(2,1)S(1)} %collective-permute-done.9.refs_4_, ...), custom_call_target="tpu_custom_call" | custom-call | flops 1073741824 | tf_op jit(solution)/shard_map/random/pallas_call | solution.py:254
  (3 shorter events, 0.1 us)
Async XLA Ops:
  0.0 38.1 %copy-start = (s32[256,8]{0,1:T(8,128)S(1)}, s32[256,8]{0,1:T(8,128)}, u32[]{:S(2)}) copy-start(s32[256,8]{0,1:T(8,128)} %param.7) | copy-start | bytes 24580
  0.9 10.4 %collective-permute-start.4 = (bf16[2,2,128,128]{3,2,1,0:T(8,128)(2,1)S(1)}, bf16[2,2,128,128]{3,2,1,0:T(8,128)(2,1)S(1)}, u32[]{:S(2)}, u32[]{:S(2)}) collective-permute-start(bf16[2,2,128,128]{3,2,1,0:T(8,128)(2,1)S(1)} %get-tuple-element.12), channel_id=1, source_target_pairs={{0,2}} | collective-permute-start | bytes 393224 | tf_op jit(solution)/shard_map/ppermute | solution.py:294
  5.9 6.6 %collective-permute-start.3 = (bf16[2,2,128,128]{3,2,1,0:T(8,128)(2,1)S(1)}, bf16[2,2,128,128]{3,2,1,0:T(8,128)(2,1)S(1)}, u32[]{:S(2)}, u32[]{:S(2)}) collective-permute-start(bf16[2,2,128,128]{3,2,1,0:T(8,128)(2,1)S(1)} %get-tuple-element.12), channel_id=1, source_target_pairs={{0,4}} | collective-permute-start | bytes 393224 | tf_op jit(solution)/shard_map/ppermute | solution.py:294
  7.6 7.8 %collective-permute-start.2 = (bf16[2,2,128,128]{3,2,1,0:T(8,128)(2,1)S(1)}, bf16[2,2,128,128]{3,2,1,0:T(8,128)(2,1)S(1)}, u32[]{:S(2)}, u32[]{:S(2)}) collective-permute-start(bf16[2,2,128,128]{3,2,1,0:T(8,128)(2,1)S(1)} %get-tuple-element.12), channel_id=1, source_target_pairs={{0,6}} | collective-permute-start | bytes 393224 | tf_op jit(solution)/shard_map/ppermute | solution.py:294
  9.2 14.8 %collective-permute-start.9 = (bf16[8,128,128]{2,1,0:T(8,128)(2,1)}, bf16[8,128,128]{2,1,0:T(8,128)(2,1)S(1)}, u32[]{:S(2)}, u32[]{:S(2)}) collective-permute-start(bf16[8,128,128]{2,1,0:T(8,128)(2,1)} %bitcast.k_first.k_last.refs_1_), channel_id=1, source_target_pairs={{0,2},{2,4},{4,6},{6,7},{7,5},{5,3},{3,1},{1,0},{8,10},{10,12},{12... | collective-permute-start | bytes 786440 | tf_op jit(solution)/shard_map/ppermute | solution.py:77
  9.3 14.8 %collective-permute-start.16 = (bf16[8,128,128]{2,1,0:T(8,128)(2,1)}, bf16[8,128,128]{2,1,0:T(8,128)(2,1)S(1)}, u32[]{:S(2)}, u32[]{:S(2)}) collective-permute-start(bf16[8,128,128]{2,1,0:T(8,128)(2,1)} %bitcast.1.v_first.v_last.refs_2_), channel_id=1, source_target_pairs={{2,0},{4,2},{6,4},{7,6},{5,7},{3,5},{1,3},{0,1},{10,8},{12,10},{14... | collective-permute-start | bytes 786440 | tf_op jit(solution)/shard_map/ppermute | solution.py:79
  15.3 4.3 %collective-permute-start.5 = (bf16[2,2,128,128]{3,2,1,0:T(8,128)(2,1)S(1)}, bf16[2,2,128,128]{3,2,1,0:T(8,128)(2,1)S(1)}, u32[]{:S(2)}, u32[]{:S(2)}) collective-permute-start(bf16[2,2,128,128]{3,2,1,0:T(8,128)(2,1)S(1)} %select_select_fusion.1), channel_id=1, source_target_pairs={{0,1},{2,3},{4,5},{6,7}} | collective-permute-start | bytes 393224 | tf_op jit(solution)/shard_map/ppermute | solution.py:300
  16.6 14.7 %collective-permute-start.20 = (bf16[8,128,128]{2,1,0:T(8,128)(2,1)}, bf16[8,128,128]{2,1,0:T(8,128)(2,1)S(1)}, u32[]{:S(2)}, u32[]{:S(2)}) collective-permute-start(bf16[8,128,128]{2,1,0:T(8,128)(2,1)} %bitcast.k_first.k_last.refs_1_), channel_id=1, source_target_pairs={{2,0},{4,2},{6,4},{7,6},{5,7},{3,5},{1,3},{0,1},{10,8},{12,10},{14... | collective-permute-start | bytes 786440 | tf_op jit(solution)/shard_map/ppermute | solution.py:77
  16.7 16.0 %collective-permute-start.10 = (bf16[8,128,128]{2,1,0:T(8,128)(2,1)}, bf16[8,128,128]{2,1,0:T(8,128)(2,1)S(1)}, u32[]{:S(2)}, u32[]{:S(2)}) collective-permute-start(bf16[8,128,128]{2,1,0:T(8,128)(2,1)} %bitcast.1.v_first.v_last.refs_2_), channel_id=1, source_target_pairs={{0,2},{2,4},{4,6},{6,7},{7,5},{5,3},{3,1},{1,0},{8,10},{10,12},{12... | collective-permute-start | bytes 786440 | tf_op jit(solution)/shard_map/ppermute | solution.py:79
  19.6 6.5 %collective-permute-start = (bf16[1,2,128,128]{3,2,1,0:T(8,128)(2,1)S(1)}, bf16[1,2,128,128]{3,2,1,0:T(8,128)(2,1)S(1)}, u32[]{:S(2)}, u32[]{:S(2)}) collective-permute-start(bf16[1,2,128,128]{3,2,1,0:T(8,128)(2,1)S(1)} %get-tuple-element.10), channel_id=1, source_target_pairs={{0,1},{1,2},{2,3},{3,4},{4,5},{5,6},{6,7},{7,8},{8,9},{9,10},{10,1... | collective-permute-start | bytes 196616 | tf_op jit(solution)/shard_map/ppermute | solution.py:286
  24.0 10.7 %collective-permute-start.11 = (bf16[8,128,128]{2,1,0:T(8,128)(2,1)S(1)}, bf16[8,128,128]{2,1,0:T(8,128)(2,1)S(1)}, u32[]{:S(2)}, u32[]{:S(2)}) collective-permute-start(bf16[8,128,128]{2,1,0:T(8,128)(2,1)S(1)} %collective-permute-done.9.refs_4_), channel_id=1, source_target_pairs={{0,2},{2,4},{4,6},{6,7},{7,5},{5,3},{3,1},{1,0},{8,10},{10,12},{12... | collective-permute-start | bytes 786440 | tf_op jit(solution)/shard_map/ppermute | solution.py:77
  24.1 10.7 %collective-permute-start.17 = (bf16[8,128,128]{2,1,0:T(8,128)(2,1)S(1)}, bf16[8,128,128]{2,1,0:T(8,128)(2,1)S(1)}, u32[]{:S(2)}, u32[]{:S(2)}) collective-permute-start(bf16[8,128,128]{2,1,0:T(8,128)(2,1)S(1)} %collective-permute-done.16.refs_17_), channel_id=1, source_target_pairs={{2,0},{4,2},{6,4},{7,6},{5,7},{3,5},{1,3},{0,1},{10,8},{12,10},{14... | collective-permute-start | bytes 786440 | tf_op jit(solution)/shard_map/ppermute | solution.py:79
  26.1 6.6 %collective-permute-start.8 = (bf16[2,2,128,128]{3,2,1,0:T(8,128)(2,1)S(1)}, bf16[2,2,128,128]{3,2,1,0:T(8,128)(2,1)S(1)}, u32[]{:S(2)}, u32[]{:S(2)}) collective-permute-start(bf16[2,2,128,128]{3,2,1,0:T(8,128)(2,1)S(1)} %broadcast_select_fusion), channel_id=1, source_target_pairs={{0,8},{1,9},{2,10},{3,11},{4,12},{5,13},{6,14},{7,15}} | collective-permute-start | bytes 393224 | tf_op jit(solution)/shard_map/ppermute | solution.py:294
  31.4 5.4 %collective-permute-start.7 = (bf16[2,2,128,128]{3,2,1,0:T(8,128)(2,1)S(1)}, bf16[2,2,128,128]{3,2,1,0:T(8,128)(2,1)S(1)}, u32[]{:S(2)}, u32[]{:S(2)}) collective-permute-start(bf16[2,2,128,128]{3,2,1,0:T(8,128)(2,1)S(1)} %broadcast_select_fusion), channel_id=1, source_target_pairs={{0,16},{1,17},{2,18},{3,19},{4,20},{5,21},{6,22},{7,23}} | collective-permute-start | bytes 393224 | tf_op jit(solution)/shard_map/ppermute | solution.py:294
  32.7 9.3 %collective-permute-start.21 = (bf16[8,128,128]{2,1,0:T(8,128)(2,1)S(1)}, bf16[8,128,128]{2,1,0:T(8,128)(2,1)S(1)}, u32[]{:S(2)}, u32[]{:S(2)}) collective-permute-start(bf16[8,128,128]{2,1,0:T(8,128)(2,1)S(1)} %collective-permute-done.20.refs_16_), channel_id=1, source_target_pairs={{2,0},{4,2},{6,4},{7,6},{5,7},{3,5},{1,3},{0,1},{10,8},{12,10},{14... | collective-permute-start | bytes 786440 | tf_op jit(solution)/shard_map/ppermute | solution.py:77
  32.8 11.8 %collective-permute-start.12 = (bf16[8,128,128]{2,1,0:T(8,128)(2,1)S(1)}, bf16[8,128,128]{2,1,0:T(8,128)(2,1)S(1)}, u32[]{:S(2)}, u32[]{:S(2)}) collective-permute-start(bf16[8,128,128]{2,1,0:T(8,128)(2,1)S(1)} %collective-permute-done.10.refs_5_), channel_id=1, source_target_pairs={{0,2},{2,4},{4,6},{6,7},{7,5},{5,3},{3,1},{1,0},{8,10},{10,12},{12... | collective-permute-start | bytes 786440 | tf_op jit(solution)/shard_map/ppermute | solution.py:79
  34.8 12.8 %collective-permute-start.13 = (bf16[8,128,128]{2,1,0:T(8,128)(2,1)S(1)}, bf16[8,128,128]{2,1,0:T(8,128)(2,1)S(1)}, u32[]{:S(2)}, u32[]{:S(2)}) collective-permute-start(bf16[8,128,128]{2,1,0:T(8,128)(2,1)S(1)} %collective-permute-done.11.refs_6_), channel_id=1, source_target_pairs={{0,2},{2,4},{4,6},{6,7},{7,5},{5,3},{3,1},{1,0},{8,10},{10,12},{12... | collective-permute-start | bytes 786440 | tf_op jit(solution)/shard_map/ppermute | solution.py:77
  34.8 12.8 %collective-permute-start.18 = (bf16[8,128,128]{2,1,0:T(8,128)(2,1)S(1)}, bf16[8,128,128]{2,1,0:T(8,128)(2,1)S(1)}, u32[]{:S(2)}, u32[]{:S(2)}) collective-permute-start(bf16[8,128,128]{2,1,0:T(8,128)(2,1)S(1)} %collective-permute-done.17.refs_15_), channel_id=1, source_target_pairs={{2,0},{4,2},{6,4},{7,6},{5,7},{3,5},{1,3},{0,1},{10,8},{12,10},{14... | collective-permute-start | bytes 786440 | tf_op jit(solution)/shard_map/ppermute | solution.py:79
  36.8 3.8 %collective-permute-start.6 = (bf16[2,2,128,128]{3,2,1,0:T(8,128)(2,1)S(1)}, bf16[2,2,128,128]{3,2,1,0:T(8,128)(2,1)S(1)}, u32[]{:S(2)}, u32[]{:S(2)}) collective-permute-start(bf16[2,2,128,128]{3,2,1,0:T(8,128)(2,1)S(1)} %broadcast_select_fusion), channel_id=1, source_target_pairs={{0,24},{1,25},{2,26},{3,27},{4,28},{5,29},{6,30},{7,31}} | collective-permute-start | bytes 393224 | tf_op jit(solution)/shard_map/ppermute | solution.py:294
  40.6 9.1 %collective-permute-start.1 = (bf16[1,2,128,128]{3,2,1,0:T(8,128)(2,1)S(1)}, bf16[1,2,128,128]{3,2,1,0:T(8,128)(2,1)S(1)}, u32[]{:S(2)}, u32[]{:S(2)}) collective-permute-start(bf16[1,2,128,128]{3,2,1,0:T(8,128)(2,1)S(1)} %get-tuple-element.11), channel_id=1, source_target_pairs={{1,0},{2,1},{3,2},{4,3},{5,4},{6,5},{7,6},{8,7},{9,8},{10,9},{11,1... | collective-permute-start | bytes 196616 | tf_op jit(solution)/shard_map/ppermute | solution.py:286
  42.0 20.3 %collective-permute-start.22 = (bf16[8,128,128]{2,1,0:T(8,128)(2,1)S(1)}, bf16[8,128,128]{2,1,0:T(8,128)(2,1)S(1)}, u32[]{:S(2)}, u32[]{:S(2)}) collective-permute-start(bf16[8,128,128]{2,1,0:T(8,128)(2,1)S(1)} %collective-permute-done.21.refs_14_), channel_id=1, source_target_pairs={{2,0},{4,2},{6,4},{7,6},{5,7},{3,5},{1,3},{0,1},{10,8},{12,10},{14... | collective-permute-start | bytes 786440 | tf_op jit(solution)/shard_map/ppermute | solution.py:77
  44.6 17.7 %collective-permute-start.14 = (bf16[8,128,128]{2,1,0:T(8,128)(2,1)S(1)}, bf16[8,128,128]{2,1,0:T(8,128)(2,1)S(1)}, u32[]{:S(2)}, u32[]{:S(2)}) collective-permute-start(bf16[8,128,128]{2,1,0:T(8,128)(2,1)S(1)} %collective-permute-done.12.refs_7_), channel_id=1, source_target_pairs={{0,2},{2,4},{4,6},{6,7},{7,5},{5,3},{3,1},{1,0},{8,10},{10,12},{12... | collective-permute-start | bytes 786440 | tf_op jit(solution)/shard_map/ppermute | solution.py:79
  47.6 14.7 %collective-permute-start.15 = (bf16[8,128,128]{2,1,0:T(8,128)(2,1)S(1)}, bf16[8,128,128]{2,1,0:T(8,128)(2,1)S(1)}, u32[]{:S(2)}, u32[]{:S(2)}) collective-permute-start(bf16[8,128,128]{2,1,0:T(8,128)(2,1)S(1)} %collective-permute-done.13.refs_8_), channel_id=1, source_target_pairs={{0,2},{2,4},{4,6},{6,7},{7,5},{5,3},{3,1},{1,0},{8,10},{10,12},{12... | collective-permute-start | bytes 786440 | tf_op jit(solution)/shard_map/ppermute | solution.py:81
  47.6 14.7 %collective-permute-start.19 = (bf16[8,128,128]{2,1,0:T(8,128)(2,1)S(1)}, bf16[8,128,128]{2,1,0:T(8,128)(2,1)S(1)}, u32[]{:S(2)}, u32[]{:S(2)}) collective-permute-start(bf16[8,128,128]{2,1,0:T(8,128)(2,1)S(1)} %collective-permute-done.18.refs_13_), channel_id=1, source_target_pairs={{2,0},{4,2},{6,4},{7,6},{5,7},{3,5},{1,3},{0,1},{10,8},{12,10},{14... | collective-permute-start | bytes 786440 | tf_op jit(solution)/shard_map/ppermute | solution.py:81
  49.7 1.6 %copy-start.1 = (bf16[1024,1024]{1,0:T(8,128)(2,1)S(1)}, bf16[1024,1024]{1,0:T(8,128)(2,1)}, u32[]{:S(2)}) copy-start(bf16[1024,1024]{1,0:T(8,128)(2,1)} %refs_1_.1) | copy-start | bytes 6291460

commit v3 on v2

v3 whole, which is shorter than its diff:
```python
import jax
import jax.numpy as jnp
from jax import lax
from jax.experimental import pallas as pl
from jax.experimental.pallas import tpu as pltpu
from jax.sharding import PartitionSpec as P

HEAD_DIM = 128
HEADS = 8
BLOCK = 128
GLOBAL = 2
RANDOM = 3
LIST = 8
TO_LOG2 = HEAD_DIM**-0.5 * 1.4426950408889634

VMEM = pl.BlockSpec(memory_space=pltpu.VMEM)
MEM = pl.BlockSpec(memory_space=pltpu.HBM)
SMEM = pl.BlockSpec(memory_space=pltpu.SMEM)


def random_start(row, n_blocks):
    low = jnp.maximum(row - 1, GLOBAL)
    high = jnp.minimum(row + 1, n_blocks - 1)
    return GLOBAL + high - low + 1


def group_rows(key_blocks):
    n_rows = key_blocks.shape[0] // lax.axis_size("pb")
    return lax.dynamic_slice_in_dim(
        key_blocks, lax.axis_index("pb") * n_rows, n_rows, 0
    ).reshape(-1)


def ring_of(n_ctx):
    return list(range(0, n_ctx, 2)) + list(range(n_ctx - 1, 0, -2))


def place_of(index, n_ctx):
    return jnp.where(index % 2 == 0, index // 2, n_ctx - 1 - index // 2)


def edges(keys, values):
    n_dev = keys.shape[0]

    def kernel(k_ref, v_ref, first_ref, edge_ref, sems):
        last = lax.axis_index("ctx") == lax.axis_size("ctx") - 1
        edge = pl.ds(jnp.where(last, n_dev - 1, 0), 1)
        copies = []
        for which, ref in enumerate((k_ref, v_ref)):
            copies += [
                pltpu.make_async_copy(ref.at[pl.ds(0, GLOBAL)], first_ref.at[:, which], sems.at[2 * which]),
                pltpu.make_async_copy(ref.at[edge], edge_ref.at[:, which], sems.at[2 * which + 1]),
            ]
        for copy in copies:
            copy.start()
        for copy in copies:
            copy.wait()

    return pl.pallas_call(
        kernel,
        out_shape=[jax.ShapeDtypeStruct((n, 2, BLOCK, HEAD_DIM), jnp.bfloat16) for n in (GLOBAL, 1)],
        in_specs=[MEM, MEM],
        out_specs=[VMEM, VMEM],
        scratch_shapes=[pltpu.SemaphoreType.DMA((4,))],
        compiler_params=pltpu.CompilerParams(vmem_limit_bytes=2 << 20),
        name="edges",
    )(keys, values)


def first_of_group(first, direct, pairs):
    def kernel(*refs):
        *parts, out_ref, sems = refs
        place = place_of(lax.axis_index("ctx"), lax.axis_size("ctx"))
        for at, n in enumerate((0, 4)):

            @pl.when(place == n)
            def _():
                copy = pltpu.make_async_copy(parts[at], out_ref, sems.at[0])
                copy.start()
                copy.wait()

        for n, away in enumerate(whole):

            @pl.when(place == away)
            def _():
                copies = [
                    pltpu.make_async_copy(
                        parts[2 + 2 * n + which].at[pl.ds(0, GLOBAL)], out_ref.at[:, which], sems.at[which]
                    )
                    for which in range(2)
                ]
                for copy in copies:
                    copy.start()
                for copy in copies:
                    copy.wait()

    whole = [away for away in range(1, 8) if away != 4]
    parts = [first, direct] + [part for away in whole for part in pairs[away - 1]]
    return pl.pallas_call(
        kernel,
        out_shape=jax.ShapeDtypeStruct(first.shape, jnp.bfloat16),
        in_specs=[MEM] * len(parts),
        out_specs=VMEM,
        scratch_shapes=[pltpu.SemaphoreType.DMA((2,))],
        compiler_params=pltpu.CompilerParams(vmem_limit_bytes=2 << 20),
        name="first",
    )(*parts)


def pass_round(keys, values, small):
    n_ctx = lax.axis_size("ctx")
    ring = ring_of(n_ctx)
    ahead = [(ring[i], ring[(i + 1) % n_ctx]) for i in range(n_ctx)]
    back = [(b, a) for a, b in ahead]
    parts = {}
    k = [keys, keys]
    v = [values, values]
    for hop in range(1, n_ctx // 2):
        if hop == n_ctx // 2 - 1:
            k[0], small = lax.optimization_barrier((k[0], small))
        for side, pairs in enumerate((ahead, back)):
            k[side] = lax.ppermute(k[side], "ctx", pairs)
        for side, pairs in enumerate((ahead, back)):
            v[side] = lax.ppermute(v[side], "ctx", pairs)
        parts[hop], parts[n_ctx - hop] = (k[0], v[0]), (k[1], v[1])
    parts[n_ctx // 2] = (lax.ppermute(k[0], "ctx", ahead), lax.ppermute(v[1], "ctx", back))
    return [parts[away] for away in range(1, n_ctx)], small


def gather_kernel(sizes, list_ref, k_ref, v_ref, *rest):
    n_pb, n_ctx, n_dev, slots = sizes
    outs, table = rest[:-1], rest[-1]
    n_blocks = n_pb * n_ctx * n_dev
    me = lax.axis_index("ctx")
    group = lax.axis_index("pb") * (n_ctx * n_dev)
    own = group + me * n_dev
    for i in range((n_ctx - 1) * slots + 1):
        table[i] = 0
    for shift in range(1, n_ctx):
        first = lax.rem(me + shift, n_ctx) * n_dev
        count = jnp.int32(0)
        for r in range(n_dev):
            row = first + r
            start = row * LIST + random_start(group + row, n_blocks)
            for j in range(RANDOM):
                local = list_ref[start + j] - own
                hit = jnp.logical_and(local >= 0, local < n_dev)
                place = jnp.where(hit, (shift - 1) * slots + count, (n_ctx - 1) * slots)
                table[place] = local
                count = count + hit.astype(jnp.int32)
    for shift in range(1, n_ctx):
        for s in range(slots):
            local = table[(shift - 1) * slots + s]
            outs[shift - 1][s, 0] = k_ref[local]
            outs[shift - 1][s, 1] = v_ref[local]


def gather(sizes, lists, key_states, value_states):
    n_pb, n_ctx, n_dev, slots = sizes
    return pl.pallas_call(
        lambda *refs: gather_kernel(sizes, *refs),
        out_shape=[jax.ShapeDtypeStruct((slots, 2, BLOCK, HEAD_DIM), jnp.bfloat16)] * (n_ctx - 1),
        in_specs=[SMEM, VMEM, VMEM],
        out_specs=[VMEM] * (n_ctx - 1),
        scratch_shapes=[pltpu.SMEM(((n_ctx - 1) * slots + 1,), jnp.int32)],
        name="gather",
    )(lists, key_states, value_states)


def attend(n_dev, q_ref, out_ref, load_keys, load_values, buffers):
    scores, weights = buffers[:2], buffers[2:4]
    half = HEADS // 2

    def lanes(h):
        return slice(h * HEAD_DIM, (h + 1) * HEAD_DIM)

    def rows_of(i):
        return pl.ds(pl.multiple_of(i * BLOCK, BLOCK), BLOCK)

    def form_scores(i, side):
        q = jnp.concatenate([q_ref[rows_of(i), lanes(side * half + n)] for n in range(half)], axis=0)
        scores[side][...] = lax.dot_general(
            q, load_keys(i), (((1,), (1,)), ((), ())), preferred_element_type=jnp.float32
        )

    def form_weights(i, side):
        for n in range(half):
            part = slice(n * BLOCK, (n + 1) * BLOCK)
            score = scores[side][part, :]
            top = jnp.max(score, axis=1, keepdims=True)
            weights[side][part, :] = jnp.exp2((score - top) * TO_LOG2).astype(jnp.bfloat16)

    def sum_up(i, side):
        total = jnp.dot(weights[side][...], load_values(i), preferred_element_type=jnp.float32)
        for n in range(half):
            part = slice(n * BLOCK, (n + 1) * BLOCK)
            out = total[part, :HEAD_DIM] / total[part, HEAD_DIM:]
            out_ref[rows_of(i), lanes(side * half + n)] = out.astype(out_ref.dtype)

    form_scores(0, 0)
    form_scores(0, 1)
    form_weights(0, 0)

    def step(u, _):
        form_scores(u, 0)
        form_weights(u - 1, 1)
        sum_up(u - 1, 0)
        form_scores(u, 1)
        form_weights(u, 0)
        sum_up(u - 1, 1)
        return 0

    lax.fori_loop(1, n_dev, step, 0)
    form_weights(n_dev - 1, 1)
    sum_up(n_dev - 1, 0)
    sum_up(n_dev - 1, 1)


def attention_kernel(sizes, where, n_shared, list_ref, q_ref, k_ref, v_ref, before_ref, after_ref, *rest):
    n_pb, n_ctx, n_dev, slots = sizes
    shared_refs, rest = rest[:n_shared], rest[n_shared:]
    parts, (out_ref, pool, table, counts, sems, *buffers) = rest[: len(where)], rest[len(where) :]
    shared = n_dev + 2
    random = shared + GLOBAL
    copies = []
    for n, (part, (at, which)) in enumerate(zip(parts, where)):
        rows = pl.ds(random + at, part.shape[0])
        target = pool.at[rows] if which is None else pool.at[rows, which]
        copies.append(pltpu.make_async_copy(part, target, sems.at[n]))
    for copy in copies:
        copy.start()
    pool[0] = before_ref[0]
    pool[1 : n_dev + 1, 0] = k_ref[...]
    pool[1 : n_dev + 1, 1] = v_ref[...]
    pool[n_dev + 1] = after_ref[0]
    if n_shared == 1:
        pool[shared:random] = shared_refs[0][...]
    else:
        for p in range(n_shared):

            @pl.when(lax.axis_index("pb") == p)
            def _():
                pool[shared:random] = shared_refs[p][...]

    n_blocks = n_pb * n_ctx * n_dev
    me = lax.axis_index("ctx")
    group = lax.axis_index("pb") * (n_ctx * n_dev)
    first = group + me * n_dev

    def brought(block):
        holder = block // n_dev
        away = lax.rem(place_of(me, n_ctx) - place_of(holder, n_ctx) + n_ctx, n_ctx)
        return random + (away - 1) * n_dev + block - holder * n_dev

    ends = (jnp.int32(0), jnp.int32(n_dev + 1))
    if n_ctx == 8:
        own = me * n_dev
        ends = (
            jnp.where(me == 0, 0, brought(jnp.maximum(own - 1, 0))),
            jnp.where(me == n_ctx - 1, n_dev + 1, brought(jnp.minimum(own + n_dev, n_ctx * n_dev - 1))),
        )
    for h in range(n_ctx):
        counts[h] = 0
    for r in range(n_dev):
        row = me * n_dev + r
        start = row * LIST + random_start(group + row, n_blocks)
        for j in range(RANDOM):
            block = list_ref[start + j] - group
            if n_ctx == 8:
                table[r * RANDOM + j] = brought(block)
            else:
                holder = block // n_dev
                rank = counts[holder]
                counts[holder] = rank + 1
                table[r * RANDOM + j] = random + (lax.rem(me - holder + n_ctx, n_ctx) - 1) * slots + rank
    for copy in copies:
        copy.wait()

    def near(i, step):
        block = first + i + step
        place = jnp.where(i + step < 0, ends[0], jnp.where(i + step >= n_dev, ends[1], i + 1 + step))
        return place, jnp.logical_and(block >= GLOBAL, block < n_blocks)

    def load_keys(i):
        places = [shared + g for g in range(GLOBAL)]
        for step in (-1, 0, 1):
            place, use = near(i, step)
            places.append(jnp.where(use, place, shared))
        places += [table[i * RANDOM + j] for j in range(RANDOM)]
        return jnp.concatenate([pool[place, 0] for place in places], axis=0)

    def load_values(i):
        one = jnp.ones((BLOCK, HEAD_DIM), jnp.bfloat16)
        parts = [jnp.concatenate([pool[shared + g, 1], one], axis=1) for g in range(GLOBAL)]
        for step in (-1, 0, 1):
            place, use = near(i, step)
            part = jnp.concatenate([pool[jnp.where(use, place, shared), 1], one], axis=1)
            parts.append(jnp.where(use, part, jnp.zeros_like(part)))
        for j in range(RANDOM):
            parts.append(jnp.concatenate([pool[table[i * RANDOM + j], 1], one], axis=1))
        return jnp.concatenate(parts, axis=0)

    attend(n_dev, q_ref, out_ref, load_keys, load_values, buffers)


def attention(sizes, queries, keys, values, before, after, shared, lists, where, parts):
    n_dev = sizes[2]
    rows, n_keys = HEADS // 2 * BLOCK, (GLOBAL + 3 + RANDOM) * BLOCK
    n_pool = n_dev + 2 + GLOBAL + max(at + part.shape[0] for part, (at, _) in zip(parts, where))
    return pl.pallas_call(
        lambda *refs: attention_kernel(sizes, where, len(shared), *refs),
        out_shape=jax.ShapeDtypeStruct(queries.shape, jnp.bfloat16),
        in_specs=[SMEM] + [VMEM] * (5 + len(shared)) + [MEM] * len(parts),
        out_specs=VMEM,
        scratch_shapes=[
            pltpu.VMEM((n_pool, 2, BLOCK, HEAD_DIM), jnp.bfloat16),
            pltpu.SMEM((n_dev * RANDOM,), jnp.int32),
            pltpu.SMEM((sizes[1],), jnp.int32),
            pltpu.SemaphoreType.DMA((len(parts),)),
            *[pltpu.VMEM((rows, n_keys), jnp.float32)] * 2,
            *[pltpu.VMEM((rows, n_keys), jnp.bfloat16)] * 2,
        ],
        compiler_params=pltpu.CompilerParams(vmem_limit_bytes=24 << 20),
        name="attention",
    )(lists, queries, keys, values, before, after, *shared, *parts)


def shift_round(sizes, lists, keys, values):
    n_ctx = sizes[1]
    return [
        lax.ppermute(part, "ctx", [(i, (i + shift) % n_ctx) for i in range(n_ctx)])
        for shift, part in enumerate(gather(sizes, lists, keys, values), 1)
    ]


def neighbours(first, last):
    axes = ("pb", "ctx")
    n = lax.axis_size(axes)
    up = [(i, i + 1) for i in range(n - 1)]
    down = [(i + 1, i) for i in range(n - 1)]
    return lax.ppermute(last, axes, up), lax.ppermute(first, axes, down)


def spread(shared):
    n_ctx, n_pb = lax.axis_size("ctx"), lax.axis_size("pb")
    column, group = lax.axis_index("ctx"), lax.axis_index("pb")

    def fan(shared, axes, index, targets):
        received = [lax.ppermute(shared, axes, [(0, target)]) for target in targets]
        for target, got in zip(targets, received):
            shared = jnp.where(index == target, got, shared)
        return shared

    shared = fan(shared, ("pb", "ctx"), column, range(2, n_ctx, 2))
    got = lax.ppermute(shared, ("pb", "ctx"), [(c, c + 1) for c in range(0, n_ctx, 2)])
    shared = jnp.where(column % 2 == 1, got, shared)
    return fan(shared, "pb", group, range(1, n_pb))


def per_device(queries, key_states, value_states, key_blocks):
    n_pb, n_ctx = lax.axis_size("pb"), lax.axis_size("ctx")
    n_dev = queries.shape[0] // BLOCK
    slots = (RANDOM * n_dev + n_ctx - 2) // (n_ctx - 1)
    sizes = (n_pb, n_ctx, n_dev, slots)
    keys = key_states.reshape(n_dev, BLOCK, HEAD_DIM)
    values = value_states.reshape(n_dev, BLOCK, HEAD_DIM)
    lists = group_rows(key_blocks)
    first, edge = edges(keys, values)
    if n_ctx == 8:
        last = n_ctx - 1
        direct = lax.ppermute(first, ("pb", "ctx"), [(0, last)])
        across = [(p * n_ctx + last, (p + 1) * n_ctx) for p in range(n_pb - 1)]
        beside = lax.ppermute(edge, ("pb", "ctx"), across + [(b, a) for a, b in across])
        pairs, (direct, lists) = pass_round(keys, values, (direct, lists))
        before = after = beside
        parts = [part for pair in pairs for part in pair]
        where = [(n * n_dev, which) for n in range(n_ctx - 1) for which in range(2)]
        mine = first_of_group(first, direct, pairs)
        shared = [mine] + [lax.ppermute(mine, "pb", [(0, p)]) for p in range(1, n_pb)]
    else:
        parts = shift_round(sizes, lists, keys, values)
        where = [(n * slots, None) for n in range(n_ctx - 1)]
        last = jnp.stack([keys[-1:], values[-1:]], axis=1)
        before, after = neighbours(first[:1], last)
        shared = [spread(first)]
    return attention(sizes, queries, keys, values, before, after, shared, lists, where, parts)


def solution(mesh):
    in_specs = (P(("pb", "ctx"), None), P(("pb", "ctx"), None), P(("pb", "ctx"), None), P())
    out_specs = P(("pb", "ctx"), None)
    return jax.shard_map(
        per_device, mesh=mesh, in_specs=in_specs, out_specs=out_specs, check_vma=False
    )
```

time: 72.6 us -> 69.8 us (0.961)
  waiting for transfers between devices: 10.3 us -> 16.4 us
  starting transfers between devices: 38 us -> 32 us
  Pallas kernels: 21.8 us -> 16.8 us
  local copies, waits for them, and re-layouts: 1.85 us -> 4.16 us
    ppermute x6, waiting for transfers between devices: 3.13 us -> 13.5 us  [pass_round(): k[side] = lax.ppermute(k[side], 'ctx', pairs)]
    ppermute x9 -> x5, starting transfers between devices: 23 us -> 16.5 us  [the longest x3 9.9 us: per_device(): lax.ppermute(mine, 'pb', [(0, p)])]
    pallas_call x3, Pallas kernels: 21.8 us -> 16.8 us  [the longest x1 16.4 us: attention(): pl.pallas_call(lambda *refs: attention_kernel(sizes, where, len(shared),...]
    ppermute x6, starting transfers between devices: 2.9 us -> 7.17 us  [pass_round(): k[side] = lax.ppermute(k[side], 'ctx', pairs)]
    ppermute x9 -> x5, waiting for transfers between devices: 7.13 us -> 2.92 us  [the longest x1 1.97 us: per_device(): direct = lax.ppermute(first, ('pb', 'ctx'), [(0, last)])]
    ppermute x6, starting transfers between devices: 10 us -> 6.14 us  [pass_round(): v[side] = lax.ppermute(v[side], 'ctx', pairs)]
    unnamed x4 -> x14, local copies, waits for them, and re-layouts: 1.59 us -> 2.54 us
    reshape x1, local copies, waits for them, and re-layouts: 0.09 us -> 0.84 us  [group_rows(): return lax.dynamic_slice_in_dim(key_blocks, lax.axis_index('pb') * n_rows...]
  transfers between devices with their start and end apart: 23 -> 19, of which waited for: 6 -> 6; matrix products, arithmetic and copies ran while one was open for 0% -> 2% of each run, Pallas kernels for 15% -> 1%
where the time goes in v3:
time: 69.8 us; the launch traced here: 69.5 us
  starting transfers between devices  32 us (46%)
  Pallas kernels  16.8 us (24%)
  waiting for transfers between devices  16.4 us (23%)
  local copies, waits for them, and re-layouts  4.16 us (6%)
    pallas_call x1, Pallas kernels, attention(): pl.pallas_call(lambda *refs: attention_kernel(sizes, where, len(shared),...  16.4 us
    ppermute x6, waiting for transfers between devices, pass_round(): k[side] = lax.ppermute(k[side], 'ctx', pairs)  13.5 us
    ppermute x3, starting transfers between devices, per_device(): lax.ppermute(mine, 'pb', [(0, p)])  9.9 us
    ppermute x6, starting transfers between devices, pass_round(): k[side] = lax.ppermute(k[side], 'ctx', pairs)  7.17 us
    ppermute x6, starting transfers between devices, pass_round(): v[side] = lax.ppermute(v[side], 'ctx', pairs)  6.14 us
    ppermute x1, starting transfers between devices, per_device(): direct = lax.ppermute(first, ('pb', 'ctx'), [(0, last)])  5.96 us
    unnamed x14, local copies, waits for them, and re-layouts  2.54 us
    ppermute x1, waiting for transfers between devices, per_device(): direct = lax.ppermute(first, ('pb', 'ctx'), [(0, last)])  1.97 us
  transfers between devices with their start and end apart: 19, of which 6 were waited for; matrix products, arithmetic and copies ran while one was open for 2% of the time, Pallas kernels for 1%

profile of v3, /device:TPU:0, one launch (start us, length us, event | category | flops | bytes accessed | tf_op | source)
XLA Modules:
  0.0 69.5 jit_solution(5388217488307921304)
XLA Ops:
  0.0 0.0 copy-start
  0.0 0.0 copy-start.1
  0.0 3.0 %collective-permute-start = (bf16[8,128,128]{2,1,0:T(8,128)(2,1)}, bf16[8,128,128]{2,1,0:T(8,128)(2,1)S(1)}, u32[]{:S(2)}, u32[]{:S(2)}) collective-permute-start(bf16[8,128,128]{2,1,0:T(8,128)(2,1)} %bitcast.2), channel_id=1, source_target_pairs={{0,2},{2,4},{4,6},{6,7},{7,5},{5,3},{3,1},{1,0},{8,10},{10,12},{12... | collective-permute-start | bytes 786440 | tf_op jit(solution)/shard_map/ppermute | solution.py:122
  3.0 0.0 collective-permute-start.11
  3.0 1.9 %collective-permute-start.8 = (bf16[8,128,128]{2,1,0:T(8,128)(2,1)}, bf16[8,128,128]{2,1,0:T(8,128)(2,1)S(1)}, u32[]{:S(2)}, u32[]{:S(2)}) collective-permute-start(bf16[8,128,128]{2,1,0:T(8,128)(2,1)} %bitcast.3), channel_id=1, source_target_pairs={{2,0},{4,2},{6,4},{7,6},{5,7},{3,5},{1,3},{0,1},{10,8},{12,10},{14... | collective-permute-start | bytes 786440 | tf_op jit(solution)/shard_map/ppermute | solution.py:122
  5.0 0.1 collective-permute-start.4
  5.1 5.2 %collective-permute-done.refs_2_.refs_10_ = bf16[8,128,128]{2,1,0:T(8,128)(2,1)S(1)} collective-permute-done((bf16[8,128,128]{2,1,0:T(8,128)(2,1)}, bf16[8,128,128]{2,1,0:T(8,128)(2,1)S(1)}, u32[]{:S(2)}, u32[]{:S(2)}) %collective-permute-start) | collective-permute-done | bytes 262176 | tf_op jit(solution)/shard_map/ppermute | solution.py:122
  10.3 2.1 %collective-permute-start.1 = (bf16[8,128,128]{2,1,0:T(8,128)(2,1)S(1)}, bf16[8,128,128]{2,1,0:T(8,128)(2,1)S(1)}, u32[]{:S(2)}, u32[]{:S(2)}) collective-permute-start(bf16[8,128,128]{2,1,0:T(8,128)(2,1)S(1)} %collective-permute-done.refs_2_.refs_10_), channel_id=1, source_target_pairs={{0,2},{2,4},{4,6},{6,7},{7,5},{5,3},{3,1},{1,0},{8,10},{10,12},{12... | collective-permute-start | bytes 786440 | tf_op jit(solution)/shard_map/ppermute | solution.py:122
  12.4 0.0 collective-permute-done.11.refs_13_.refs_23_
  12.5 0.0 collective-permute-start.12
  12.5 0.0 copy-start.2
  12.5 0.9 %copy-done.2 = bf16[1024,128]{1,0:T(8,128)(2,1)S(1)} copy-done((bf16[1024,128]{1,0:T(8,128)(2,1)S(1)}, bf16[1024,128]{1,0:T(8,128)(2,1)}, u32[]{:S(2)}) %copy-start.2) | copy-done | bytes 262168
  13.4 0.0 copy-start.4
  13.4 0.9 %copy-done.4 = bf16[1024,128]{1,0:T(8,128)(2,1)S(1)} copy-done((bf16[1024,128]{1,0:T(8,128)(2,1)S(1)}, bf16[1024,128]{1,0:T(8,128)(2,1)}, u32[]{:S(2)}) %copy-start.4) | copy-done | bytes 262168
  14.4 0.2 edges.1
  14.6 0.0 copy-start.6
  14.6 0.6 copy-done.6
  15.2 2.9 %collective-permute-done.8.refs_12_.refs_22_ = bf16[8,128,128]{2,1,0:T(8,128)(2,1)S(1)} collective-permute-done((bf16[8,128,128]{2,1,0:T(8,128)(2,1)}, bf16[8,128,128]{2,1,0:T(8,128)(2,1)S(1)}, u32[]{:S(2)}, u32[]{:S(2)}) %collective-permute-start.8) | collective-permute-done | bytes 262176 | tf_op jit(solution)/shard_map/ppermute | solution.py:122
  18.1 0.0 collective-permute-start.9
  18.1 0.0 collective-permute-done.4.refs_3_.refs_11_
  18.1 2.0 %collective-permute-start.5 = (bf16[8,128,128]{2,1,0:T(8,128)(2,1)S(1)}, bf16[8,128,128]{2,1,0:T(8,128)(2,1)}, u32[]{:S(2)}, u32[]{:S(2)}) collective-permute-start(bf16[8,128,128]{2,1,0:T(8,128)(2,1)S(1)} %collective-permute-done.4.refs_3_.refs_11_), channel_id=1, source_target_pairs={{0,2},{2,4},{4,6},{6,7},{7,5},{5,3},{3,1},{1,0},{8,10},{10,12},{12... | collective-permute-start | bytes 786440 | tf_op jit(solution)/shard_map/ppermute | solution.py:124
  20.1 6.0 %collective-permute-start.2 = (bf16[2,2,128,128]{3,2,1,0:T(8,128)(2,1)S(1)}, bf16[2,2,128,128]{3,2,1,0:T(8,128)(2,1)}, u32[]{:S(2)}, u32[]{:S(2)}) collective-permute-start(bf16[2,2,128,128]{3,2,1,0:T(8,128)(2,1)S(1)} %get-tuple-element.10.refs_0_), channel_id=1, source_target_pairs={{0,7}} | collective-permute-start | bytes 393224 | tf_op jit(solution)/shard_map/ppermute | solution.py:371
  26.1 0.0 copy-done
  26.1 0.1 constant_dynamic-slice_fusion
  26.2 0.7 %copy.5 = s32[64,8]{1,0:T(8,128)} copy(s32[64,8]{0,1:T(8,128)S(1)} %constant_dynamic-slice_fusion) | data formatting | bytes 4096 | tf_op jit(solution)/shard_map/dynamic_slice | solution.py:29
  26.9 0.8 %reshape.11.refs_0_ = s32[512]{0:T(512)S(1)} reshape(s32[64,8]{1,0:T(8,128)} %copy.5) | data formatting | bytes 4096 | tf_op jit(solution)/shard_map/reshape | solution.py:31
  27.7 0.0 copy-start.3
  27.7 0.0 copy-start.5
  27.7 2.0 %collective-permute-done.2.refs_1_ = bf16[2,2,128,128]{3,2,1,0:T(8,128)(2,1)} collective-permute-done((bf16[2,2,128,128]{3,2,1,0:T(8,128)(2,1)S(1)}, bf16[2,2,128,128]{3,2,1,0:T(8,128)(2,1)}, u32[]{:S(2)}, u32[]{:S(2)}) %collective-permute-start.2) | collective-permute-done | bytes 131104 | tf_op jit(solution)/shard_map/ppermute | solution.py:371
  29.7 0.0 collective-permute-done.1.refs_4_.refs_12_
  29.7 0.0 collective-permute-start.6
  29.7 0.0 collective-permute-done.12.refs_11_.refs_21_
  29.7 2.0 %collective-permute-start.13 = (bf16[8,128,128]{2,1,0:T(8,128)(2,1)}, bf16[8,128,128]{2,1,0:T(8,128)(2,1)S(1)}, u32[]{:S(2)}, u32[]{:S(2)}) collective-permute-start(bf16[8,128,128]{2,1,0:T(8,128)(2,1)} %collective-permute-done.12.refs_11_.refs_21_), channel_id=1, source_target_pairs={{2,0},{4,2},{6,4},{7,6},{5,7},{3,5},{1,3},{0,1},{10,8},{12,10},{14... | collective-permute-start | bytes 786440 | tf_op jit(solution)/shard_map/ppermute | solution.py:124
  31.7 0.0 collective-permute-done.9.refs_10_.refs_20_
  31.7 0.1 collective-permute-start.10
  31.8 0.0 collective-permute-done.5.refs_5_.refs_13_
  31.8 2.0 %collective-permute-start.7 = (bf16[8,128,128]{2,1,0:T(8,128)(2,1)}, bf16[8,128,128]{2,1,0:T(8,128)(2,1)S(1)}, u32[]{:S(2)}, u32[]{:S(2)}) collective-permute-start(bf16[8,128,128]{2,1,0:T(8,128)(2,1)} %collective-permute-done.5.refs_5_.refs_13_), channel_id=1, source_target_pairs={{0,2},{2,4},{4,6},{6,7},{7,5},{5,3},{3,1},{1,0},{8,10},{10,12},{12... | collective-permute-start | bytes 786440 | tf_op jit(solution)/shard_map/ppermute | solution.py:124
  33.8 5.0 %collective-permute-done.6.refs_6_.refs_14_ = bf16[8,128,128]{2,1,0:T(8,128)(2,1)S(1)} collective-permute-done((bf16[8,128,128]{2,1,0:T(8,128)(2,1)S(1)}, bf16[8,128,128]{2,1,0:T(8,128)(2,1)S(1)}, u32[]{:S(2)}, u32[]{:S(2)}) %collective-permute-start.6) | collective-permute-done | bytes 262176 | tf_op jit(solution)/shard_map/ppermute | solution.py:122
  38.7 0.2 collective-permute-start.17
  38.9 0.0 collective-permute-done.13.refs_9_.refs_19_
  38.9 1.9 %collective-permute-start.18 = (bf16[8,128,128]{2,1,0:T(8,128)(2,1)S(1)}, bf16[8,128,128]{2,1,0:T(8,128)(2,1)S(1)}, u32[]{:S(2)}, u32[]{:S(2)}) collective-permute-start(bf16[8,128,128]{2,1,0:T(8,128)(2,1)S(1)} %collective-permute-done.13.refs_9_.refs_19_), channel_id=1, source_target_pairs={{2,0},{4,2},{6,4},{7,6},{5,7},{3,5},{1,3},{0,1},{10,8},{12,10},{14... | collective-permute-start | bytes 786440 | tf_op jit(solution)/shard_map/ppermute | solution.py:126
  40.9 0.7 collective-permute-start.3
  41.5 0.4 collective-permute-done.10.refs_8_.refs_18_
  42.0 0.0 collective-permute-done.7.refs_7_.refs_15_
  42.0 0.2 first.1.refs_6_
  42.2 3.1 %collective-permute-start.16 = (bf16[2,2,128,128]{3,2,1,0:T(8,128)(2,1)S(1)}, bf16[2,2,128,128]{3,2,1,0:T(8,128)(2,1)S(1)}, u32[]{:S(2)}, u32[]{:S(2)}) collective-permute-start(bf16[2,2,128,128]{3,2,1,0:T(8,128)(2,1)S(1)} %first.1.refs_6_), channel_id=1, source_target_pairs={{0,24},{1,25},{2,26},{3,27},{4,28},{5,29},{6,30},{7,31}} | collective-permute-start | bytes 393224 | tf_op jit(solution)/shard_map/ppermute | solution.py:379
  45.3 1.3 %collective-permute-start.15 = (bf16[2,2,128,128]{3,2,1,0:T(8,128)(2,1)S(1)}, bf16[2,2,128,128]{3,2,1,0:T(8,128)(2,1)S(1)}, u32[]{:S(2)}, u32[]{:S(2)}) collective-permute-start(bf16[2,2,128,128]{3,2,1,0:T(8,128)(2,1)S(1)} %first.1.refs_6_), channel_id=1, source_target_pairs={{0,16},{1,17},{2,18},{3,19},{4,20},{5,21},{6,22},{7,23}} | collective-permute-start | bytes 393224 | tf_op jit(solution)/shard_map/ppermute | solution.py:379
  46.6 0.0 collective-permute-done.3.refs_4_.refs_5_
  46.6 5.5 %collective-permute-start.14 = (bf16[2,2,128,128]{3,2,1,0:T(8,128)(2,1)S(1)}, bf16[2,2,128,128]{3,2,1,0:T(8,128)(2,1)S(1)}, u32[]{:S(2)}, u32[]{:S(2)}) collective-permute-start(bf16[2,2,128,128]{3,2,1,0:T(8,128)(2,1)S(1)} %first.1.refs_6_), channel_id=1, source_target_pairs={{0,8},{1,9},{2,10},{3,11},{4,12},{5,13},{6,14},{7,15}} | collective-permute-start | bytes 393224 | tf_op jit(solution)/shard_map/ppermute | solution.py:379
  52.1 0.0 collective-permute-done.16.refs_9_
  52.1 0.0 collective-permute-done.15.refs_8_
  52.1 0.9 %collective-permute-done.14.refs_7_ = bf16[2,2,128,128]{3,2,1,0:T(8,128)(2,1)S(1)} collective-permute-done((bf16[2,2,128,128]{3,2,1,0:T(8,128)(2,1)S(1)}, bf16[2,2,128,128]{3,2,1,0:T(8,128)(2,1)S(1)}, u32[]{:S(2)}, u32[]{:S(2)}) %collective-permute-start.14) | collective-permute-done | bytes 131104 | tf_op jit(solution)/shard_map/ppermute | solution.py:379
  53.1 0.0 collective-permute-done.17.refs_16_
  53.1 0.0 collective-permute-done.18.refs_17_
  53.1 0.0 copy-done.1
  53.1 0.0 copy-done.3
  53.1 0.0 copy-done.5
  53.1 16.4 %attention.1 = bf16[1024,1024]{1,0:T(8,128)(2,1)} custom-call(s32[512]{0:T(512)S(1)} %reshape.11.refs_0_, bf16[1024,1024]{1,0:T(8,128)(2,1)S(1)} %copy-done.1, bf16[8,128,128]{2,1,0:T(8,128)(2,1)S(1)} %bitcast.5, bf16[8,128,128]{2,1,0:T(8,128)(2,1)S(1)} %bitcast.9, bf16[1,2,128,128]{3,2,1,0:T(8,128)(2,1)S(1)} %collective-permute-done.3.refs_4_.refs_5_, ...), custom_call_target="tpu_custom_call" | custom-call | tf_op jit(solution)/shard_map/attention/pallas_call | solution.py:310
Async XLA Ops:
  0.0 26.1 %copy-start = (s32[256,8]{0,1:T(8,128)S(1)}, s32[256,8]{0,1:T(8,128)}, u32[]{:S(2)}) copy-start(s32[256,8]{0,1:T(8,128)} %param.7) | copy-start | bytes 24580
  0.0 53.1 %copy-start.1 = (bf16[1024,1024]{1,0:T(8,128)(2,1)S(1)}, bf16[1024,1024]{1,0:T(8,128)(2,1)}, u32[]{:S(2)}) copy-start(bf16[1024,1024]{1,0:T(8,128)(2,1)} %refs_1_.1) | copy-start | bytes 6291460
  0.0 10.3 %collective-permute-start = (bf16[8,128,128]{2,1,0:T(8,128)(2,1)}, bf16[8,128,128]{2,1,0:T(8,128)(2,1)S(1)}, u32[]{:S(2)}, u32[]{:S(2)}) collective-permute-start(bf16[8,128,128]{2,1,0:T(8,128)(2,1)} %bitcast.2), channel_id=1, source_target_pairs={{0,2},{2,4},{4,6},{6,7},{7,5},{5,3},{3,1},{1,0},{8,10},{10,12},{12... | collective-permute-start | bytes 786440 | tf_op jit(solution)/shard_map/ppermute | solution.py:122
  3.0 9.4 %collective-permute-start.11 = (bf16[8,128,128]{2,1,0:T(8,128)(2,1)}, bf16[8,128,128]{2,1,0:T(8,128)(2,1)S(1)}, u32[]{:S(2)}, u32[]{:S(2)}) collective-permute-start(bf16[8,128,128]{2,1,0:T(8,128)(2,1)} %bitcast.6), channel_id=1, source_target_pairs={{2,0},{4,2},{6,4},{7,6},{5,7},{3,5},{1,3},{0,1},{10,8},{12,10},{14... | collective-permute-start | bytes 786440 | tf_op jit(solution)/shard_map/ppermute | solution.py:124
  3.0 15.1 %collective-permute-start.8 = (bf16[8,128,128]{2,1,0:T(8,128)(2,1)}, bf16[8,128,128]{2,1,0:T(8,128)(2,1)S(1)}, u32[]{:S(2)}, u32[]{:S(2)}) collective-permute-start(bf16[8,128,128]{2,1,0:T(8,128)(2,1)} %bitcast.3), channel_id=1, source_target_pairs={{2,0},{4,2},{6,4},{7,6},{5,7},{3,5},{1,3},{0,1},{10,8},{12,10},{14... | collective-permute-start | bytes 786440 | tf_op jit(solution)/shard_map/ppermute | solution.py:122
  5.0 13.1 %collective-permute-start.4 = (bf16[8,128,128]{2,1,0:T(8,128)(2,1)}, bf16[8,128,128]{2,1,0:T(8,128)(2,1)S(1)}, u32[]{:S(2)}, u32[]{:S(2)}) collective-permute-start(bf16[8,128,128]{2,1,0:T(8,128)(2,1)} %bitcast.7), channel_id=1, source_target_pairs={{0,2},{2,4},{4,6},{6,7},{7,5},{5,3},{3,1},{1,0},{8,10},{10,12},{12... | collective-permute-start | bytes 786440 | tf_op jit(solution)/shard_map/ppermute | solution.py:124
  10.3 19.4 %collective-permute-start.1 = (bf16[8,128,128]{2,1,0:T(8,128)(2,1)S(1)}, bf16[8,128,128]{2,1,0:T(8,128)(2,1)S(1)}, u32[]{:S(2)}, u32[]{:S(2)}) collective-permute-start(bf16[8,128,128]{2,1,0:T(8,128)(2,1)S(1)} %collective-permute-done.refs_2_.refs_10_), channel_id=1, source_target_pairs={{0,2},{2,4},{4,6},{6,7},{7,5},{5,3},{3,1},{1,0},{8,10},{10,12},{12... | collective-permute-start | bytes 786440 | tf_op jit(solution)/shard_map/ppermute | solution.py:122
  12.5 17.2 %collective-permute-start.12 = (bf16[8,128,128]{2,1,0:T(8,128)(2,1)S(1)}, bf16[8,128,128]{2,1,0:T(8,128)(2,1)}, u32[]{:S(2)}, u32[]{:S(2)}) collective-permute-start(bf16[8,128,128]{2,1,0:T(8,128)(2,1)S(1)} %collective-permute-done.11.refs_13_.refs_23_), channel_id=1, source_target_pairs={{2,0},{4,2},{6,4},{7,6},{5,7},{3,5},{1,3},{0,1},{10,8},{12,10},{14... | collective-permute-start | bytes 786440 | tf_op jit(solution)/shard_map/ppermute | solution.py:124
  12.5 1.0 %copy-start.2 = (bf16[1024,128]{1,0:T(8,128)(2,1)S(1)}, bf16[1024,128]{1,0:T(8,128)(2,1)}, u32[]{:S(2)}) copy-start(bf16[1024,128]{1,0:T(8,128)(2,1)} %param.5) | copy-start | bytes 786436
  13.4 0.9 %copy-start.4 = (bf16[1024,128]{1,0:T(8,128)(2,1)S(1)}, bf16[1024,128]{1,0:T(8,128)(2,1)}, u32[]{:S(2)}) copy-start(bf16[1024,128]{1,0:T(8,128)(2,1)} %param.6) | copy-start | bytes 786436
  14.6 0.6 copy-start.6
  18.1 13.6 %collective-permute-start.9 = (bf16[8,128,128]{2,1,0:T(8,128)(2,1)S(1)}, bf16[8,128,128]{2,1,0:T(8,128)(2,1)}, u32[]{:S(2)}, u32[]{:S(2)}) collective-permute-start(bf16[8,128,128]{2,1,0:T(8,128)(2,1)S(1)} %collective-permute-done.8.refs_12_.refs_22_), channel_id=1, source_target_pairs={{2,0},{4,2},{6,4},{7,6},{5,7},{3,5},{1,3},{0,1},{10,8},{12,10},{14... | collective-permute-start | bytes 786440 | tf_op jit(solution)/shard_map/ppermute | solution.py:122
  18.1 13.7 %collective-permute-start.5 = (bf16[8,128,128]{2,1,0:T(8,128)(2,1)S(1)}, bf16[8,128,128]{2,1,0:T(8,128)(2,1)}, u32[]{:S(2)}, u32[]{:S(2)}) collective-permute-start(bf16[8,128,128]{2,1,0:T(8,128)(2,1)S(1)} %collective-permute-done.4.refs_3_.refs_11_), channel_id=1, source_target_pairs={{0,2},{2,4},{4,6},{6,7},{7,5},{5,3},{3,1},{1,0},{8,10},{10,12},{12... | collective-permute-start | bytes 786440 | tf_op jit(solution)/shard_map/ppermute | solution.py:124
  20.1 9.6 %collective-permute-start.2 = (bf16[2,2,128,128]{3,2,1,0:T(8,128)(2,1)S(1)}, bf16[2,2,128,128]{3,2,1,0:T(8,128)(2,1)}, u32[]{:S(2)}, u32[]{:S(2)}) collective-permute-start(bf16[2,2,128,128]{3,2,1,0:T(8,128)(2,1)S(1)} %get-tuple-element.10.refs_0_), channel_id=1, source_target_pairs={{0,7}} | collective-permute-start | bytes 393224 | tf_op jit(solution)/shard_map/ppermute | solution.py:371
  27.7 25.4 %copy-start.3 = (bf16[1024,128]{1,0:T(8,128)(2,1)S(1)}, bf16[1024,128]{1,0:T(8,128)(2,1)}, u32[]{:S(2)}) copy-start(bf16[1024,128]{1,0:T(8,128)(2,1)} %param.5) | copy-start | bytes 786436
  27.7 25.4 %copy-start.5 = (bf16[1024,128]{1,0:T(8,128)(2,1)S(1)}, bf16[1024,128]{1,0:T(8,128)(2,1)}, u32[]{:S(2)}) copy-start(bf16[1024,128]{1,0:T(8,128)(2,1)} %param.6) | copy-start | bytes 786436
  29.7 9.0 %collective-permute-start.6 = (bf16[8,128,128]{2,1,0:T(8,128)(2,1)S(1)}, bf16[8,128,128]{2,1,0:T(8,128)(2,1)S(1)}, u32[]{:S(2)}, u32[]{:S(2)}) collective-permute-start(bf16[8,128,128]{2,1,0:T(8,128)(2,1)S(1)} %collective-permute-done.1.refs_4_.refs_12_), channel_id=1, source_target_pairs={{0,2},{2,4},{4,6},{6,7},{7,5},{5,3},{3,1},{1,0},{8,10},{10,12},{12... | collective-permute-start | bytes 786440 | tf_op jit(solution)/shard_map/ppermute | solution.py:122
  29.7 9.2 %collective-permute-start.13 = (bf16[8,128,128]{2,1,0:T(8,128)(2,1)}, bf16[8,128,128]{2,1,0:T(8,128)(2,1)S(1)}, u32[]{:S(2)}, u32[]{:S(2)}) collective-permute-start(bf16[8,128,128]{2,1,0:T(8,128)(2,1)} %collective-permute-done.12.refs_11_.refs_21_), channel_id=1, source_target_pairs={{2,0},{4,2},{6,4},{7,6},{5,7},{3,5},{1,3},{0,1},{10,8},{12,10},{14... | collective-permute-start | bytes 786440 | tf_op jit(solution)/shard_map/ppermute | solution.py:124
  31.7 10.2 %collective-permute-start.10 = (bf16[8,128,128]{2,1,0:T(8,128)(2,1)}, bf16[8,128,128]{2,1,0:T(8,128)(2,1)S(1)}, u32[]{:S(2)}, u32[]{:S(2)}) collective-permute-start(bf16[8,128,128]{2,1,0:T(8,128)(2,1)} %collective-permute-done.9.refs_10_.refs_20_), channel_id=1, source_target_pairs={{2,0},{4,2},{6,4},{7,6},{5,7},{3,5},{1,3},{0,1},{10,8},{12,10},{14... | collective-permute-start | bytes 786440 | tf_op jit(solution)/shard_map/ppermute | solution.py:122
  31.8 10.2 %collective-permute-start.7 = (bf16[8,128,128]{2,1,0:T(8,128)(2,1)}, bf16[8,128,128]{2,1,0:T(8,128)(2,1)S(1)}, u32[]{:S(2)}, u32[]{:S(2)}) collective-permute-start(bf16[8,128,128]{2,1,0:T(8,128)(2,1)} %collective-permute-done.5.refs_5_.refs_13_), channel_id=1, source_target_pairs={{0,2},{2,4},{4,6},{6,7},{7,5},{5,3},{3,1},{1,0},{8,10},{10,12},{12... | collective-permute-start | bytes 786440 | tf_op jit(solution)/shard_map/ppermute | solution.py:124
  38.7 14.3 %collective-permute-start.17 = (bf16[8,128,128]{2,1,0:T(8,128)(2,1)S(1)}, bf16[8,128,128]{2,1,0:T(8,128)(2,1)S(1)}, u32[]{:S(2)}, u32[]{:S(2)}) collective-permute-start(bf16[8,128,128]{2,1,0:T(8,128)(2,1)S(1)} %collective-permute-done.6.refs_6_.refs_14_), channel_id=1, source_target_pairs={{0,2},{2,4},{4,6},{6,7},{7,5},{5,3},{3,1},{1,0},{8,10},{10,12},{12... | collective-permute-start | bytes 786440 | tf_op jit(solution)/shard_map/ppermute | solution.py:126
  38.9 14.1 %collective-permute-start.18 = (bf16[8,128,128]{2,1,0:T(8,128)(2,1)S(1)}, bf16[8,128,128]{2,1,0:T(8,128)(2,1)S(1)}, u32[]{:S(2)}, u32[]{:S(2)}) collective-permute-start(bf16[8,128,128]{2,1,0:T(8,128)(2,1)S(1)} %collective-permute-done.13.refs_9_.refs_19_), channel_id=1, source_target_pairs={{2,0},{4,2},{6,4},{7,6},{5,7},{3,5},{1,3},{0,1},{10,8},{12,10},{14... | collective-permute-start | bytes 786440 | tf_op jit(solution)/shard_map/ppermute | solution.py:126
  40.9 5.7 %collective-permute-start.3 = (bf16[1,2,128,128]{3,2,1,0:T(8,128)(2,1)}, bf16[1,2,128,128]{3,2,1,0:T(8,128)(2,1)S(1)}, u32[]{:S(2)}, u32[]{:S(2)}) collective-permute-start(bf16[1,2,128,128]{3,2,1,0:T(8,128)(2,1)} %copy-done.6), channel_id=1, source_target_pairs={{7,8},{15,16},{23,24},{8,7},{16,15},{24,23}} | collective-permute-start | bytes 196616 | tf_op jit(solution)/shard_map/ppermute | solution.py:373
  42.2 9.9 %collective-permute-start.16 = (bf16[2,2,128,128]{3,2,1,0:T(8,128)(2,1)S(1)}, bf16[2,2,128,128]{3,2,1,0:T(8,128)(2,1)S(1)}, u32[]{:S(2)}, u32[]{:S(2)}) collective-permute-start(bf16[2,2,128,128]{3,2,1,0:T(8,128)(2,1)S(1)} %first.1.refs_6_), channel_id=1, source_target_pairs={{0,24},{1,25},{2,26},{3,27},{4,28},{5,29},{6,30},{7,31}} | collective-permute-start | bytes 393224 | tf_op jit(solution)/shard_map/ppermute | solution.py:379
  45.3 6.8 %collective-permute-start.15 = (bf16[2,2,128,128]{3,2,1,0:T(8,128)(2,1)S(1)}, bf16[2,2,128,128]{3,2,1,0:T(8,128)(2,1)S(1)}, u32[]{:S(2)}, u32[]{:S(2)}) collective-permute-start(bf16[2,2,128,128]{3,2,1,0:T(8,128)(2,1)S(1)} %first.1.refs_6_), channel_id=1, source_target_pairs={{0,16},{1,17},{2,18},{3,19},{4,20},{5,21},{6,22},{7,23}} | collective-permute-start | bytes 393224 | tf_op jit(solution)/shard_map/ppermute | solution.py:379
  46.6 6.5 %collective-permute-start.14 = (bf16[2,2,128,128]{3,2,1,0:T(8,128)(2,1)S(1)}, bf16[2,2,128,128]{3,2,1,0:T(8,128)(2,1)S(1)}, u32[]{:S(2)}, u32[]{:S(2)}) collective-permute-start(bf16[2,2,128,128]{3,2,1,0:T(8,128)(2,1)S(1)} %first.1.refs_6_), channel_id=1, source_target_pairs={{0,8},{1,9},{2,10},{3,11},{4,12},{5,13},{6,14},{7,15}} | collective-permute-start | bytes 393224 | tf_op jit(solution)/shard_map/ppermute | solution.py:379

commit v4 on v3

--- a/solution.py
+++ b/solution.py
@@ -11,6 +11,7 @@
 GLOBAL = 2
 RANDOM = 3
 LIST = 8
+PARTS = 4
 TO_LOG2 = HEAD_DIM**-0.5 * 1.4426950408889634
 
 VMEM = pl.BlockSpec(memory_space=pltpu.VMEM)
@@ -168,8 +169,8 @@
 
 
 def attend(n_dev, q_ref, out_ref, load_keys, load_values, buffers):
-    scores, weights = buffers[:2], buffers[2:4]
-    half = HEADS // 2
+    scores, weights, done, sems = buffers[:2], buffers[2:4], buffers[4], buffers[5]
+    heads = HEADS // PARTS
 
     def lanes(h):
         return slice(h * HEAD_DIM, (h + 1) * HEAD_DIM)
@@ -177,43 +178,53 @@
     def rows_of(i):
         return pl.ds(pl.multiple_of(i * BLOCK, BLOCK), BLOCK)
 
-    def form_scores(i, side):
-        q = jnp.concatenate([q_ref[rows_of(i), lanes(side * half + n)] for n in range(half)], axis=0)
-        scores[side][...] = lax.dot_general(
+    def form_scores(i, part):
+        q = jnp.concatenate([q_ref[rows_of(i), lanes(part * heads + n)] for n in range(heads)], axis=0)
+        scores[part % 2][...] = lax.dot_general(
             q, load_keys(i), (((1,), (1,)), ((), ())), preferred_element_type=jnp.float32
         )
 
-    def form_weights(i, side):
-        for n in range(half):
-            part = slice(n * BLOCK, (n + 1) * BLOCK)
-            score = scores[side][part, :]
+    def form_weights(i, part):
+        for n in range(heads):
+            rows = slice(n * BLOCK, (n + 1) * BLOCK)
+            score = scores[part % 2][rows, :]
             top = jnp.max(score, axis=1, keepdims=True)
-            weights[side][part, :] = jnp.exp2((score - top) * TO_LOG2).astype(jnp.bfloat16)
-
-    def sum_up(i, side):
-        total = jnp.dot(weights[side][...], load_values(i), preferred_element_type=jnp.float32)
-        for n in range(half):
-            part = slice(n * BLOCK, (n + 1) * BLOCK)
-            out = total[part, :HEAD_DIM] / total[part, HEAD_DIM:]
-            out_ref[rows_of(i), lanes(side * half + n)] = out.astype(out_ref.dtype)
-
-    form_scores(0, 0)
-    form_scores(0, 1)
-    form_weights(0, 0)
+            weights[part % 2][rows, :] = jnp.exp2((score - top) * TO_LOG2).astype(jnp.bfloat16)
+
+    def sent(i):
+        return pltpu.make_async_copy(done.at[rows_of(i)], out_ref.at[rows_of(i)], sems.at[i])
+
+    def sum_up(i, part):
+        total = jnp.dot(weights[part % 2][...], load_values(i), preferred_element_type=jnp.float32)
+        for n in range(heads):
+            rows = slice(n * BLOCK, (n + 1) * BLOCK)
+            out = total[rows, :HEAD_DIM] / total[rows, HEAD_DIM:]
+            done[rows_of(i), lanes(part * heads + n)] = out.astype(done.dtype)
+        if part == PARTS - 1:
+            sent(i).start()
+
+    def turn(i, part, before):
+        form_scores(i, part)
+        for work, lag in ((form_weights, 1), (sum_up, 2)):
+            if part >= lag:
+                work(i, part - lag)
+            elif before is not None:
+                work(before, part - lag + PARTS)
+
+    for part in range(PARTS):
+        turn(0, part, None)
 
     def step(u, _):
-        form_scores(u, 0)
-        form_weights(u - 1, 1)
-        sum_up(u - 1, 0)
-        form_scores(u, 1)
-        form_weights(u, 0)
-        sum_up(u - 1, 1)
+        for part in range(PARTS):
+            turn(u, part, u - 1)
         return 0
 
     lax.fori_loop(1, n_dev, step, 0)
-    form_weights(n_dev - 1, 1)
-    sum_up(n_dev - 1, 0)
-    sum_up(n_dev - 1, 1)
+    form_weights(n_dev - 1, PARTS - 1)
+    sum_up(n_dev - 1, PARTS - 2)
+    sum_up(n_dev - 1, PARTS - 1)
+    for i in range(n_dev):
+        sent(i).wait()
 
 
 def attention_kernel(sizes, where, n_shared, list_ref, q_ref, k_ref, v_ref, before_ref, after_ref, *rest):
@@ -305,13 +316,13 @@
 
 def attention(sizes, queries, keys, values, before, after, shared, lists, where, parts):
     n_dev = sizes[2]
-    rows, n_keys = HEADS // 2 * BLOCK, (GLOBAL + 3 + RANDOM) * BLOCK
+    rows, n_keys = HEADS // PARTS * BLOCK, (GLOBAL + 3 + RANDOM) * BLOCK
     n_pool = n_dev + 2 + GLOBAL + max(at + part.shape[0] for part, (at, _) in zip(parts, where))
     return pl.pallas_call(
         lambda *refs: attention_kernel(sizes, where, len(shared), *refs),
         out_shape=jax.ShapeDtypeStruct(queries.shape, jnp.bfloat16),
         in_specs=[SMEM] + [VMEM] * (5 + len(shared)) + [MEM] * len(parts),
-        out_specs=VMEM,
+        out_specs=MEM,
         scratch_shapes=[
             pltpu.VMEM((n_pool, 2, BLOCK, HEAD_DIM), jnp.bfloat16),
             pltpu.SMEM((n_dev * RANDOM,), jnp.int32),
@@ -319,6 +330,8 @@
             pltpu.SemaphoreType.DMA((len(parts),)),
             *[pltpu.VMEM((rows, n_keys), jnp.float32)] * 2,
             *[pltpu.VMEM((rows, n_keys), jnp.bfloat16)] * 2,
+            pltpu.VMEM(queries.shape, jnp.bfloat16),
+            pltpu.SemaphoreType.DMA((n_dev,)),
         ],
         compiler_params=pltpu.CompilerParams(vmem_limit_bytes=24 << 20),
         name="attention",

time: 69.8 us -> 67.3 us (0.964)
  Pallas kernels: 16.8 us -> 14.3 us
    pallas_call x1, Pallas kernels: 16.4 us -> 13.9 us  [attention(): pl.pallas_call(lambda *refs: attention_kernel(sizes, where, len(shared),...]
where the time goes in v4:
time: 67.3 us; the launch traced here: 67 us
  starting transfers between devices  32 us (48%)
  waiting for transfers between devices  16.4 us (24%)
  Pallas kernels  14.3 us (21%)
  local copies, waits for them, and re-layouts  4.16 us (6%)
    pallas_call x1, Pallas kernels, attention(): pl.pallas_call(lambda *refs: attention_kernel(sizes, where, len(shared),...  13.9 us
    ppermute x6, waiting for transfers between devices, pass_round(): k[side] = lax.ppermute(k[side], 'ctx', pairs)  13.5 us
    ppermute x3, starting transfers between devices, per_device(): lax.ppermute(mine, 'pb', [(0, p)])  9.9 us
    ppermute x6, starting transfers between devices, pass_round(): k[side] = lax.ppermute(k[side], 'ctx', pairs)  7.17 us
    ppermute x6, starting transfers between devices, pass_round(): v[side] = lax.ppermute(v[side], 'ctx', pairs)  6.14 us
    ppermute x1, starting transfers between devices, per_device(): direct = lax.ppermute(first, ('pb', 'ctx'), [(0, last)])  5.96 us
    unnamed x14, local copies, waits for them, and re-layouts  2.54 us
    ppermute x1, waiting for transfers between devices, per_device(): direct = lax.ppermute(first, ('pb', 'ctx'), [(0, last)])  1.97 us
  transfers between devices with their start and end apart: 19, of which 6 were waited for; matrix products, arithmetic and copies ran while one was open for 2% of the time, Pallas kernels for 1%

profile of v4, /device:TPU:0, one launch (start us, length us, event | category | flops | bytes accessed | tf_op | source)
XLA Modules:
  0.0 67.0 jit_solution(9620684138717278781)
XLA Ops:
  0.0 0.0 copy-start
  0.0 0.0 copy-start.1
  0.0 3.0 %collective-permute-start = (bf16[8,128,128]{2,1,0:T(8,128)(2,1)}, bf16[8,128,128]{2,1,0:T(8,128)(2,1)S(1)}, u32[]{:S(2)}, u32[]{:S(2)}) collective-permute-start(bf16[8,128,128]{2,1,0:T(8,128)(2,1)} %bitcast.2), channel_id=1, source_target_pairs={{0,2},{2,4},{4,6},{6,7},{7,5},{5,3},{3,1},{1,0},{8,10},{10,12},{12... | collective-permute-start | bytes 786440 | tf_op jit(solution)/shard_map/ppermute | solution.py:123
  3.0 0.0 collective-permute-start.11
  3.0 1.9 %collective-permute-start.8 = (bf16[8,128,128]{2,1,0:T(8,128)(2,1)}, bf16[8,128,128]{2,1,0:T(8,128)(2,1)S(1)}, u32[]{:S(2)}, u32[]{:S(2)}) collective-permute-start(bf16[8,128,128]{2,1,0:T(8,128)(2,1)} %bitcast.3), channel_id=1, source_target_pairs={{2,0},{4,2},{6,4},{7,6},{5,7},{3,5},{1,3},{0,1},{10,8},{12,10},{14... | collective-permute-start | bytes 786440 | tf_op jit(solution)/shard_map/ppermute | solution.py:123
  5.0 0.1 collective-permute-start.4
  5.1 5.2 %collective-permute-done.refs_2_.refs_10_ = bf16[8,128,128]{2,1,0:T(8,128)(2,1)S(1)} collective-permute-done((bf16[8,128,128]{2,1,0:T(8,128)(2,1)}, bf16[8,128,128]{2,1,0:T(8,128)(2,1)S(1)}, u32[]{:S(2)}, u32[]{:S(2)}) %collective-permute-start) | collective-permute-done | bytes 262176 | tf_op jit(solution)/shard_map/ppermute | solution.py:123
  10.3 2.1 %collective-permute-start.1 = (bf16[8,128,128]{2,1,0:T(8,128)(2,1)S(1)}, bf16[8,128,128]{2,1,0:T(8,128)(2,1)S(1)}, u32[]{:S(2)}, u32[]{:S(2)}) collective-permute-start(bf16[8,128,128]{2,1,0:T(8,128)(2,1)S(1)} %collective-permute-done.refs_2_.refs_10_), channel_id=1, source_target_pairs={{0,2},{2,4},{4,6},{6,7},{7,5},{5,3},{3,1},{1,0},{8,10},{10,12},{12... | collective-permute-start | bytes 786440 | tf_op jit(solution)/shard_map/ppermute | solution.py:123
  12.4 0.0 collective-permute-done.11.refs_13_.refs_23_
  12.5 0.0 collective-permute-start.12
  12.5 0.0 copy-start.2
  12.5 0.9 %copy-done.2 = bf16[1024,128]{1,0:T(8,128)(2,1)S(1)} copy-done((bf16[1024,128]{1,0:T(8,128)(2,1)S(1)}, bf16[1024,128]{1,0:T(8,128)(2,1)}, u32[]{:S(2)}) %copy-start.2) | copy-done | bytes 262168
  13.4 0.0 copy-start.4
  13.4 0.9 %copy-done.4 = bf16[1024,128]{1,0:T(8,128)(2,1)S(1)} copy-done((bf16[1024,128]{1,0:T(8,128)(2,1)S(1)}, bf16[1024,128]{1,0:T(8,128)(2,1)}, u32[]{:S(2)}) %copy-start.4) | copy-done | bytes 262168
  14.4 0.2 edges.1
  14.6 0.0 copy-start.6
  14.6 0.6 copy-done.6
  15.2 2.9 %collective-permute-done.8.refs_12_.refs_22_ = bf16[8,128,128]{2,1,0:T(8,128)(2,1)S(1)} collective-permute-done((bf16[8,128,128]{2,1,0:T(8,128)(2,1)}, bf16[8,128,128]{2,1,0:T(8,128)(2,1)S(1)}, u32[]{:S(2)}, u32[]{:S(2)}) %collective-permute-start.8) | collective-permute-done | bytes 262176 | tf_op jit(solution)/shard_map/ppermute | solution.py:123
  18.1 0.0 collective-permute-start.9
  18.1 0.0 collective-permute-done.4.refs_3_.refs_11_
  18.1 2.0 %collective-permute-start.5 = (bf16[8,128,128]{2,1,0:T(8,128)(2,1)S(1)}, bf16[8,128,128]{2,1,0:T(8,128)(2,1)}, u32[]{:S(2)}, u32[]{:S(2)}) collective-permute-start(bf16[8,128,128]{2,1,0:T(8,128)(2,1)S(1)} %collective-permute-done.4.refs_3_.refs_11_), channel_id=1, source_target_pairs={{0,2},{2,4},{4,6},{6,7},{7,5},{5,3},{3,1},{1,0},{8,10},{10,12},{12... | collective-permute-start | bytes 786440 | tf_op jit(solution)/shard_map/ppermute | solution.py:125
  20.1 6.0 %collective-permute-start.2 = (bf16[2,2,128,128]{3,2,1,0:T(8,128)(2,1)S(1)}, bf16[2,2,128,128]{3,2,1,0:T(8,128)(2,1)}, u32[]{:S(2)}, u32[]{:S(2)}) collective-permute-start(bf16[2,2,128,128]{3,2,1,0:T(8,128)(2,1)S(1)} %get-tuple-element.10.refs_0_), channel_id=1, source_target_pairs={{0,7}} | collective-permute-start | bytes 393224 | tf_op jit(solution)/shard_map/ppermute | solution.py:384
  26.1 0.0 copy-done
  26.1 0.1 constant_dynamic-slice_fusion
  26.2 0.7 %copy.5 = s32[64,8]{1,0:T(8,128)} copy(s32[64,8]{0,1:T(8,128)S(1)} %constant_dynamic-slice_fusion) | data formatting | bytes 4096 | tf_op jit(solution)/shard_map/dynamic_slice | solution.py:30
  26.9 0.8 %reshape.11.refs_0_ = s32[512]{0:T(512)S(1)} reshape(s32[64,8]{1,0:T(8,128)} %copy.5) | data formatting | bytes 4096 | tf_op jit(solution)/shard_map/reshape | solution.py:32
  27.7 0.0 copy-start.3
  27.7 0.0 copy-start.5
  27.7 2.0 %collective-permute-done.2.refs_1_ = bf16[2,2,128,128]{3,2,1,0:T(8,128)(2,1)} collective-permute-done((bf16[2,2,128,128]{3,2,1,0:T(8,128)(2,1)S(1)}, bf16[2,2,128,128]{3,2,1,0:T(8,128)(2,1)}, u32[]{:S(2)}, u32[]{:S(2)}) %collective-permute-start.2) | collective-permute-done | bytes 131104 | tf_op jit(solution)/shard_map/ppermute | solution.py:384
  29.7 0.0 collective-permute-done.1.refs_4_.refs_12_
  29.7 0.0 collective-permute-start.6
  29.7 0.0 collective-permute-done.12.refs_11_.refs_21_
  29.7 2.0 %collective-permute-start.13 = (bf16[8,128,128]{2,1,0:T(8,128)(2,1)}, bf16[8,128,128]{2,1,0:T(8,128)(2,1)S(1)}, u32[]{:S(2)}, u32[]{:S(2)}) collective-permute-start(bf16[8,128,128]{2,1,0:T(8,128)(2,1)} %collective-permute-done.12.refs_11_.refs_21_), channel_id=1, source_target_pairs={{2,0},{4,2},{6,4},{7,6},{5,7},{3,5},{1,3},{0,1},{10,8},{12,10},{14... | collective-permute-start | bytes 786440 | tf_op jit(solution)/shard_map/ppermute | solution.py:125
  31.7 0.0 collective-permute-done.9.refs_10_.refs_20_
  31.7 0.1 collective-permute-start.10
  31.8 0.0 collective-permute-done.5.refs_5_.refs_13_
  31.8 2.0 %collective-permute-start.7 = (bf16[8,128,128]{2,1,0:T(8,128)(2,1)}, bf16[8,128,128]{2,1,0:T(8,128)(2,1)S(1)}, u32[]{:S(2)}, u32[]{:S(2)}) collective-permute-start(bf16[8,128,128]{2,1,0:T(8,128)(2,1)} %collective-permute-done.5.refs_5_.refs_13_), channel_id=1, source_target_pairs={{0,2},{2,4},{4,6},{6,7},{7,5},{5,3},{3,1},{1,0},{8,10},{10,12},{12... | collective-permute-start | bytes 786440 | tf_op jit(solution)/shard_map/ppermute | solution.py:125
  33.8 5.0 %collective-permute-done.6.refs_6_.refs_14_ = bf16[8,128,128]{2,1,0:T(8,128)(2,1)S(1)} collective-permute-done((bf16[8,128,128]{2,1,0:T(8,128)(2,1)S(1)}, bf16[8,128,128]{2,1,0:T(8,128)(2,1)S(1)}, u32[]{:S(2)}, u32[]{:S(2)}) %collective-permute-start.6) | collective-permute-done | bytes 262176 | tf_op jit(solution)/shard_map/ppermute | solution.py:123
  38.7 0.2 collective-permute-start.17
  38.9 0.0 collective-permute-done.13.refs_9_.refs_19_
  38.9 1.9 %collective-permute-start.18 = (bf16[8,128,128]{2,1,0:T(8,128)(2,1)S(1)}, bf16[8,128,128]{2,1,0:T(8,128)(2,1)S(1)}, u32[]{:S(2)}, u32[]{:S(2)}) collective-permute-start(bf16[8,128,128]{2,1,0:T(8,128)(2,1)S(1)} %collective-permute-done.13.refs_9_.refs_19_), channel_id=1, source_target_pairs={{2,0},{4,2},{6,4},{7,6},{5,7},{3,5},{1,3},{0,1},{10,8},{12,10},{14... | collective-permute-start | bytes 786440 | tf_op jit(solution)/shard_map/ppermute | solution.py:127
  40.9 0.7 collective-permute-start.3
  41.5 0.4 collective-permute-done.10.refs_8_.refs_18_
  42.0 0.0 collective-permute-done.7.refs_7_.refs_15_
  42.0 0.2 first.1.refs_6_
  42.2 3.1 %collective-permute-start.16 = (bf16[2,2,128,128]{3,2,1,0:T(8,128)(2,1)S(1)}, bf16[2,2,128,128]{3,2,1,0:T(8,128)(2,1)S(1)}, u32[]{:S(2)}, u32[]{:S(2)}) collective-permute-start(bf16[2,2,128,128]{3,2,1,0:T(8,128)(2,1)S(1)} %first.1.refs_6_), channel_id=1, source_target_pairs={{0,24},{1,25},{2,26},{3,27},{4,28},{5,29},{6,30},{7,31}} | collective-permute-start | bytes 393224 | tf_op jit(solution)/shard_map/ppermute | solution.py:392
  45.3 1.3 %collective-permute-start.15 = (bf16[2,2,128,128]{3,2,1,0:T(8,128)(2,1)S(1)}, bf16[2,2,128,128]{3,2,1,0:T(8,128)(2,1)S(1)}, u32[]{:S(2)}, u32[]{:S(2)}) collective-permute-start(bf16[2,2,128,128]{3,2,1,0:T(8,128)(2,1)S(1)} %first.1.refs_6_), channel_id=1, source_target_pairs={{0,16},{1,17},{2,18},{3,19},{4,20},{5,21},{6,22},{7,23}} | collective-permute-start | bytes 393224 | tf_op jit(solution)/shard_map/ppermute | solution.py:392
  46.6 0.0 collective-permute-done.3.refs_4_.refs_5_
  46.6 5.5 %collective-permute-start.14 = (bf16[2,2,128,128]{3,2,1,0:T(8,128)(2,1)S(1)}, bf16[2,2,128,128]{3,2,1,0:T(8,128)(2,1)S(1)}, u32[]{:S(2)}, u32[]{:S(2)}) collective-permute-start(bf16[2,2,128,128]{3,2,1,0:T(8,128)(2,1)S(1)} %first.1.refs_6_), channel_id=1, source_target_pairs={{0,8},{1,9},{2,10},{3,11},{4,12},{5,13},{6,14},{7,15}} | collective-permute-start | bytes 393224 | tf_op jit(solution)/shard_map/ppermute | solution.py:392
  52.1 0.0 collective-permute-done.16.refs_9_
  52.1 0.0 collective-permute-done.15.refs_8_
  52.1 0.9 %collective-permute-done.14.refs_7_ = bf16[2,2,128,128]{3,2,1,0:T(8,128)(2,1)S(1)} collective-permute-done((bf16[2,2,128,128]{3,2,1,0:T(8,128)(2,1)S(1)}, bf16[2,2,128,128]{3,2,1,0:T(8,128)(2,1)S(1)}, u32[]{:S(2)}, u32[]{:S(2)}) %collective-permute-start.14) | collective-permute-done | bytes 131104 | tf_op jit(solution)/shard_map/ppermute | solution.py:392
  53.1 0.0 collective-permute-done.17.refs_16_
  53.1 0.0 collective-permute-done.18.refs_17_
  53.1 0.0 copy-done.1
  53.1 0.0 copy-done.3
  53.1 0.0 copy-done.5
  53.1 13.9 %attention.1 = bf16[1024,1024]{1,0:T(8,128)(2,1)} custom-call(s32[512]{0:T(512)S(1)} %reshape.11.refs_0_, bf16[1024,1024]{1,0:T(8,128)(2,1)S(1)} %copy-done.1, bf16[8,128,128]{2,1,0:T(8,128)(2,1)S(1)} %bitcast.5, bf16[8,128,128]{2,1,0:T(8,128)(2,1)S(1)} %bitcast.9, bf16[1,2,128,128]{3,2,1,0:T(8,128)(2,1)S(1)} %collective-permute-done.3.refs_4_.refs_5_, ...), custom_call_target="tpu_custom_call" | custom-call | tf_op jit(solution)/shard_map/attention/pallas_call | solution.py:321
Async XLA Ops:
  0.0 26.1 %copy-start = (s32[256,8]{0,1:T(8,128)S(1)}, s32[256,8]{0,1:T(8,128)}, u32[]{:S(2)}) copy-start(s32[256,8]{0,1:T(8,128)} %param.7) | copy-start | bytes 24580
  0.0 53.1 %copy-start.1 = (bf16[1024,1024]{1,0:T(8,128)(2,1)S(1)}, bf16[1024,1024]{1,0:T(8,128)(2,1)}, u32[]{:S(2)}) copy-start(bf16[1024,1024]{1,0:T(8,128)(2,1)} %refs_1_.1) | copy-start | bytes 6291460
  0.0 10.3 %collective-permute-start = (bf16[8,128,128]{2,1,0:T(8,128)(2,1)}, bf16[8,128,128]{2,1,0:T(8,128)(2,1)S(1)}, u32[]{:S(2)}, u32[]{:S(2)}) collective-permute-start(bf16[8,128,128]{2,1,0:T(8,128)(2,1)} %bitcast.2), channel_id=1, source_target_pairs={{0,2},{2,4},{4,6},{6,7},{7,5},{5,3},{3,1},{1,0},{8,10},{10,12},{12... | collective-permute-start | bytes 786440 | tf_op jit(solution)/shard_map/ppermute | solution.py:123
  3.0 9.4 %collective-permute-start.11 = (bf16[8,128,128]{2,1,0:T(8,128)(2,1)}, bf16[8,128,128]{2,1,0:T(8,128)(2,1)S(1)}, u32[]{:S(2)}, u32[]{:S(2)}) collective-permute-start(bf16[8,128,128]{2,1,0:T(8,128)(2,1)} %bitcast.6), channel_id=1, source_target_pairs={{2,0},{4,2},{6,4},{7,6},{5,7},{3,5},{1,3},{0,1},{10,8},{12,10},{14... | collective-permute-start | bytes 786440 | tf_op jit(solution)/shard_map/ppermute | solution.py:125
  3.0 15.1 %collective-permute-start.8 = (bf16[8,128,128]{2,1,0:T(8,128)(2,1)}, bf16[8,128,128]{2,1,0:T(8,128)(2,1)S(1)}, u32[]{:S(2)}, u32[]{:S(2)}) collective-permute-start(bf16[8,128,128]{2,1,0:T(8,128)(2,1)} %bitcast.3), channel_id=1, source_target_pairs={{2,0},{4,2},{6,4},{7,6},{5,7},{3,5},{1,3},{0,1},{10,8},{12,10},{14... | collective-permute-start | bytes 786440 | tf_op jit(solution)/shard_map/ppermute | solution.py:123
  5.0 13.1 %collective-permute-start.4 = (bf16[8,128,128]{2,1,0:T(8,128)(2,1)}, bf16[8,128,128]{2,1,0:T(8,128)(2,1)S(1)}, u32[]{:S(2)}, u32[]{:S(2)}) collective-permute-start(bf16[8,128,128]{2,1,0:T(8,128)(2,1)} %bitcast.7), channel_id=1, source_target_pairs={{0,2},{2,4},{4,6},{6,7},{7,5},{5,3},{3,1},{1,0},{8,10},{10,12},{12... | collective-permute-start | bytes 786440 | tf_op jit(solution)/shard_map/ppermute | solution.py:125
  10.3 19.4 %collective-permute-start.1 = (bf16[8,128,128]{2,1,0:T(8,128)(2,1)S(1)}, bf16[8,128,128]{2,1,0:T(8,128)(2,1)S(1)}, u32[]{:S(2)}, u32[]{:S(2)}) collective-permute-start(bf16[8,128,128]{2,1,0:T(8,128)(2,1)S(1)} %collective-permute-done.refs_2_.refs_10_), channel_id=1, source_target_pairs={{0,2},{2,4},{4,6},{6,7},{7,5},{5,3},{3,1},{1,0},{8,10},{10,12},{12... | collective-permute-start | bytes 786440 | tf_op jit(solution)/shard_map/ppermute | solution.py:123
  12.5 17.2 %collective-permute-start.12 = (bf16[8,128,128]{2,1,0:T(8,128)(2,1)S(1)}, bf16[8,128,128]{2,1,0:T(8,128)(2,1)}, u32[]{:S(2)}, u32[]{:S(2)}) collective-permute-start(bf16[8,128,128]{2,1,0:T(8,128)(2,1)S(1)} %collective-permute-done.11.refs_13_.refs_23_), channel_id=1, source_target_pairs={{2,0},{4,2},{6,4},{7,6},{5,7},{3,5},{1,3},{0,1},{10,8},{12,10},{14... | collective-permute-start | bytes 786440 | tf_op jit(solution)/shard_map/ppermute | solution.py:125
  12.5 1.0 %copy-start.2 = (bf16[1024,128]{1,0:T(8,128)(2,1)S(1)}, bf16[1024,128]{1,0:T(8,128)(2,1)}, u32[]{:S(2)}) copy-start(bf16[1024,128]{1,0:T(8,128)(2,1)} %param.5) | copy-start | bytes 786436
  13.4 0.9 %copy-start.4 = (bf16[1024,128]{1,0:T(8,128)(2,1)S(1)}, bf16[1024,128]{1,0:T(8,128)(2,1)}, u32[]{:S(2)}) copy-start(bf16[1024,128]{1,0:T(8,128)(2,1)} %param.6) | copy-start | bytes 786436
  14.6 0.6 copy-start.6
  18.1 13.6 %collective-permute-start.9 = (bf16[8,128,128]{2,1,0:T(8,128)(2,1)S(1)}, bf16[8,128,128]{2,1,0:T(8,128)(2,1)}, u32[]{:S(2)}, u32[]{:S(2)}) collective-permute-start(bf16[8,128,128]{2,1,0:T(8,128)(2,1)S(1)} %collective-permute-done.8.refs_12_.refs_22_), channel_id=1, source_target_pairs={{2,0},{4,2},{6,4},{7,6},{5,7},{3,5},{1,3},{0,1},{10,8},{12,10},{14... | collective-permute-start | bytes 786440 | tf_op jit(solution)/shard_map/ppermute | solution.py:123
  18.1 13.7 %collective-permute-start.5 = (bf16[8,128,128]{2,1,0:T(8,128)(2,1)S(1)}, bf16[8,128,128]{2,1,0:T(8,128)(2,1)}, u32[]{:S(2)}, u32[]{:S(2)}) collective-permute-start(bf16[8,128,128]{2,1,0:T(8,128)(2,1)S(1)} %collective-permute-done.4.refs_3_.refs_11_), channel_id=1, source_target_pairs={{0,2},{2,4},{4,6},{6,7},{7,5},{5,3},{3,1},{1,0},{8,10},{10,12},{12... | collective-permute-start | bytes 786440 | tf_op jit(solution)/shard_map/ppermute | solution.py:125
  20.1 9.6 %collective-permute-start.2 = (bf16[2,2,128,128]{3,2,1,0:T(8,128)(2,1)S(1)}, bf16[2,2,128,128]{3,2,1,0:T(8,128)(2,1)}, u32[]{:S(2)}, u32[]{:S(2)}) collective-permute-start(bf16[2,2,128,128]{3,2,1,0:T(8,128)(2,1)S(1)} %get-tuple-element.10.refs_0_), channel_id=1, source_target_pairs={{0,7}} | collective-permute-start | bytes 393224 | tf_op jit(solution)/shard_map/ppermute | solution.py:384
  27.7 25.4 %copy-start.3 = (bf16[1024,128]{1,0:T(8,128)(2,1)S(1)}, bf16[1024,128]{1,0:T(8,128)(2,1)}, u32[]{:S(2)}) copy-start(bf16[1024,128]{1,0:T(8,128)(2,1)} %param.5) | copy-start | bytes 786436
  27.7 25.4 %copy-start.5 = (bf16[1024,128]{1,0:T(8,128)(2,1)S(1)}, bf16[1024,128]{1,0:T(8,128)(2,1)}, u32[]{:S(2)}) copy-start(bf16[1024,128]{1,0:T(8,128)(2,1)} %param.6) | copy-start | bytes 786436
  29.7 9.0 %collective-permute-start.6 = (bf16[8,128,128]{2,1,0:T(8,128)(2,1)S(1)}, bf16[8,128,128]{2,1,0:T(8,128)(2,1)S(1)}, u32[]{:S(2)}, u32[]{:S(2)}) collective-permute-start(bf16[8,128,128]{2,1,0:T(8,128)(2,1)S(1)} %collective-permute-done.1.refs_4_.refs_12_), channel_id=1, source_target_pairs={{0,2},{2,4},{4,6},{6,7},{7,5},{5,3},{3,1},{1,0},{8,10},{10,12},{12... | collective-permute-start | bytes 786440 | tf_op jit(solution)/shard_map/ppermute | solution.py:123
  29.7 9.2 %collective-permute-start.13 = (bf16[8,128,128]{2,1,0:T(8,128)(2,1)}, bf16[8,128,128]{2,1,0:T(8,128)(2,1)S(1)}, u32[]{:S(2)}, u32[]{:S(2)}) collective-permute-start(bf16[8,128,128]{2,1,0:T(8,128)(2,1)} %collective-permute-done.12.refs_11_.refs_21_), channel_id=1, source_target_pairs={{2,0},{4,2},{6,4},{7,6},{5,7},{3,5},{1,3},{0,1},{10,8},{12,10},{14... | collective-permute-start | bytes 786440 | tf_op jit(solution)/shard_map/ppermute | solution.py:125
  31.7 10.2 %collective-permute-start.10 = (bf16[8,128,128]{2,1,0:T(8,128)(2,1)}, bf16[8,128,128]{2,1,0:T(8,128)(2,1)S(1)}, u32[]{:S(2)}, u32[]{:S(2)}) collective-permute-start(bf16[8,128,128]{2,1,0:T(8,128)(2,1)} %collective-permute-done.9.refs_10_.refs_20_), channel_id=1, source_target_pairs={{2,0},{4,2},{6,4},{7,6},{5,7},{3,5},{1,3},{0,1},{10,8},{12,10},{14... | collective-permute-start | bytes 786440 | tf_op jit(solution)/shard_map/ppermute | solution.py:123
  31.8 10.2 %collective-permute-start.7 = (bf16[8,128,128]{2,1,0:T(8,128)(2,1)}, bf16[8,128,128]{2,1,0:T(8,128)(2,1)S(1)}, u32[]{:S(2)}, u32[]{:S(2)}) collective-permute-start(bf16[8,128,128]{2,1,0:T(8,128)(2,1)} %collective-permute-done.5.refs_5_.refs_13_), channel_id=1, source_target_pairs={{0,2},{2,4},{4,6},{6,7},{7,5},{5,3},{3,1},{1,0},{8,10},{10,12},{12... | collective-permute-start | bytes 786440 | tf_op jit(solution)/shard_map/ppermute | solution.py:125
  38.7 14.3 %collective-permute-start.17 = (bf16[8,128,128]{2,1,0:T(8,128)(2,1)S(1)}, bf16[8,128,128]{2,1,0:T(8,128)(2,1)S(1)}, u32[]{:S(2)}, u32[]{:S(2)}) collective-permute-start(bf16[8,128,128]{2,1,0:T(8,128)(2,1)S(1)} %collective-permute-done.6.refs_6_.refs_14_), channel_id=1, source_target_pairs={{0,2},{2,4},{4,6},{6,7},{7,5},{5,3},{3,1},{1,0},{8,10},{10,12},{12... | collective-permute-start | bytes 786440 | tf_op jit(solution)/shard_map/ppermute | solution.py:127
  38.9 14.1 %collective-permute-start.18 = (bf16[8,128,128]{2,1,0:T(8,128)(2,1)S(1)}, bf16[8,128,128]{2,1,0:T(8,128)(2,1)S(1)}, u32[]{:S(2)}, u32[]{:S(2)}) collective-permute-start(bf16[8,128,128]{2,1,0:T(8,128)(2,1)S(1)} %collective-permute-done.13.refs_9_.refs_19_), channel_id=1, source_target_pairs={{2,0},{4,2},{6,4},{7,6},{5,7},{3,5},{1,3},{0,1},{10,8},{12,10},{14... | collective-permute-start | bytes 786440 | tf_op jit(solution)/shard_map/ppermute | solution.py:127
  40.9 5.7 %collective-permute-start.3 = (bf16[1,2,128,128]{3,2,1,0:T(8,128)(2,1)}, bf16[1,2,128,128]{3,2,1,0:T(8,128)(2,1)S(1)}, u32[]{:S(2)}, u32[]{:S(2)}) collective-permute-start(bf16[1,2,128,128]{3,2,1,0:T(8,128)(2,1)} %copy-done.6), channel_id=1, source_target_pairs={{7,8},{15,16},{23,24},{8,7},{16,15},{24,23}} | collective-permute-start | bytes 196616 | tf_op jit(solution)/shard_map/ppermute | solution.py:386
  42.2 9.9 %collective-permute-start.16 = (bf16[2,2,128,128]{3,2,1,0:T(8,128)(2,1)S(1)}, bf16[2,2,128,128]{3,2,1,0:T(8,128)(2,1)S(1)}, u32[]{:S(2)}, u32[]{:S(2)}) collective-permute-start(bf16[2,2,128,128]{3,2,1,0:T(8,128)(2,1)S(1)} %first.1.refs_6_), channel_id=1, source_target_pairs={{0,24},{1,25},{2,26},{3,27},{4,28},{5,29},{6,30},{7,31}} | collective-permute-start | bytes 393224 | tf_op jit(solution)/shard_map/ppermute | solution.py:392
  45.3 6.8 %collective-permute-start.15 = (bf16[2,2,128,128]{3,2,1,0:T(8,128)(2,1)S(1)}, bf16[2,2,128,128]{3,2,1,0:T(8,128)(2,1)S(1)}, u32[]{:S(2)}, u32[]{:S(2)}) collective-permute-start(bf16[2,2,128,128]{3,2,1,0:T(8,128)(2,1)S(1)} %first.1.refs_6_), channel_id=1, source_target_pairs={{0,16},{1,17},{2,18},{3,19},{4,20},{5,21},{6,22},{7,23}} | collective-permute-start | bytes 393224 | tf_op jit(solution)/shard_map/ppermute | solution.py:392
  46.6 6.5 %collective-permute-start.14 = (bf16[2,2,128,128]{3,2,1,0:T(8,128)(2,1)S(1)}, bf16[2,2,128,128]{3,2,1,0:T(8,128)(2,1)S(1)}, u32[]{:S(2)}, u32[]{:S(2)}) collective-permute-start(bf16[2,2,128,128]{3,2,1,0:T(8,128)(2,1)S(1)} %first.1.refs_6_), channel_id=1, source_target_pairs={{0,8},{1,9},{2,10},{3,11},{4,12},{5,13},{6,14},{7,15}} | collective-permute-start | bytes 393224 | tf_op jit(solution)/shard_map/ppermute | solution.py:392

commit v5 on v4

--- a/solution.py
+++ b/solution.py
@@ -168,7 +168,7 @@
     )(lists, key_states, value_states)
 
 
-def attend(n_dev, q_ref, out_ref, load_keys, load_values, buffers):
+def attend(n_dev, q_ref, out_ref, load_keys, load_values, late, buffers):
     scores, weights, done, sems = buffers[:2], buffers[2:4], buffers[4], buffers[5]
     heads = HEADS // PARTS
 
@@ -212,6 +212,9 @@
                 work(before, part - lag + PARTS)
 
     for part in range(PARTS):
+        if part == 2:
+            for copy in late:
+                copy.wait()
         turn(0, part, None)
 
     def step(u, _):
@@ -284,8 +287,10 @@
                 rank = counts[holder]
                 counts[holder] = rank + 1
                 table[r * RANDOM + j] = random + (lax.rem(me - holder + n_ctx, n_ctx) - 1) * slots + rank
-    for copy in copies:
-        copy.wait()
+    late = [copy for copy, (_, which) in zip(copies, where) if which == 1]
+    for copy, (_, which) in zip(copies, where):
+        if which != 1:
+            copy.wait()
 
     def near(i, step):
         block = first + i + step
@@ -311,7 +316,7 @@
             parts.append(jnp.concatenate([pool[table[i * RANDOM + j], 1], one], axis=1))
         return jnp.concatenate(parts, axis=0)
 
-    attend(n_dev, q_ref, out_ref, load_keys, load_values, buffers)
+    attend(n_dev, q_ref, out_ref, load_keys, load_values, late, buffers)
 
 
 def attention(sizes, queries, keys, values, before, after, shared, lists, where, parts):

time: 67.3 us -> 67.5 us (level)
  no operation moved by 1% of the time
where the time goes in v5:
time: 67.5 us; the launch traced here: 67.1 us
  starting transfers between devices  32 us (47%)
  waiting for transfers between devices  16.4 us (24%)
  Pallas kernels  14.4 us (21%)
  local copies, waits for them, and re-layouts  4.16 us (6%)
    pallas_call x1, Pallas kernels, attention(): pl.pallas_call(lambda *refs: attention_kernel(sizes, where, len(shared),...  14 us
    ppermute x6, waiting for transfers between devices, pass_round(): k[side] = lax.ppermute(k[side], 'ctx', pairs)  13.5 us
    ppermute x3, starting transfers between devices, per_device(): lax.ppermute(mine, 'pb', [(0, p)])  9.9 us
    ppermute x6, starting transfers between devices, pass_round(): k[side] = lax.ppermute(k[side], 'ctx', pairs)  7.17 us
    ppermute x6, starting transfers between devices, pass_round(): v[side] = lax.ppermute(v[side], 'ctx', pairs)  6.14 us
    ppermute x1, starting transfers between devices, per_device(): direct = lax.ppermute(first, ('pb', 'ctx'), [(0, last)])  5.96 us
    unnamed x14, local copies, waits for them, and re-layouts  2.54 us
    ppermute x1, waiting for transfers between devices, per_device(): direct = lax.ppermute(first, ('pb', 'ctx'), [(0, last)])  1.97 us
  transfers between devices with their start and end apart: 19, of which 6 were waited for; matrix products, arithmetic and copies ran while one was open for 2% of the time, Pallas kernels for 1%

profile of v5, /device:TPU:0, one launch (start us, length us, event | category | flops | bytes accessed | tf_op | source)
XLA Modules:
  0.0 67.1 jit_solution(4570623849348680900)
XLA Ops:
  0.0 0.0 copy-start
  0.0 0.0 copy-start.1
  0.0 3.0 %collective-permute-start = (bf16[8,128,128]{2,1,0:T(8,128)(2,1)}, bf16[8,128,128]{2,1,0:T(8,128)(2,1)S(1)}, u32[]{:S(2)}, u32[]{:S(2)}) collective-permute-start(bf16[8,128,128]{2,1,0:T(8,128)(2,1)} %bitcast.2), channel_id=1, source_target_pairs={{0,2},{2,4},{4,6},{6,7},{7,5},{5,3},{3,1},{1,0},{8,10},{10,12},{12... | collective-permute-start | bytes 786440 | tf_op jit(solution)/shard_map/ppermute | solution.py:123
  3.0 0.0 collective-permute-start.11
  3.0 1.9 %collective-permute-start.8 = (bf16[8,128,128]{2,1,0:T(8,128)(2,1)}, bf16[8,128,128]{2,1,0:T(8,128)(2,1)S(1)}, u32[]{:S(2)}, u32[]{:S(2)}) collective-permute-start(bf16[8,128,128]{2,1,0:T(8,128)(2,1)} %bitcast.3), channel_id=1, source_target_pairs={{2,0},{4,2},{6,4},{7,6},{5,7},{3,5},{1,3},{0,1},{10,8},{12,10},{14... | collective-permute-start | bytes 786440 | tf_op jit(solution)/shard_map/ppermute | solution.py:123
  5.0 0.1 collective-permute-start.4
  5.1 5.2 %collective-permute-done.refs_2_.refs_10_ = bf16[8,128,128]{2,1,0:T(8,128)(2,1)S(1)} collective-permute-done((bf16[8,128,128]{2,1,0:T(8,128)(2,1)}, bf16[8,128,128]{2,1,0:T(8,128)(2,1)S(1)}, u32[]{:S(2)}, u32[]{:S(2)}) %collective-permute-start) | collective-permute-done | bytes 262176 | tf_op jit(solution)/shard_map/ppermute | solution.py:123
  10.3 2.1 %collective-permute-start.1 = (bf16[8,128,128]{2,1,0:T(8,128)(2,1)S(1)}, bf16[8,128,128]{2,1,0:T(8,128)(2,1)S(1)}, u32[]{:S(2)}, u32[]{:S(2)}) collective-permute-start(bf16[8,128,128]{2,1,0:T(8,128)(2,1)S(1)} %collective-permute-done.refs_2_.refs_10_), channel_id=1, source_target_pairs={{0,2},{2,4},{4,6},{6,7},{7,5},{5,3},{3,1},{1,0},{8,10},{10,12},{12... | collective-permute-start | bytes 786440 | tf_op jit(solution)/shard_map/ppermute | solution.py:123
  12.4 0.0 collective-permute-done.11.refs_13_.refs_23_
  12.5 0.0 collective-permute-start.12
  12.5 0.0 copy-start.2
  12.5 0.9 %copy-done.2 = bf16[1024,128]{1,0:T(8,128)(2,1)S(1)} copy-done((bf16[1024,128]{1,0:T(8,128)(2,1)S(1)}, bf16[1024,128]{1,0:T(8,128)(2,1)}, u32[]{:S(2)}) %copy-start.2) | copy-done | bytes 262168
  13.4 0.0 copy-start.4
  13.4 0.9 %copy-done.4 = bf16[1024,128]{1,0:T(8,128)(2,1)S(1)} copy-done((bf16[1024,128]{1,0:T(8,128)(2,1)S(1)}, bf16[1024,128]{1,0:T(8,128)(2,1)}, u32[]{:S(2)}) %copy-start.4) | copy-done | bytes 262168
  14.4 0.2 edges.1
  14.6 0.0 copy-start.6
  14.6 0.6 copy-done.6
  15.2 2.9 %collective-permute-done.8.refs_12_.refs_22_ = bf16[8,128,128]{2,1,0:T(8,128)(2,1)S(1)} collective-permute-done((bf16[8,128,128]{2,1,0:T(8,128)(2,1)}, bf16[8,128,128]{2,1,0:T(8,128)(2,1)S(1)}, u32[]{:S(2)}, u32[]{:S(2)}) %collective-permute-start.8) | collective-permute-done | bytes 262176 | tf_op jit(solution)/shard_map/ppermute | solution.py:123
  18.1 0.0 collective-permute-start.9
  18.1 0.0 collective-permute-done.4.refs_3_.refs_11_
  18.1 2.0 %collective-permute-start.5 = (bf16[8,128,128]{2,1,0:T(8,128)(2,1)S(1)}, bf16[8,128,128]{2,1,0:T(8,128)(2,1)}, u32[]{:S(2)}, u32[]{:S(2)}) collective-permute-start(bf16[8,128,128]{2,1,0:T(8,128)(2,1)S(1)} %collective-permute-done.4.refs_3_.refs_11_), channel_id=1, source_target_pairs={{0,2},{2,4},{4,6},{6,7},{7,5},{5,3},{3,1},{1,0},{8,10},{10,12},{12... | collective-permute-start | bytes 786440 | tf_op jit(solution)/shard_map/ppermute | solution.py:125
  20.1 6.0 %collective-permute-start.2 = (bf16[2,2,128,128]{3,2,1,0:T(8,128)(2,1)S(1)}, bf16[2,2,128,128]{3,2,1,0:T(8,128)(2,1)}, u32[]{:S(2)}, u32[]{:S(2)}) collective-permute-start(bf16[2,2,128,128]{3,2,1,0:T(8,128)(2,1)S(1)} %get-tuple-element.10.refs_0_), channel_id=1, source_target_pairs={{0,7}} | collective-permute-start | bytes 393224 | tf_op jit(solution)/shard_map/ppermute | solution.py:389
  26.1 0.0 copy-done
  26.1 0.1 constant_dynamic-slice_fusion
  26.2 0.7 %copy.5 = s32[64,8]{1,0:T(8,128)} copy(s32[64,8]{0,1:T(8,128)S(1)} %constant_dynamic-slice_fusion) | data formatting | bytes 4096 | tf_op jit(solution)/shard_map/dynamic_slice | solution.py:30
  26.9 0.8 %reshape.11.refs_0_ = s32[512]{0:T(512)S(1)} reshape(s32[64,8]{1,0:T(8,128)} %copy.5) | data formatting | bytes 4096 | tf_op jit(solution)/shard_map/reshape | solution.py:32
  27.7 0.0 copy-start.3
  27.7 0.0 copy-start.5
  27.7 2.0 %collective-permute-done.2.refs_1_ = bf16[2,2,128,128]{3,2,1,0:T(8,128)(2,1)} collective-permute-done((bf16[2,2,128,128]{3,2,1,0:T(8,128)(2,1)S(1)}, bf16[2,2,128,128]{3,2,1,0:T(8,128)(2,1)}, u32[]{:S(2)}, u32[]{:S(2)}) %collective-permute-start.2) | collective-permute-done | bytes 131104 | tf_op jit(solution)/shard_map/ppermute | solution.py:389
  29.7 0.0 collective-permute-done.1.refs_4_.refs_12_
  29.7 0.0 collective-permute-start.6
  29.7 0.0 collective-permute-done.12.refs_11_.refs_21_
  29.7 2.0 %collective-permute-start.13 = (bf16[8,128,128]{2,1,0:T(8,128)(2,1)}, bf16[8,128,128]{2,1,0:T(8,128)(2,1)S(1)}, u32[]{:S(2)}, u32[]{:S(2)}) collective-permute-start(bf16[8,128,128]{2,1,0:T(8,128)(2,1)} %collective-permute-done.12.refs_11_.refs_21_), channel_id=1, source_target_pairs={{2,0},{4,2},{6,4},{7,6},{5,7},{3,5},{1,3},{0,1},{10,8},{12,10},{14... | collective-permute-start | bytes 786440 | tf_op jit(solution)/shard_map/ppermute | solution.py:125
  31.7 0.0 collective-permute-done.9.refs_10_.refs_20_
  31.7 0.1 collective-permute-start.10
  31.8 0.0 collective-permute-done.5.refs_5_.refs_13_
  31.8 2.0 %collective-permute-start.7 = (bf16[8,128,128]{2,1,0:T(8,128)(2,1)}, bf16[8,128,128]{2,1,0:T(8,128)(2,1)S(1)}, u32[]{:S(2)}, u32[]{:S(2)}) collective-permute-start(bf16[8,128,128]{2,1,0:T(8,128)(2,1)} %collective-permute-done.5.refs_5_.refs_13_), channel_id=1, source_target_pairs={{0,2},{2,4},{4,6},{6,7},{7,5},{5,3},{3,1},{1,0},{8,10},{10,12},{12... | collective-permute-start | bytes 786440 | tf_op jit(solution)/shard_map/ppermute | solution.py:125
  33.8 5.0 %collective-permute-done.6.refs_6_.refs_14_ = bf16[8,128,128]{2,1,0:T(8,128)(2,1)S(1)} collective-permute-done((bf16[8,128,128]{2,1,0:T(8,128)(2,1)S(1)}, bf16[8,128,128]{2,1,0:T(8,128)(2,1)S(1)}, u32[]{:S(2)}, u32[]{:S(2)}) %collective-permute-start.6) | collective-permute-done | bytes 262176 | tf_op jit(solution)/shard_map/ppermute | solution.py:123
  38.7 0.2 collective-permute-start.17
  38.9 0.0 collective-permute-done.13.refs_9_.refs_19_
  38.9 1.9 %collective-permute-start.18 = (bf16[8,128,128]{2,1,0:T(8,128)(2,1)S(1)}, bf16[8,128,128]{2,1,0:T(8,128)(2,1)S(1)}, u32[]{:S(2)}, u32[]{:S(2)}) collective-permute-start(bf16[8,128,128]{2,1,0:T(8,128)(2,1)S(1)} %collective-permute-done.13.refs_9_.refs_19_), channel_id=1, source_target_pairs={{2,0},{4,2},{6,4},{7,6},{5,7},{3,5},{1,3},{0,1},{10,8},{12,10},{14... | collective-permute-start | bytes 786440 | tf_op jit(solution)/shard_map/ppermute | solution.py:127
  40.9 0.7 collective-permute-start.3
  41.5 0.4 collective-permute-done.10.refs_8_.refs_18_
  42.0 0.0 collective-permute-done.7.refs_7_.refs_15_
  42.0 0.2 first.1.refs_6_
  42.2 3.1 %collective-permute-start.16 = (bf16[2,2,128,128]{3,2,1,0:T(8,128)(2,1)S(1)}, bf16[2,2,128,128]{3,2,1,0:T(8,128)(2,1)S(1)}, u32[]{:S(2)}, u32[]{:S(2)}) collective-permute-start(bf16[2,2,128,128]{3,2,1,0:T(8,128)(2,1)S(1)} %first.1.refs_6_), channel_id=1, source_target_pairs={{0,24},{1,25},{2,26},{3,27},{4,28},{5,29},{6,30},{7,31}} | collective-permute-start | bytes 393224 | tf_op jit(solution)/shard_map/ppermute | solution.py:397
  45.3 1.3 %collective-permute-start.15 = (bf16[2,2,128,128]{3,2,1,0:T(8,128)(2,1)S(1)}, bf16[2,2,128,128]{3,2,1,0:T(8,128)(2,1)S(1)}, u32[]{:S(2)}, u32[]{:S(2)}) collective-permute-start(bf16[2,2,128,128]{3,2,1,0:T(8,128)(2,1)S(1)} %first.1.refs_6_), channel_id=1, source_target_pairs={{0,16},{1,17},{2,18},{3,19},{4,20},{5,21},{6,22},{7,23}} | collective-permute-start | bytes 393224 | tf_op jit(solution)/shard_map/ppermute | solution.py:397
  46.6 0.0 collective-permute-done.3.refs_4_.refs_5_
  46.6 5.5 %collective-permute-start.14 = (bf16[2,2,128,128]{3,2,1,0:T(8,128)(2,1)S(1)}, bf16[2,2,128,128]{3,2,1,0:T(8,128)(2,1)S(1)}, u32[]{:S(2)}, u32[]{:S(2)}) collective-permute-start(bf16[2,2,128,128]{3,2,1,0:T(8,128)(2,1)S(1)} %first.1.refs_6_), channel_id=1, source_target_pairs={{0,8},{1,9},{2,10},{3,11},{4,12},{5,13},{6,14},{7,15}} | collective-permute-start | bytes 393224 | tf_op jit(solution)/shard_map/ppermute | solution.py:397
  52.1 0.0 collective-permute-done.16.refs_9_
  52.1 0.0 collective-permute-done.15.refs_8_
  52.1 0.9 %collective-permute-done.14.refs_7_ = bf16[2,2,128,128]{3,2,1,0:T(8,128)(2,1)S(1)} collective-permute-done((bf16[2,2,128,128]{3,2,1,0:T(8,128)(2,1)S(1)}, bf16[2,2,128,128]{3,2,1,0:T(8,128)(2,1)S(1)}, u32[]{:S(2)}, u32[]{:S(2)}) %collective-permute-start.14) | collective-permute-done | bytes 131104 | tf_op jit(solution)/shard_map/ppermute | solution.py:397
  53.1 0.0 collective-permute-done.17.refs_16_
  53.1 0.0 collective-permute-done.18.refs_17_
  53.1 0.0 copy-done.1
  53.1 0.0 copy-done.3
  53.1 0.0 copy-done.5
  53.1 14.0 %attention.1 = bf16[1024,1024]{1,0:T(8,128)(2,1)} custom-call(s32[512]{0:T(512)S(1)} %reshape.11.refs_0_, bf16[1024,1024]{1,0:T(8,128)(2,1)S(1)} %copy-done.1, bf16[8,128,128]{2,1,0:T(8,128)(2,1)S(1)} %bitcast.5, bf16[8,128,128]{2,1,0:T(8,128)(2,1)S(1)} %bitcast.9, bf16[1,2,128,128]{3,2,1,0:T(8,128)(2,1)S(1)} %collective-permute-done.3.refs_4_.refs_5_, ...), custom_call_target="tpu_custom_call" | custom-call | tf_op jit(solution)/shard_map/attention/pallas_call | solution.py:326
Async XLA Ops:
  0.0 26.1 %copy-start = (s32[256,8]{0,1:T(8,128)S(1)}, s32[256,8]{0,1:T(8,128)}, u32[]{:S(2)}) copy-start(s32[256,8]{0,1:T(8,128)} %param.7) | copy-start | bytes 24580
  0.0 53.1 %copy-start.1 = (bf16[1024,1024]{1,0:T(8,128)(2,1)S(1)}, bf16[1024,1024]{1,0:T(8,128)(2,1)}, u32[]{:S(2)}) copy-start(bf16[1024,1024]{1,0:T(8,128)(2,1)} %refs_1_.1) | copy-start | bytes 6291460
  0.0 10.3 %collective-permute-start = (bf16[8,128,128]{2,1,0:T(8,128)(2,1)}, bf16[8,128,128]{2,1,0:T(8,128)(2,1)S(1)}, u32[]{:S(2)}, u32[]{:S(2)}) collective-permute-start(bf16[8,128,128]{2,1,0:T(8,128)(2,1)} %bitcast.2), channel_id=1, source_target_pairs={{0,2},{2,4},{4,6},{6,7},{7,5},{5,3},{3,1},{1,0},{8,10},{10,12},{12... | collective-permute-start | bytes 786440 | tf_op jit(solution)/shard_map/ppermute | solution.py:123
  3.0 9.4 %collective-permute-start.11 = (bf16[8,128,128]{2,1,0:T(8,128)(2,1)}, bf16[8,128,128]{2,1,0:T(8,128)(2,1)S(1)}, u32[]{:S(2)}, u32[]{:S(2)}) collective-permute-start(bf16[8,128,128]{2,1,0:T(8,128)(2,1)} %bitcast.6), channel_id=1, source_target_pairs={{2,0},{4,2},{6,4},{7,6},{5,7},{3,5},{1,3},{0,1},{10,8},{12,10},{14... | collective-permute-start | bytes 786440 | tf_op jit(solution)/shard_map/ppermute | solution.py:125
  3.0 15.1 %collective-permute-start.8 = (bf16[8,128,128]{2,1,0:T(8,128)(2,1)}, bf16[8,128,128]{2,1,0:T(8,128)(2,1)S(1)}, u32[]{:S(2)}, u32[]{:S(2)}) collective-permute-start(bf16[8,128,128]{2,1,0:T(8,128)(2,1)} %bitcast.3), channel_id=1, source_target_pairs={{2,0},{4,2},{6,4},{7,6},{5,7},{3,5},{1,3},{0,1},{10,8},{12,10},{14... | collective-permute-start | bytes 786440 | tf_op jit(solution)/shard_map/ppermute | solution.py:123
  5.0 13.1 %collective-permute-start.4 = (bf16[8,128,128]{2,1,0:T(8,128)(2,1)}, bf16[8,128,128]{2,1,0:T(8,128)(2,1)S(1)}, u32[]{:S(2)}, u32[]{:S(2)}) collective-permute-start(bf16[8,128,128]{2,1,0:T(8,128)(2,1)} %bitcast.7), channel_id=1, source_target_pairs={{0,2},{2,4},{4,6},{6,7},{7,5},{5,3},{3,1},{1,0},{8,10},{10,12},{12... | collective-permute-start | bytes 786440 | tf_op jit(solution)/shard_map/ppermute | solution.py:125
  10.3 19.4 %collective-permute-start.1 = (bf16[8,128,128]{2,1,0:T(8,128)(2,1)S(1)}, bf16[8,128,128]{2,1,0:T(8,128)(2,1)S(1)}, u32[]{:S(2)}, u32[]{:S(2)}) collective-permute-start(bf16[8,128,128]{2,1,0:T(8,128)(2,1)S(1)} %collective-permute-done.refs_2_.refs_10_), channel_id=1, source_target_pairs={{0,2},{2,4},{4,6},{6,7},{7,5},{5,3},{3,1},{1,0},{8,10},{10,12},{12... | collective-permute-start | bytes 786440 | tf_op jit(solution)/shard_map/ppermute | solution.py:123
  12.5 17.2 %collective-permute-start.12 = (bf16[8,128,128]{2,1,0:T(8,128)(2,1)S(1)}, bf16[8,128,128]{2,1,0:T(8,128)(2,1)}, u32[]{:S(2)}, u32[]{:S(2)}) collective-permute-start(bf16[8,128,128]{2,1,0:T(8,128)(2,1)S(1)} %collective-permute-done.11.refs_13_.refs_23_), channel_id=1, source_target_pairs={{2,0},{4,2},{6,4},{7,6},{5,7},{3,5},{1,3},{0,1},{10,8},{12,10},{14... | collective-permute-start | bytes 786440 | tf_op jit(solution)/shard_map/ppermute | solution.py:125
  12.5 1.0 %copy-start.2 = (bf16[1024,128]{1,0:T(8,128)(2,1)S(1)}, bf16[1024,128]{1,0:T(8,128)(2,1)}, u32[]{:S(2)}) copy-start(bf16[1024,128]{1,0:T(8,128)(2,1)} %param.5) | copy-start | bytes 786436
  13.4 0.9 %copy-start.4 = (bf16[1024,128]{1,0:T(8,128)(2,1)S(1)}, bf16[1024,128]{1,0:T(8,128)(2,1)}, u32[]{:S(2)}) copy-start(bf16[1024,128]{1,0:T(8,128)(2,1)} %param.6) | copy-start | bytes 786436
  14.6 0.6 copy-start.6
  18.1 13.6 %collective-permute-start.9 = (bf16[8,128,128]{2,1,0:T(8,128)(2,1)S(1)}, bf16[8,128,128]{2,1,0:T(8,128)(2,1)}, u32[]{:S(2)}, u32[]{:S(2)}) collective-permute-start(bf16[8,128,128]{2,1,0:T(8,128)(2,1)S(1)} %collective-permute-done.8.refs_12_.refs_22_), channel_id=1, source_target_pairs={{2,0},{4,2},{6,4},{7,6},{5,7},{3,5},{1,3},{0,1},{10,8},{12,10},{14... | collective-permute-start | bytes 786440 | tf_op jit(solution)/shard_map/ppermute | solution.py:123
  18.1 13.7 %collective-permute-start.5 = (bf16[8,128,128]{2,1,0:T(8,128)(2,1)S(1)}, bf16[8,128,128]{2,1,0:T(8,128)(2,1)}, u32[]{:S(2)}, u32[]{:S(2)}) collective-permute-start(bf16[8,128,128]{2,1,0:T(8,128)(2,1)S(1)} %collective-permute-done.4.refs_3_.refs_11_), channel_id=1, source_target_pairs={{0,2},{2,4},{4,6},{6,7},{7,5},{5,3},{3,1},{1,0},{8,10},{10,12},{12... | collective-permute-start | bytes 786440 | tf_op jit(solution)/shard_map/ppermute | solution.py:125
  20.1 9.6 %collective-permute-start.2 = (bf16[2,2,128,128]{3,2,1,0:T(8,128)(2,1)S(1)}, bf16[2,2,128,128]{3,2,1,0:T(8,128)(2,1)}, u32[]{:S(2)}, u32[]{:S(2)}) collective-permute-start(bf16[2,2,128,128]{3,2,1,0:T(8,128)(2,1)S(1)} %get-tuple-element.10.refs_0_), channel_id=1, source_target_pairs={{0,7}} | collective-permute-start | bytes 393224 | tf_op jit(solution)/shard_map/ppermute | solution.py:389
  27.7 25.4 %copy-start.3 = (bf16[1024,128]{1,0:T(8,128)(2,1)S(1)}, bf16[1024,128]{1,0:T(8,128)(2,1)}, u32[]{:S(2)}) copy-start(bf16[1024,128]{1,0:T(8,128)(2,1)} %param.5) | copy-start | bytes 786436
  27.7 25.4 %copy-start.5 = (bf16[1024,128]{1,0:T(8,128)(2,1)S(1)}, bf16[1024,128]{1,0:T(8,128)(2,1)}, u32[]{:S(2)}) copy-start(bf16[1024,128]{1,0:T(8,128)(2,1)} %param.6) | copy-start | bytes 786436
  29.7 9.0 %collective-permute-start.6 = (bf16[8,128,128]{2,1,0:T(8,128)(2,1)S(1)}, bf16[8,128,128]{2,1,0:T(8,128)(2,1)S(1)}, u32[]{:S(2)}, u32[]{:S(2)}) collective-permute-start(bf16[8,128,128]{2,1,0:T(8,128)(2,1)S(1)} %collective-permute-done.1.refs_4_.refs_12_), channel_id=1, source_target_pairs={{0,2},{2,4},{4,6},{6,7},{7,5},{5,3},{3,1},{1,0},{8,10},{10,12},{12... | collective-permute-start | bytes 786440 | tf_op jit(solution)/shard_map/ppermute | solution.py:123
  29.7 9.2 %collective-permute-start.13 = (bf16[8,128,128]{2,1,0:T(8,128)(2,1)}, bf16[8,128,128]{2,1,0:T(8,128)(2,1)S(1)}, u32[]{:S(2)}, u32[]{:S(2)}) collective-permute-start(bf16[8,128,128]{2,1,0:T(8,128)(2,1)} %collective-permute-done.12.refs_11_.refs_21_), channel_id=1, source_target_pairs={{2,0},{4,2},{6,4},{7,6},{5,7},{3,5},{1,3},{0,1},{10,8},{12,10},{14... | collective-permute-start | bytes 786440 | tf_op jit(solution)/shard_map/ppermute | solution.py:125
  31.7 10.2 %collective-permute-start.10 = (bf16[8,128,128]{2,1,0:T(8,128)(2,1)}, bf16[8,128,128]{2,1,0:T(8,128)(2,1)S(1)}, u32[]{:S(2)}, u32[]{:S(2)}) collective-permute-start(bf16[8,128,128]{2,1,0:T(8,128)(2,1)} %collective-permute-done.9.refs_10_.refs_20_), channel_id=1, source_target_pairs={{2,0},{4,2},{6,4},{7,6},{5,7},{3,5},{1,3},{0,1},{10,8},{12,10},{14... | collective-permute-start | bytes 786440 | tf_op jit(solution)/shard_map/ppermute | solution.py:123
  31.8 10.2 %collective-permute-start.7 = (bf16[8,128,128]{2,1,0:T(8,128)(2,1)}, bf16[8,128,128]{2,1,0:T(8,128)(2,1)S(1)}, u32[]{:S(2)}, u32[]{:S(2)}) collective-permute-start(bf16[8,128,128]{2,1,0:T(8,128)(2,1)} %collective-permute-done.5.refs_5_.refs_13_), channel_id=1, source_target_pairs={{0,2},{2,4},{4,6},{6,7},{7,5},{5,3},{3,1},{1,0},{8,10},{10,12},{12... | collective-permute-start | bytes 786440 | tf_op jit(solution)/shard_map/ppermute | solution.py:125
  38.7 14.3 %collective-permute-start.17 = (bf16[8,128,128]{2,1,0:T(8,128)(2,1)S(1)}, bf16[8,128,128]{2,1,0:T(8,128)(2,1)S(1)}, u32[]{:S(2)}, u32[]{:S(2)}) collective-permute-start(bf16[8,128,128]{2,1,0:T(8,128)(2,1)S(1)} %collective-permute-done.6.refs_6_.refs_14_), channel_id=1, source_target_pairs={{0,2},{2,4},{4,6},{6,7},{7,5},{5,3},{3,1},{1,0},{8,10},{10,12},{12... | collective-permute-start | bytes 786440 | tf_op jit(solution)/shard_map/ppermute | solution.py:127
  38.9 14.1 %collective-permute-start.18 = (bf16[8,128,128]{2,1,0:T(8,128)(2,1)S(1)}, bf16[8,128,128]{2,1,0:T(8,128)(2,1)S(1)}, u32[]{:S(2)}, u32[]{:S(2)}) collective-permute-start(bf16[8,128,128]{2,1,0:T(8,128)(2,1)S(1)} %collective-permute-done.13.refs_9_.refs_19_), channel_id=1, source_target_pairs={{2,0},{4,2},{6,4},{7,6},{5,7},{3,5},{1,3},{0,1},{10,8},{12,10},{14... | collective-permute-start | bytes 786440 | tf_op jit(solution)/shard_map/ppermute | solution.py:127
  40.9 5.7 %collective-permute-start.3 = (bf16[1,2,128,128]{3,2,1,0:T(8,128)(2,1)}, bf16[1,2,128,128]{3,2,1,0:T(8,128)(2,1)S(1)}, u32[]{:S(2)}, u32[]{:S(2)}) collective-permute-start(bf16[1,2,128,128]{3,2,1,0:T(8,128)(2,1)} %copy-done.6), channel_id=1, source_target_pairs={{7,8},{15,16},{23,24},{8,7},{16,15},{24,23}} | collective-permute-start | bytes 196616 | tf_op jit(solution)/shard_map/ppermute | solution.py:391
  42.2 9.9 %collective-permute-start.16 = (bf16[2,2,128,128]{3,2,1,0:T(8,128)(2,1)S(1)}, bf16[2,2,128,128]{3,2,1,0:T(8,128)(2,1)S(1)}, u32[]{:S(2)}, u32[]{:S(2)}) collective-permute-start(bf16[2,2,128,128]{3,2,1,0:T(8,128)(2,1)S(1)} %first.1.refs_6_), channel_id=1, source_target_pairs={{0,24},{1,25},{2,26},{3,27},{4,28},{5,29},{6,30},{7,31}} | collective-permute-start | bytes 393224 | tf_op jit(solution)/shard_map/ppermute | solution.py:397
  45.3 6.8 %collective-permute-start.15 = (bf16[2,2,128,128]{3,2,1,0:T(8,128)(2,1)S(1)}, bf16[2,2,128,128]{3,2,1,0:T(8,128)(2,1)S(1)}, u32[]{:S(2)}, u32[]{:S(2)}) collective-permute-start(bf16[2,2,128,128]{3,2,1,0:T(8,128)(2,1)S(1)} %first.1.refs_6_), channel_id=1, source_target_pairs={{0,16},{1,17},{2,18},{3,19},{4,20},{5,21},{6,22},{7,23}} | collective-permute-start | bytes 393224 | tf_op jit(solution)/shard_map/ppermute | solution.py:397
  46.6 6.5 %collective-permute-start.14 = (bf16[2,2,128,128]{3,2,1,0:T(8,128)(2,1)S(1)}, bf16[2,2,128,128]{3,2,1,0:T(8,128)(2,1)S(1)}, u32[]{:S(2)}, u32[]{:S(2)}) collective-permute-start(bf16[2,2,128,128]{3,2,1,0:T(8,128)(2,1)S(1)} %first.1.refs_6_), channel_id=1, source_target_pairs={{0,8},{1,9},{2,10},{3,11},{4,12},{5,13},{6,14},{7,15}} | collective-permute-start | bytes 393224 | tf_op jit(solution)/shard_map/ppermute | solution.py:397
